TPU v7x, 32 devices: a whole 2x2x4 slice. The times are simulated.
32 devices in a mesh: dp: 16 (over z, y, core), seq: 2 (over x).
Axes of the slice: x: 2, y: 2, z: 4, core: 2. Of those that a mesh axis runs over, the one named last changes fastest.
Arguments:
- tokens: bfloat16 [16, 1024, 1024], P('dp', 'seq'), may hold values from -6 to 6
- segment_ids: int32 [16, 1024], P('dp'), may hold values from 0 to 3, never falling along the last dimension, each value on 1 to 512 neighbouring positions
- norm1_gain: bfloat16 [1024], P(('dp', 'seq')), may hold values from 0.5 to 1.5
- w_mamba_in: bfloat16 [1024, 3328], P(('dp', 'seq')), may hold values from -0.1875 to 0.1875
- w_delta: bfloat16 [1024, 24], P(('dp', 'seq')), may hold values from -0.09375 to 0.09375
- conv_weight: bfloat16 [4, 1792], P(None, ('dp', 'seq')), may hold values from -3 to 3
- conv_bias: bfloat16 [1792], P(('dp', 'seq')), may hold values from -3 to 3
- delta_bias: bfloat16 [24], replicated, may hold values from -6 to -2
- decay_log: bfloat16 [24], replicated, may hold values from -1 to 1.5
- skip_gain: bfloat16 [24], replicated, may hold values from 0.5 to 1.5
- w_mamba_out: bfloat16 [1536, 1024], P(('dp', 'seq')), may hold values from -0.15625 to 0.15625
- w_qkv: bfloat16 [1024, 768], P(('dp', 'seq')), may hold values from -0.1875 to 0.1875
- w_attn_out: bfloat16 [512, 1024], P(('dp', 'seq')), may hold values from -0.75 to 0.75
- norm2_gain: bfloat16 [1024], P(('dp', 'seq')), may hold values from 0.5 to 1.5
- w_gate_up: bfloat16 [1024, 4096], P(('dp', 'seq')), may hold values from -0.1875 to 0.1875
- w_down: bfloat16 [2048, 1024], P(('dp', 'seq')), may hold values from -0.125 to 0.125
- cotangent: bfloat16 [16, 1024, 1024], P('dp', 'seq'), may hold values from -6 to 6
Outputs:
- block_out: bfloat16 [16, 1024, 1024], P('dp', 'seq')
- grad_tokens: float32 [16, 1024, 1024], P('dp', 'seq')
- grad_norm1_gain: float32 [1024], P(('dp', 'seq'))
- grad_w_mamba_in: float32 [1024, 3328], P(('dp', 'seq'))
- grad_w_delta: float32 [1024, 24], P(('dp', 'seq'))
- grad_conv_weight: float32 [4, 1792], P(None, ('dp', 'seq'))
- grad_conv_bias: float32 [1792], P(('dp', 'seq'))
- grad_delta_bias: float32 [24], replicated
- grad_decay_log: float32 [24], replicated
- grad_skip_gain: float32 [24], replicated
- grad_w_mamba_out: float32 [1536, 1024], P(('dp', 'seq'))
- grad_w_qkv: float32 [1024, 768], P(('dp', 'seq'))
- grad_w_attn_out: float32 [512, 1024], P(('dp', 'seq'))
- grad_norm2_gain: float32 [1024], P(('dp', 'seq'))
- grad_w_gate_up: float32 [1024, 4096], P(('dp', 'seq'))
- grad_w_down: float32 [2048, 1024], P(('dp', 'seq'))
All inputs are finite; a program needn't handle non-finite values.
Results may differ from a plain program's by a relative error of at most 0.012.
Values may be sent and summed in bfloat16 or wider, within the bound.
No kernel may reach another device: no remote copies, remote signals or barrier semaphores. Data moves between devices by JAX's collectives and lax.ppermute only.
A program may use at most 256 MiB of HBM per device.

v0:
```python
from functools import partial

import jax
import jax.numpy as jnp
from jax import lax
from jax.sharding import PartitionSpec as P

MHEADS = 24
MHDIM = 64
STATE = 128
AHEADS = 8
KVHEADS = 2
AHDIM = 64


EPSILON = 1e-05
ROPE_BASE = 100000000000.0
NEGATIVE = -1e30


def from_behind(value, axis, steps):
    count = lax.axis_size(axis)
    initial, last = (max(0, -steps), min(count, count - steps))
    return lax.ppermute(value, axis, [(source, source + steps) for source in range(initial, last)])


def carried_in(x, axis, join, neutral):
    place = lax.axis_index(axis)
    gathered = jax.tree.map(
        lambda a, kind: lax.all_gather(a.astype(kind), axis), x, (jnp.bfloat16, jnp.bfloat16)
    )
    state = jax.tree.map(lambda a, e: jnp.zeros_like(a) + jnp.asarray(e, a.dtype), x, neutral)

    def one(step, state):
        return join(
            state,
            jax.tree.map(
                lambda a, own: lax.dynamic_index_in_dim(a, step, 0, False).astype(own.dtype),
                gathered,
                x,
            ),
        )

    return lax.fori_loop(0, place, one, state)


def carried_in_2(x, axis, combine, identity):
    count, position = (lax.axis_size(axis), lax.axis_index(axis))
    everything = jax.tree.map(
        lambda part, kind: lax.all_gather(part.astype(kind), axis),
        x,
        jax.tree.map(lambda a: jnp.bfloat16 if a.dtype == jnp.float32 else a.dtype, x),
    )
    start = jax.tree.map(
        lambda part, zero: jnp.broadcast_to(jnp.asarray(zero, part.dtype), part.shape), x, identity
    )

    def step(k, before):
        at = count - 1 - k
        reached = at > position
        new = combine(
            before, jax.tree.map(lambda part, own: part[at].astype(own.dtype), everything, x)
        )
        return jax.tree.map(lambda a, b: jnp.where(reached, a, b), new, before)

    return lax.fori_loop(0, count, step, start)


def rms_gain(values, gain):
    scale_inv = lax.rsqrt(jnp.mean(values * values, axis=-1, keepdims=True) + EPSILON)
    return values * scale_inv * gain


def swiglu(joined):
    half_width = joined.shape[-1] // 2
    return jax.nn.silu(joined[:, :half_width]) * joined[:, half_width:]


def cross_rows(left, right):
    return lax.dot_general(
        left, right, (((0,), (0,)), ((), ())), preferred_element_type=jnp.float32
    )


def times_transposed(left, right):
    return lax.dot_general(
        left, right, (((1,), (1,)), ((), ())), preferred_element_type=jnp.float32
    )


def compose_maps(earlier, later):
    return (later[0] * earlier[0], later[0][:, None, None] * earlier[1] + later[1])


def tap_masks(seg_padded, first_row, row_count, tap_count):
    own_ids = lax.dynamic_slice_in_dim(seg_padded, first_row + tap_count - 1, row_count)
    listed = []
    for offset in range(tap_count):
        earlier_ids = lax.dynamic_slice_in_dim(
            seg_padded, first_row + tap_count - 1 - offset, row_count
        )
        listed.append(earlier_ids == own_ids)
    return jnp.stack(listed).astype(jnp.float32)


def mamba_pre(taps, extended, delta_raw, conv_kernel, conv_shift, delta_bias, decay_log):
    row_count = delta_raw.shape[0]
    tap_count = conv_kernel.shape[0]
    convolved = jnp.zeros((row_count, conv_shift.shape[0]), jnp.float32) + conv_shift[None, :]
    for offset in range(tap_count):
        first_row = tap_count - 1 - offset
        convolved = (
            convolved
            + conv_kernel[offset][None, :]
            * extended[first_row : first_row + row_count]
            * taps[offset][:, None]
        )
    activated = jax.nn.silu(convolved)
    inner_width = MHEADS * MHDIM
    heads_in = activated[:, :inner_width].reshape(row_count, MHEADS, MHDIM)
    b_proj = activated[:, inner_width : inner_width + STATE]
    c_proj = activated[:, inner_width + STATE :]
    step_size = jax.nn.softplus(delta_raw + delta_bias[None, :])
    log_decay = -step_size * jnp.exp(decay_log)[None, :]
    return (heads_in, b_proj, c_proj, step_size, log_decay)


def mamba_state(seg_rows, seg_before, heads_in, b_proj, step_size, log_decay):
    cumulative = jnp.cumsum(log_decay, axis=0)
    final_sum = cumulative[-1]
    carry_gate = jnp.where(seg_rows[-1] == seg_before, jnp.exp(final_sum), 0.0)
    remaining = (
        jnp.where(
            (seg_rows == seg_rows[-1])[:, None], jnp.exp(final_sum[None, :] - cumulative), 0.0
        )
        * step_size
    )
    state_part = jnp.einsum(
        "shp,sn->hpn", remaining[:, :, None] * heads_in, b_proj, precision=lax.Precision.HIGHEST
    )
    return (carry_gate, state_part)


def mamba_out(
    seg_rows,
    seg_before,
    heads_in,
    b_proj,
    c_proj,
    step_size,
    log_decay,
    state_in,
    skip_gain,
    z_rows,
):
    row_count = heads_in.shape[0]
    cumulative = jnp.cumsum(log_decay, axis=0)
    places = jnp.arange(row_count, dtype=jnp.int32)
    allowed = ((places[:, None] >= places[None, :]) & (seg_rows[:, None] == seg_rows[None, :]))[
        :, :, None
    ]
    spread = cumulative[:, None, :] - cumulative[None, :, :]
    decay_map = jnp.where(allowed, jnp.exp(jnp.where(allowed, spread, 0.0)), 0.0)
    cross_terms = jnp.dot(c_proj, b_proj.T, precision=lax.Precision.HIGHEST)
    within = jnp.einsum(
        "tsh,shp->thp",
        decay_map * cross_terms[:, :, None],
        step_size[:, :, None] * heads_in,
        precision=lax.Precision.HIGHEST,
    )
    entering = jnp.where((seg_rows == seg_before)[:, None], jnp.exp(cumulative), 0.0)
    carried = (
        jnp.einsum("tn,hpn->thp", c_proj, state_in, precision=lax.Precision.HIGHEST)
        * entering[:, :, None]
    )
    summed = within + carried + skip_gain[None, :, None] * heads_in
    return summed.reshape(row_count, MHEADS * MHDIM) * jax.nn.silu(z_rows)


def rope_tables(positions):
    freqs = ROPE_BASE ** (-(jnp.arange(AHDIM // 2).astype(jnp.float32) * 2.0 / AHDIM))
    angles = positions.astype(jnp.float32)[:, None] * freqs[None, :]
    return (jnp.cos(angles)[:, None, :], jnp.sin(angles)[:, None, :])


def rotate_half(values, cosine, sine_vals):
    half_dim = AHDIM // 2
    first_half = values[..., :half_dim]
    second_half = values[..., half_dim:]
    return jnp.concatenate(
        [
            first_half * cosine - second_half * sine_vals,
            first_half * sine_vals + second_half * cosine,
        ],
        axis=-1,
    )


def split_heads(cosine, sine_vals, qkv_rows):
    row_count = qkv_rows.shape[0]
    query_width = AHEADS * AHDIM
    key_width = KVHEADS * AHDIM
    queries = qkv_rows[:, :query_width].reshape(row_count, AHEADS, AHDIM)
    keys_rows = qkv_rows[:, query_width : query_width + key_width].reshape(
        row_count, KVHEADS, AHDIM
    )
    values_rows = qkv_rows[:, query_width + key_width :].reshape(row_count, KVHEADS, AHDIM)
    return (
        rotate_half(queries, cosine, sine_vals),
        rotate_half(keys_rows, cosine, sine_vals),
        values_rows,
    )


def on_device(
    tokens,
    segment_ids,
    norm1_gain,
    w_mamba_in,
    w_delta,
    conv_weight,
    conv_bias,
    delta_bias,
    decay_log,
    skip_gain,
    w_mamba_out,
    w_qkv,
    w_attn_out,
    norm2_gain,
    w_gate_up,
    w_down,
    cotangent,
):
    gathered = (
        lax.all_gather(norm1_gain, ("dp", "seq"), axis=0, tiled=True),
        lax.all_gather(w_mamba_in, ("dp", "seq"), axis=0, tiled=True),
        lax.all_gather(w_delta, ("dp", "seq"), axis=0, tiled=True),
        lax.all_gather(conv_weight, ("dp", "seq"), axis=1, tiled=True),
        lax.all_gather(conv_bias, ("dp", "seq"), axis=0, tiled=True),
        lax.all_gather(w_mamba_out, ("dp", "seq"), axis=0, tiled=True),
        lax.all_gather(w_qkv, ("dp", "seq"), axis=0, tiled=True),
        lax.all_gather(w_attn_out, ("dp", "seq"), axis=0, tiled=True),
        lax.all_gather(norm2_gain, ("dp", "seq"), axis=0, tiled=True),
        lax.all_gather(w_gate_up, ("dp", "seq"), axis=0, tiled=True),
        lax.all_gather(w_down, ("dp", "seq"), axis=0, tiled=True),
    )
    (
        gain_one,
        mamba_in,
        delta_proj,
        conv_kernel,
        conv_shift,
        mamba_outw,
        qkv_proj,
        attn_proj,
        gain_two,
        gate_up,
        down_proj,
    ) = gathered
    seq_rank = lax.axis_index("seq")
    row_count = tokens.shape[1]
    seg_full = segment_ids[0]
    seq_length = seg_full.shape[0]
    first_row = seq_rank * row_count
    tap_count = conv_kernel.shape[0]
    seg_padded = jnp.concatenate([jnp.full((tap_count - 1,), -1, jnp.int32), seg_full])
    seg_rows = lax.dynamic_slice_in_dim(seg_full, first_row, row_count)
    seg_before = lax.dynamic_slice_in_dim(seg_padded, first_row + tap_count - 2, 1)[0]
    taps = tap_masks(seg_padded, first_row, row_count, tap_count)
    inner_width = MHEADS * MHDIM
    inputs = tokens[0].astype(jnp.float32)
    normed_one, norm_one_back = jax.vjp(rms_gain, inputs, gain_one.astype(jnp.float32))
    normed_low = normed_one.astype(jnp.bfloat16)
    projected = jnp.dot(normed_low, mamba_in, preferred_element_type=jnp.float32).astype(
        jnp.bfloat16
    )
    delta_raw = jnp.dot(normed_low, delta_proj, preferred_element_type=jnp.float32)
    qkv_rows = jnp.dot(normed_low, qkv_proj, preferred_element_type=jnp.float32)
    z_rows = projected[:, :inner_width].astype(jnp.float32)
    conv_in = projected[:, inner_width:]
    halo_rows = from_behind(conv_in[row_count - tap_count + 1 :], "seq", 1)
    extended = jnp.concatenate([halo_rows, conv_in]).astype(jnp.float32)
    pre_values, pre_back = jax.vjp(
        partial(mamba_pre, taps),
        extended,
        delta_raw,
        conv_kernel.astype(jnp.float32),
        conv_shift.astype(jnp.float32),
        delta_bias.astype(jnp.float32),
        decay_log.astype(jnp.float32),
    )
    heads_in, b_proj, c_proj, step_size, log_decay = pre_values
    state_values, state_back = jax.vjp(
        partial(mamba_state, seg_rows, seg_before), heads_in, b_proj, step_size, log_decay
    )
    carry_gate, state_part = state_values
    identity = (jnp.ones_like(carry_gate), jnp.zeros_like(state_part))
    prefix = carried_in((carry_gate, state_part), "seq", compose_maps, identity)
    state_in = prefix[1]
    mixed_out, out_back = jax.vjp(
        partial(mamba_out, seg_rows, seg_before),
        heads_in,
        b_proj,
        c_proj,
        step_size,
        log_decay,
        state_in,
        skip_gain.astype(jnp.float32),
        z_rows,
    )
    mixed_low = mixed_out.astype(jnp.bfloat16)
    mixer = jnp.dot(mixed_low, mamba_outw, preferred_element_type=jnp.float32)
    positions = first_row + jnp.arange(row_count, dtype=jnp.int32)
    cosine, sine_vals = rope_tables(positions)
    rotated, rope_back = jax.vjp(partial(split_heads, cosine, sine_vals), qkv_rows)
    key_width = KVHEADS * AHDIM
    group_size = AHEADS // KVHEADS
    queries = rotated[0].astype(jnp.bfloat16)
    keyvals = jnp.concatenate(
        [rotated[1].reshape(row_count, key_width), rotated[2].reshape(row_count, key_width)], axis=1
    ).astype(jnp.bfloat16)
    all_keyvals = lax.all_gather(keyvals, "seq", axis=0, tiled=True)
    query_groups = queries.reshape(row_count, KVHEADS, group_size, AHDIM)
    block_len = min(512, seq_length)
    block_count = seq_length // block_len
    key_blocks = (
        all_keyvals.reshape(block_count, block_len, 2 * key_width),
        seg_full.reshape(block_count, block_len),
        jnp.arange(seq_length, dtype=jnp.int32).reshape(block_count, block_len),
    )
    score_scale = AHDIM ** (-0.5)

    def scores_for(block):
        block_kv, block_seg, block_pos = block
        keys_blk = block_kv[:, :key_width].reshape(block_len, KVHEADS, AHDIM)
        allowed = (block_pos[None, :] <= positions[:, None]) & (
            block_seg[None, :] == seg_rows[:, None]
        )
        raw_scores = (
            jnp.einsum("tgid,kgd->gitk", query_groups, keys_blk, preferred_element_type=jnp.float32)
            * score_scale
        )
        return jnp.where(allowed[None, None], raw_scores, NEGATIVE)

    def max_step(carry, block):
        running_top, running_sum = carry
        scores = scores_for(block)
        new_top = jnp.maximum(running_top, jnp.max(scores, axis=-1))
        running_sum = running_sum * jnp.exp(running_top - new_top) + jnp.sum(
            jnp.exp(scores - new_top[..., None]), axis=-1
        )
        return ((new_top, running_sum), None)

    start_top = jnp.full((KVHEADS, group_size, row_count), NEGATIVE, jnp.float32)
    (top_final, sum_final), _ = lax.scan(
        max_step, (start_top, jnp.zeros_like(start_top)), key_blocks
    )
    log_total = top_final + jnp.log(sum_final)

    def value_step(rounded_acc, block):
        probs = jnp.exp(scores_for(block) - log_total[..., None])
        vals_blk = block[0][:, key_width:].reshape(block_len, KVHEADS, AHDIM)
        rounded_acc = rounded_acc + jnp.einsum(
            "gitk,kgd->tgid",
            probs.astype(jnp.bfloat16),
            vals_blk,
            preferred_element_type=jnp.float32,
        )
        return (rounded_acc, None)

    empty_acc = jnp.zeros((row_count, KVHEADS, group_size, AHDIM), jnp.float32)
    attended, _ = lax.scan(value_step, empty_acc, key_blocks)
    attended_low = attended.reshape(row_count, AHEADS * AHDIM).astype(jnp.bfloat16)
    attn_rows = jnp.dot(attended_low, attn_proj, preferred_element_type=jnp.float32)
    residual = inputs + mixer + attn_rows
    normed_two, norm_two_back = jax.vjp(rms_gain, residual, gain_two.astype(jnp.float32))
    normed_two_low = normed_two.astype(jnp.bfloat16)
    gate_rows = jnp.dot(normed_two_low, gate_up, preferred_element_type=jnp.float32)
    hidden_full, swiglu_back = jax.vjp(swiglu, gate_rows)
    hidden_low = hidden_full.astype(jnp.bfloat16)
    block_out = (
        residual + jnp.dot(hidden_low, down_proj, preferred_element_type=jnp.float32)
    ).astype(jnp.bfloat16)
    again = (
        lax.all_gather(norm1_gain, ("dp", "seq"), axis=0, tiled=True),
        lax.all_gather(w_mamba_in, ("dp", "seq"), axis=0, tiled=True),
        lax.all_gather(w_delta, ("dp", "seq"), axis=0, tiled=True),
        lax.all_gather(conv_weight, ("dp", "seq"), axis=1, tiled=True),
        lax.all_gather(conv_bias, ("dp", "seq"), axis=0, tiled=True),
        lax.all_gather(w_mamba_out, ("dp", "seq"), axis=0, tiled=True),
        lax.all_gather(w_qkv, ("dp", "seq"), axis=0, tiled=True),
        lax.all_gather(w_attn_out, ("dp", "seq"), axis=0, tiled=True),
        lax.all_gather(norm2_gain, ("dp", "seq"), axis=0, tiled=True),
        lax.all_gather(w_gate_up, ("dp", "seq"), axis=0, tiled=True),
        lax.all_gather(w_down, ("dp", "seq"), axis=0, tiled=True),
    )
    upstream = cotangent[0].astype(jnp.float32)
    upstream_low = cotangent[0]
    grad_down = cross_rows(hidden_low, upstream_low)
    hidden_grad = times_transposed(upstream_low, again[10])
    (gate_grad,) = swiglu_back(hidden_grad)
    gate_grad_low = gate_grad.astype(jnp.bfloat16)
    grad_gate_up = cross_rows(normed_two_low, gate_grad_low)
    normed_two_grad = times_transposed(gate_grad_low, again[9])
    residual_part, grad_gain_two = norm_two_back(normed_two_grad)
    residual_grad = upstream + residual_part
    residual_low = residual_grad.astype(jnp.bfloat16)
    grad_mamba_out = cross_rows(mixed_low, residual_low)
    grad_attn_out = cross_rows(attended_low, residual_low)
    mixed_grad = times_transposed(residual_low, again[5])
    attended_grad = times_transposed(residual_low, again[7]).astype(jnp.bfloat16)
    out_groups = attended_grad.reshape(row_count, KVHEADS, group_size, AHDIM)
    row_delta = jnp.transpose(
        jnp.sum(out_groups.astype(jnp.float32) * attended, axis=-1), (1, 2, 0)
    )

    def grad_step(query_acc, block):
        probs = jnp.exp(scores_for(block) - log_total[..., None])
        keys_blk = block[0][:, :key_width].reshape(block_len, KVHEADS, AHDIM)
        vals_blk = block[0][:, key_width:].reshape(block_len, KVHEADS, AHDIM)
        prob_grad = jnp.einsum(
            "tgid,kgd->gitk", out_groups, vals_blk, preferred_element_type=jnp.float32
        )
        score_grad = (probs * (prob_grad - row_delta[..., None])).astype(jnp.bfloat16)
        query_acc = (
            query_acc
            + jnp.einsum("gitk,kgd->tgid", score_grad, keys_blk, preferred_element_type=jnp.float32)
            * score_scale
        )
        key_grad = (
            jnp.einsum(
                "gitk,tgid->kgd", score_grad, query_groups, preferred_element_type=jnp.float32
            )
            * score_scale
        )
        value_grad = jnp.einsum(
            "gitk,tgid->kgd",
            probs.astype(jnp.bfloat16),
            out_groups,
            preferred_element_type=jnp.float32,
        )
        return (
            query_acc,
            jnp.concatenate(
                [key_grad.reshape(block_len, key_width), value_grad.reshape(block_len, key_width)],
                axis=1,
            ),
        )

    query_grad, keyval_blocks = lax.scan(grad_step, empty_acc, key_blocks)
    keyval_grad = lax.psum_scatter(
        keyval_blocks.reshape(seq_length, 2 * key_width).astype(jnp.bfloat16),
        "seq",
        scatter_dimension=0,
        tiled=True,
    ).astype(jnp.float32)
    (qkv_grad,) = rope_back(
        (
            query_grad.reshape(row_count, AHEADS, AHDIM),
            keyval_grad[:, :key_width].reshape(row_count, KVHEADS, AHDIM),
            keyval_grad[:, key_width:].reshape(row_count, KVHEADS, AHDIM),
        )
    )
    qkv_low = qkv_grad.astype(jnp.bfloat16)
    grad_qkv = cross_rows(normed_low, qkv_low)
    normed_grad = times_transposed(qkv_low, again[6])
    heads_grad, b_grad, c_grad, step_grad, decay_grad, state_in_grad, skip_grad, z_grad = out_back(
        mixed_grad
    )
    suffix = carried_in_2((carry_gate, state_in_grad), "seq", compose_maps, identity)
    state_out_grad = suffix[1]
    gate_grad_total = jnp.sum(state_out_grad * state_in, axis=(1, 2))
    heads_more, b_more, step_more, decay_more = state_back((gate_grad_total, state_out_grad))
    pre_grads = pre_back(
        (
            heads_grad + heads_more,
            b_grad + b_more,
            c_grad,
            step_grad + step_more,
            decay_grad + decay_more,
        )
    )
    ext_grad, delta_grad, kernel_grad, shift_grad, bias_grad, decay_log_grad = pre_grads
    incoming = from_behind(ext_grad[: tap_count - 1], "seq", -1)
    conv_grad = ext_grad[tap_count - 1 :]
    conv_grad = jnp.concatenate(
        [conv_grad[: row_count - tap_count + 1], conv_grad[row_count - tap_count + 1 :] + incoming]
    )
    projected_grad = jnp.concatenate([z_grad, conv_grad], axis=1).astype(jnp.bfloat16)
    grad_mamba_in = cross_rows(normed_low, projected_grad)
    normed_grad = normed_grad + times_transposed(projected_grad, again[1])
    delta_low = delta_grad.astype(jnp.bfloat16)
    grad_delta = cross_rows(normed_low, delta_low)
    normed_grad = normed_grad + times_transposed(delta_low, again[2])
    input_part, grad_gain_one = norm_one_back(normed_grad)
    input_grad = residual_grad + input_part
    owned = (
        lax.psum_scatter(grad_gain_one, ("dp", "seq"), scatter_dimension=0, tiled=True),
        lax.psum_scatter(grad_mamba_in, ("dp", "seq"), scatter_dimension=0, tiled=True),
        lax.psum_scatter(grad_delta, ("dp", "seq"), scatter_dimension=0, tiled=True),
        lax.psum_scatter(kernel_grad, ("dp", "seq"), scatter_dimension=1, tiled=True),
        lax.psum_scatter(shift_grad, ("dp", "seq"), scatter_dimension=0, tiled=True),
        lax.psum_scatter(grad_mamba_out, ("dp", "seq"), scatter_dimension=0, tiled=True),
        lax.psum_scatter(grad_qkv, ("dp", "seq"), scatter_dimension=0, tiled=True),
        lax.psum_scatter(grad_attn_out, ("dp", "seq"), scatter_dimension=0, tiled=True),
        lax.psum_scatter(grad_gain_two, ("dp", "seq"), scatter_dimension=0, tiled=True),
        lax.psum_scatter(grad_gate_up, ("dp", "seq"), scatter_dimension=0, tiled=True),
        lax.psum_scatter(grad_down, ("dp", "seq"), scatter_dimension=0, tiled=True),
    )
    head_grads = lax.psum((bias_grad, decay_log_grad, skip_grad), ("dp", "seq"))
    return (
        block_out[None],
        input_grad[None],
        owned[0],
        owned[1],
        owned[2],
        owned[3],
        owned[4],
        head_grads[0],
        head_grads[1],
        head_grads[2],
        owned[5],
        owned[6],
        owned[7],
        owned[8],
        owned[9],
        owned[10],
    )


def solution(mesh):
    in_specs = (
        P("dp", "seq", None),
        P("dp", None),
        P(("dp", "seq")),
        P(("dp", "seq"), None),
        P(("dp", "seq"), None),
        P(None, ("dp", "seq")),
        P(("dp", "seq")),
        P(),
        P(),
        P(),
        P(("dp", "seq"), None),
        P(("dp", "seq"), None),
        P(("dp", "seq"), None),
        P(("dp", "seq")),
        P(("dp", "seq"), None),
        P(("dp", "seq"), None),
        P("dp", "seq", None),
    )
    out_specs = (
        P("dp", "seq", None),
        P("dp", "seq", None),
        P(("dp", "seq")),
        P(("dp", "seq"), None),
        P(("dp", "seq"), None),
        P(None, ("dp", "seq")),
        P(("dp", "seq")),
        P(),
        P(),
        P(),
        P(("dp", "seq"), None),
        P(("dp", "seq"), None),
        P(("dp", "seq"), None),
        P(("dp", "seq")),
        P(("dp", "seq"), None),
        P(("dp", "seq"), None),
    )
    return jax.shard_map(
        on_device, mesh=mesh, in_specs=in_specs, out_specs=out_specs, check_vma=False
    )
```

profile of v0, /device:TPU:0, one launch (start us, length us, event | category | flops | bytes accessed | tf_op | source)
XLA Modules:
  0.0 1934.8 jit_solution(6124527263256673677)
XLA Ops:
  20.5 42.2 %all-reduce.30 = (bf16[1024]{0:T(1024)(128)(2,1)S(1)}, bf16[1792]{0:T(1024)(128)(2,1)S(1)}, bf16[1024]{0:T(1024)(128)(2,1)S(1)}) all-reduce(bf16[1024]{0:T(1024)(128)(2,1)S(1)} %dynamic-update-slice, bf16[1792]{0:T(1024)(128)(2,1)S(1)} %dynamic-update-slice.1, ...), channel_id=1, replica_groups=mesh['dp'=16,'seq'=2] {'dp','seq'}, use_global_device_ids=true, to_apply=%add.22 | all-reduce | flops 3840 | bytes 15360
  67.9 66.5 %all-gather.3 = bf16[32,56,4]{1,2,0:T(4,128)(2,1)S(1)} all-gather(bf16[1,56,4]{1,2,0:T(4,128)(2,1)} %bitcast.555), channel_id=1, replica_groups=mesh['dp'=16,'seq'=2] {'dp','seq'}, dimensions={0}, use_global_device_ids=true | all-gather | bytes 14784 | tf_op jit(solution)/shard_map/all_gather | solution.py:238
  135.8 65.1 %all-gather.2 = bf16[32,32,24]{1,2,0:T(8,128)(2,1)S(1)} all-gather(bf16[1,32,24]{1,2,0:T(8,128)(2,1)} %bitcast.553), channel_id=1, replica_groups=mesh['dp'=16,'seq'=2] {'dp','seq'}, dimensions={0}, use_global_device_ids=true | all-gather | bytes 50688 | tf_op jit(solution)/shard_map/all_gather | solution.py:237
  228.0 20.6 %while.66 = (s32[]{:T(128)}, f32[2,4,512]{2,1,0:T(4,128)S(1)}, f32[2,4,512]{2,1,0:T(4,128)S(1)}, s32[2,512]{1,0:T(2,128)S(1)}, s32[2,512]{1,0:T(2,128)S(1)}, /*i...) while((s32[]{:T(128)}, f32[2,4,512]{2,1,0:T(4,128)S(1)}, ...), condition=%wide.region_8.9_spmd.clone, body=%wide.region_5.8_spmd.clone.sunk | while | flops 283922944 | bytes 19237004 | solution.py:355
  288.7 14.0 all-gather
  310.0 31.2 %fusion.75 = f32[512,24,64]{0,2,1:T(8,128)} fusion(f32[512,24,64]{0,2,1:T(8,128)S(1)} %bitcast.498, f32[512,24,64]{0,2,1:T(8,128)S(1)} %fusion.134, f32[512,512]{1,0:T(8,128)S(1)} %copy-done.49, f32[512,24]{0,1:T(8,128)S(1)} %copy-done.72, pred[512,512]{1,0:T(8,128)(4,1)S(1)} %copy-done.62, f32[24]{0:T(128)S(1)} %copy-done.113, ...), kind=kOutput, calls=%fused_computation.127 | convolution fusion | flops 4860936192 | bytes 10895456 | tf_op jit(solution)/shard_map/jvp(tsh,shp->thp)/dot_general | solution.py:165
  357.6 11.2 fusion.185
  368.9 40.0 %all-gather.22.cloned.1.call-done = bf16[2048,1024]{1,0:T(8,128)(2,1)} async-done(((bf16[64,1024]{1,0:T(8,128)(2,1)}), bf16[2048,1024]{1,0:T(8,128)(2,1)}) %all-gather.22.cloned.1.call-update) | async-done | bytes 4194320 | tf_op jit(solution)/shard_map/all_gather | solution.py:245
  408.9 9.9 fusion.129
  418.8 10.5 multiply_reduce_fusion.7
  442.8 25.7 %fusion.44 = f32[24,64,512]{2,1,0:T(8,128)} fusion(f32[24,64,512]{2,1,0:T(8,128)S(1)} %bitcast.490, f32[512,512]{1,0:T(8,128)} %fusion.139, f32[512,24]{0,1:T(8,128)} %copy-done.71, pred[512,512]{1,0:T(8,128)(4,1)S(1)} %copy-done.62), kind=kOutput, calls=%fused_computation.67 | convolution fusion | flops 4857004032 | bytes 7651328 | tf_op jit(solution)/shard_map/transpose(jvp(tsh,shp->thp))/dot_general | solution.py:165
  468.6 34.4 %fusion.49 = (f32[512,24]{0,1:T(8,128)}, f32[512,24]{0,1:T(8,128)}, f32[512,512]{1,0:T(8,128)}) fusion(f32[512,512]{1,0:T(8,128)S(1)} %copy-done.50, f32[512,24]{0,1:T(8,128)S(1)} %copy-done.73, pred[512,512]{1,0:T(8,128)(4,1)S(1)} %copy-done.62, f32[24,64,512]{2,1,0:T(8,128)S(1)} %bitcast.491, f32[512,24,64]{0,2,1:T(8,128)S(1)} %bitcast.499, ...), kind=kOutput, calls=%fused_computation.70 | convolution fusion | flops 4901543936 | bytes 8847360 | tf_op jit(solution)/shard_map/transpose(jvp(tsh,shp->thp))/dot_general | solution.py:165
  507.6 12.1 all-gather.1
  526.1 9.0 multiply_reduce_fusion.6
  539.5 35.2 %while.68 = (s32[]{:T(128)}, f32[512,2,4,64]{0,3,2,1:T(8,128)S(1)}, bf16[2,512,256]{2,1,0:T(8,128)(2,1)}, bf16[2,512,256]{1,2,0:T(8,128)(2,1)S(1)}, s32[2,512]{1...) while((s32[]{:T(128)}, f32[512,2,4,64]{0,3,2,1:T(8,128)S(1)}, ...), condition=%wide.region_15.16_spmd.clone, body=%wide.region_14.15_spmd.clone.sunk | while | flops 1365377536 | bytes 96405720 | solution.py:450
  657.7 11.8 fusion.127
  682.6 41.8 %reduce-scatter.26.cloned.1.call-done = f32[32,24]{1,0:T(8,128)} async-done(((f32[1024,24]{1,0:T(8,128)}), f32[32,24]{1,0:T(8,128)}) %reduce-scatter.26.cloned.1.call-update) | async-done | bytes 3088
  737.7 38.2 %all-reduce.29 = (f32[1024]{0:T(1024)S(1)}, f32[4,1792]{1,0:T(4,128)S(1)}, f32[1792]{0:T(1024)S(1)}, f32[24]{0:T(128)}, f32[24]{0:T(128)}, /*index=5*/f32[24]{0:T(128)}, f32[1024]{0:T(1024)S(1)}) all-reduce(f32[1024]{0:T(1024)S(1)} %get-tuple-element.643, ...), channel_id=5, replica_groups=mesh['dp'=16,'seq'=2] {'dp','seq'}, use_global_device_ids=true, to_apply=%region_33.34.clone | all-reduce | flops 11080 | bytes 88640
  783.2 77.6 %reduce-scatter.20.cloned.1.call-done = f32[16,1024]{1,0:T(8,128)} async-done(((f32[512,1024]{1,0:T(8,128)}), f32[16,1024]{1,0:T(8,128)}) %reduce-scatter.20.cloned.1.call-update) | async-done | bytes 65552 | tf_op jit(solution)/shard_map/reduce_scatter | solution.py:505
  860.8 104.2 %reduce-scatter.18.cloned.1.call-done = f32[32,768]{1,0:T(8,128)} async-done(((f32[1024,768]{1,0:T(8,128)}), f32[32,768]{1,0:T(8,128)}) %reduce-scatter.18.cloned.1.call-update) | async-done | bytes 98320 | tf_op jit(solution)/shard_map/reduce_scatter | solution.py:504
  965.0 120.5 %reduce-scatter.16.cloned.1.call-done = f32[48,1024]{1,0:T(8,128)} async-done(((f32[1536,1024]{1,0:T(8,128)}), f32[48,1024]{1,0:T(8,128)}) %reduce-scatter.16.cloned.1.call-update) | async-done | bytes 196624 | tf_op jit(solution)/shard_map/reduce_scatter | solution.py:503
  1085.4 185.1 %reduce-scatter.24.cloned.1.call-done = f32[64,1024]{1,0:T(8,128)} async-done(((f32[2048,1024]{1,0:T(8,128)}), f32[64,1024]{1,0:T(8,128)}) %reduce-scatter.24.cloned.1.call-update) | async-done | bytes 262160 | tf_op jit(solution)/shard_map/reduce_scatter | solution.py:508
  1270.5 295.9 %reduce-scatter.14.cloned.1.call-done = f32[32,3328]{1,0:T(8,128)} async-done(((f32[1024,3328]{1,0:T(8,128)}), f32[32,3328]{1,0:T(8,128)}) %reduce-scatter.14.cloned.1.call-update) | async-done | bytes 426000 | tf_op jit(solution)/shard_map/reduce_scatter | solution.py:499
  1566.4 361.6 %reduce-scatter.22.cloned.1.call-done = f32[32,4096]{1,0:T(8,128)} async-done(((f32[1024,4096]{1,0:T(8,128)}), f32[32,4096]{1,0:T(8,128)}) %reduce-scatter.22.cloned.1.call-update) | async-done | bytes 524304 | tf_op jit(solution)/shard_map/reduce_scatter | solution.py:507
  (502 shorter events, 321.2 us)
Async XLA Ops:
  7.2 205.5 %copy-start.21 = (bf16[1,512,1024]{2,1,0:T(8,128)(2,1)S(1)}, bf16[1,512,1024]{2,1,0:T(8,128)(2,1)}, u32[]{:S(2)}) copy-start(bf16[1,512,1024]{2,1,0:T(8,128)(2,1)} %param.27) | copy-start | bytes 3145732
  7.2 203.9 %copy-start.116 = (bf16[24]{0:T(256)(128)(2,1)S(1)}, bf16[24]{0:T(256)(128)(2,1)}, u32[]{:S(2)}) copy-start(bf16[24]{0:T(256)(128)(2,1)} %param.36) | copy-start | bytes 148
  7.2 205.5 %all-gather.16.cloned.1.call-start = ((), (), s32[]{:S(2)}) async-start(), calls=%async_computation.10 | async-start | bytes 1622016 | tf_op jit(solution)/shard_map/all_gather | solution.py:241
  7.9 241.3 %all-gather.12.cloned.1.call-start = ((), (), s32[]{:S(2)}) async-start(), calls=%async_computation.8 | async-start | bytes 7028736 | tf_op jit(solution)/shard_map/all_gather | solution.py:236
  8.7 340.3 %all-gather.14.cloned.1.call-start = ((), (), s32[]{:S(2)}) async-start(), calls=%async_computation.9 | async-start | bytes 3244032 | tf_op jit(solution)/shard_map/all_gather | solution.py:240
  9.4 345.2 %all-gather.18.cloned.1.call-start = ((), (), s32[]{:S(2)}) async-start(), calls=%async_computation.11 | async-start | bytes 1081344 | tf_op jit(solution)/shard_map/all_gather | solution.py:242
  10.0 347.6 %all-gather.20.cloned.1.call-start = ((), (), s32[]{:S(2)}) async-start(), calls=%async_computation.12 | async-start | bytes 8650752 | tf_op jit(solution)/shard_map/all_gather | solution.py:244
  10.6 398.3 %all-gather.22.cloned.1.call-start = ((), (), s32[]{:S(2)}) async-start(), calls=%async_computation.13 | async-start | bytes 4325376 | tf_op jit(solution)/shard_map/all_gather | solution.py:245
  11.2 584.0 %reduce-scatter.12.cloned.1.call-start = ((), (), s32[]{:S(2)}) async-start(), calls=%async_computation.14 | async-start | bytes 786432 | tf_op jit(solution)/shard_map/reduce_scatter | solution.py:451
  17.1 198.1 %copy-start.106 = (pred[512]{0:T(512)(128)(4,1)}, pred[512]{0:T(512)(128)(4,1)S(1)}, u32[]{:S(2)}) copy-start(pred[512]{0:T(512)(128)(4,1)S(1)} %get-tuple-element.795) | copy-start | bytes 1540
  17.1 198.1 %copy-start.108 = (pred[512]{0:T(512)(128)(4,1)}, pred[512]{0:T(512)(128)(4,1)S(1)}, u32[]{:S(2)}) copy-start(pred[512]{0:T(512)(128)(4,1)S(1)} %get-tuple-element.794) | copy-start | bytes 1540
  62.7 186.5 %copy-start.56 = (f32[1024]{0:T(1024)}, f32[1024]{0:T(1024)S(1)}, u32[]{:S(2)}) copy-start(f32[1024]{0:T(1024)S(1)} %convert_element_type.178) | copy-start | bytes 12292
  64.3 185.0 %copy-start.64 = (f32[512]{0:T(512)}, f32[512]{0:T(512)S(1)}, u32[]{:S(2)}) copy-start(f32[512]{0:T(512)S(1)} %fusion.173) | copy-start | bytes 6148
  135.2 137.9 %copy-start.80 = (f32[1792]{0:T(1024)}, f32[1792]{0:T(1024)S(1)}, u32[]{:S(2)}) copy-start(f32[1792]{0:T(1024)S(1)} %get-tuple-element.649) | copy-start | bytes 21508
  211.6 217.7 %copy-start.86 = (f32[1024]{0:T(1024)}, f32[1024]{0:T(1024)S(1)}, u32[]{:S(2)}) copy-start(f32[1024]{0:T(1024)S(1)} %convert_element_type.196) | copy-start | bytes 12292
  258.0 13.2 collective-permute-start
  574.8 149.6 %reduce-scatter.26.cloned.1.call-start = ((), (), s32[]{:S(2)}) async-start(), calls=%async_computation.21 | async-start | bytes 540672
  591.4 269.3 %reduce-scatter.20.cloned.1.call-start = ((), (), s32[]{:S(2)}) async-start(), calls=%async_computation.18 | async-start | bytes 2162688 | tf_op jit(solution)/shard_map/reduce_scatter | solution.py:505
  593.6 371.4 %reduce-scatter.18.cloned.1.call-start = ((), (), s32[]{:S(2)}) async-start(), calls=%async_computation.17 | async-start | bytes 3244032 | tf_op jit(solution)/shard_map/reduce_scatter | solution.py:504
  600.6 484.8 %reduce-scatter.16.cloned.1.call-start = ((), (), s32[]{:S(2)}) async-start(), calls=%async_computation.16 | async-start | bytes 6488064 | tf_op jit(solution)/shard_map/reduce_scatter | solution.py:503
  606.5 664.0 %reduce-scatter.24.cloned.1.call-start = ((), (), s32[]{:S(2)}) async-start(), calls=%async_computation.20 | async-start | bytes 8650752 | tf_op jit(solution)/shard_map/reduce_scatter | solution.py:508
  614.1 952.3 %reduce-scatter.14.cloned.1.call-start = ((), (), s32[]{:S(2)}) async-start(), calls=%async_computation.15 | async-start | bytes 14057472 | tf_op jit(solution)/shard_map/reduce_scatter | solution.py:499
  642.7 5.8 collective-permute-start.1
  656.1 1271.9 %reduce-scatter.22.cloned.1.call-start = ((), (), s32[]{:S(2)}) async-start(), calls=%async_computation.19 | async-start | bytes 17301504 | tf_op jit(solution)/shard_map/reduce_scatter | solution.py:507
  (114 other events, 1555.8 us)
Sparse Core Ops, SparseCore 0:
  10.9 57.9 all-gather.15
  71.8 71.5 all-gather.11
  146.3 57.8 all-gather.13
  206.9 52.7 all-gather.17
  262.6 82.6 all-gather.19
  348.2 60.6 all-gather.21
  574.9 13.1 reduce-scatter.11
  591.5 132.8 reduce-scatter.25
  727.2 133.4 reduce-scatter.19
  867.5 97.4 reduce-scatter.17
  972.1 113.2 reduce-scatter.15
  1088.2 182.3 reduce-scatter.23
  1273.4 292.9 reduce-scatter.13
  1569.1 358.8 reduce-scatter.21
where the time goes:
time: 1950 us; the launch traced here: 1930 us
  waiting for transfers between devices  1230 us (63%)
  matrix products  303 us (16%)
  blocking collectives  249 us (13%)
  other arithmetic  72.9 us (4%)
  local copies, waits for them, and re-layouts  52.1 us (3%)
    reduce_scatter x1, waiting for transfers between devices, on_device(): lax.psum_scatter(grad_gate_up, ('dp', 'seq'), scatter_dimension=0, tiled=...  362 us
    reduce_scatter x1, waiting for transfers between devices, on_device(): lax.psum_scatter(grad_mamba_in, ('dp', 'seq'), scatter_dimension=0, tiled...  296 us
    reduce_scatter x1, waiting for transfers between devices, on_device(): lax.psum_scatter(grad_down, ('dp', 'seq'), scatter_dimension=0, tiled=True)  185 us
    reduce_scatter x1, waiting for transfers between devices, on_device(): lax.psum_scatter(grad_mamba_out, ('dp', 'seq'), scatter_dimension=0, tile...  120 us
    reduce_scatter x1, waiting for transfers between devices, on_device(): lax.psum_scatter(grad_qkv, ('dp', 'seq'), scatter_dimension=0, tiled=True)  104 us
    dot_general x3, matrix products, mamba_out(): jnp.einsum('tsh,shp->thp', decay_map * cross_terms[:, :, None], step_size...  91.3 us
    unnamed x2, blocking collectives  80.3 us
    reduce_scatter x1, waiting for transfers between devices, on_device(): lax.psum_scatter(grad_attn_out, ('dp', 'seq'), scatter_dimension=0, tiled...  77.6 us
  transfers between devices with their start and end apart: 16, of which 9 were waited for; matrix products, arithmetic and copies ran while one was open for 14% of the time, Pallas kernels for 0%

commit v1 on v0

v1 whole, which is shorter than its diff:
```python
import math
from functools import partial

import jax
import jax.numpy as jnp
from jax import lax
from jax.experimental import pallas as pl
from jax.experimental.pallas import tpu as pltpu
from jax.sharding import PartitionSpec as P

MHEADS = 24
MHDIM = 64
STATE = 128
AHEADS = 8
KVHEADS = 2
AHDIM = 64

INNER = MHEADS * MHDIM
CONVD = INNER + 2 * STATE
QWIDTH = AHEADS * AHDIM
KWIDTH = KVHEADS * AHDIM
GROUPS = 3
GHEADS = MHEADS // GROUPS
GLANES = GHEADS * MHDIM
STRIP = 128

EPSILON = 1e-05
ROPE_BASE = 100000000000.0
NEGATIVE = -1e30
LOG2E = math.log2(math.e)

F32 = jnp.float32
BF16 = jnp.bfloat16


def dot_nn(a, b):
    return lax.dot_general(a, b, (((1,), (0,)), ((), ())), preferred_element_type=F32)


def dot_nt(a, b):
    return lax.dot_general(a, b, (((1,), (1,)), ((), ())), preferred_element_type=F32)


def dot_tn(a, b):
    return lax.dot_general(a, b, (((0,), (0,)), ((), ())), preferred_element_type=F32)


def mesh_bits():
    bits = []
    for axis in ("dp", "seq"):
        size = lax.axis_size(axis)
        level = size // 2
        while level:
            bits.append((axis, level))
            level //= 2
    return bits


def bit_orders():
    bits = mesh_bits()
    seq = [b for b in bits if b[0] == "seq"][::-1]
    dp = [b for b in bits if b[0] == "dp"][::-1]
    pair, second, rest = dp[:1], dp[1:2], dp[2:]
    return (
        pair + seq + second + rest,
        pair + second + rest + seq,
        pair + rest + seq + second,
    )


def swap(value, bit):
    axis, level = bit
    size = lax.axis_size(axis)
    return lax.ppermute(value, axis, [(i, i ^ level) for i in range(size)])


def bit_here(bit):
    axis, level = bit
    return (lax.axis_index(axis) // level) % 2


def halve(full, order):
    left = mesh_bits()
    total = full.shape[0]
    rows = total >> len(left)
    value = full.reshape((2,) * len(left) + (rows, full.shape[1]))
    for bit in order:
        place = left.index(bit)
        here = bit_here(bit)
        out = lax.dynamic_index_in_dim(value, 1 - here, place, keepdims=False)
        kept = lax.dynamic_index_in_dim(value, here, place, keepdims=False)
        got = swap(out, bit)
        left.remove(bit)
        value = kept.astype(F32) + got.astype(F32)
        if left:
            value = value.astype(BF16)
    return value


def double(shard, order):
    bits = mesh_bits()
    held = []
    value = shard
    for bit in reversed(order):
        got = swap(value, bit)
        here = bit_here(bit)
        held = [b for b in bits if b in held or b == bit]
        place = held.index(bit)
        low = jnp.where(here == 0, value, got)
        high = jnp.where(here == 0, got, value)
        value = jnp.stack([low, high], axis=place)
    return value.reshape((shard.shape[0] << len(bits), shard.shape[1]))


def total_everywhere(value):
    for bit in mesh_bits():
        value = value + swap(value, bit)
    return value


def compose_maps(earlier, later):
    return (later[0] * earlier[0], later[0][None, :] * earlier[1] + later[1])


def state_from_behind(gate, part):
    count = lax.axis_size("seq")
    low = part.astype(BF16)
    if count == 2:
        return lax.ppermute(low, "seq", [(0, 1)]).astype(F32)
    gates = lax.all_gather(gate.astype(BF16), "seq")
    parts = lax.all_gather(low, "seq")
    start = (jnp.ones_like(gate), jnp.zeros_like(part))

    def one(step, state):
        return compose_maps(
            state,
            (
                lax.dynamic_index_in_dim(gates, step, 0, False).astype(F32),
                lax.dynamic_index_in_dim(parts, step, 0, False).astype(F32),
            ),
        )

    return lax.fori_loop(0, lax.axis_index("seq"), one, start)[1]


def state_from_ahead(gate, part):
    count = lax.axis_size("seq")
    low = part.astype(BF16)
    if count == 2:
        return lax.ppermute(low, "seq", [(1, 0)]).astype(F32)
    gates = lax.all_gather(gate.astype(BF16), "seq")
    parts = lax.all_gather(low, "seq")
    start = (jnp.ones_like(gate), jnp.zeros_like(part))
    place = lax.axis_index("seq")

    def one(step, state):
        at = count - 1 - step
        return compose_maps(
            state,
            (
                lax.dynamic_index_in_dim(gates, at, 0, False).astype(F32),
                lax.dynamic_index_in_dim(parts, at, 0, False).astype(F32),
            ),
        )

    return lax.fori_loop(0, count - 1 - place, one, start)[1]


def neighbour(value, steps):
    count = lax.axis_size("seq")
    first, last = (max(0, -steps), min(count, count - steps))
    return lax.ppermute(value, "seq", [(s, s + steps) for s in range(first, last)])


PARAMS = pltpu.CompilerParams(vmem_limit_bytes=48 * 1024 * 1024)


def lane_is_low(rows):
    return lax.broadcasted_iota(jnp.int32, (rows, 128), 1) < MHDIM


def spread(low, vec, head):
    return jnp.where(low, vec[:, head : head + 1], vec[:, head + 1 : head + 2])


def ssd_forward_kernel(x_ref, b_ref, c_ref, vec_ref, row_ref, segc_ref, segr_ref, y_ref, st_ref, cb_ref):
    length = x_ref.shape[0]

    @pl.when(pl.program_id(0) == 0)
    def _():
        t = lax.broadcasted_iota(jnp.int32, (length, length), 0)
        s = lax.broadcasted_iota(jnp.int32, (length, length), 1)
        seen = (t >= s) & (segc_ref[...] == segr_ref[...])
        cb = dot_nt(c_ref[...].astype(BF16), b_ref[...].astype(BF16))
        cb_ref[...] = jnp.where(seen, cb, 0.0)

    b_low = b_ref[...].astype(BF16)
    wide = lane_is_low(length)
    narrow = lane_is_low(STRIP)
    dt = vec_ref[0, :, 0:GHEADS]
    rem = vec_ref[0, :, 2 * GHEADS : 3 * GHEADS]
    for pair in range(GHEADS // 2):
        lanes = slice(pair * 128, (pair + 1) * 128)
        xd = x_ref[:, lanes] * spread(wide, dt, 2 * pair)
        xd_low = xd.astype(BF16)
        st_ref[:, lanes] = dot_tn(b_low, (xd * spread(wide, rem, 2 * pair)).astype(BF16))
        for strip in range(length // STRIP):
            first, width = strip * STRIP, (strip + 1) * STRIP
            halves = []
            for head in (2 * pair, 2 * pair + 1):
                at = GHEADS + head
                gap = vec_ref[0, first : first + STRIP, at : at + 1] - row_ref[head : head + 1, :width]
                decay = jnp.exp2(jnp.minimum(gap, 0.0))
                m = (decay * cb_ref[first : first + STRIP, :width]).astype(BF16)
                halves.append(dot_nn(m, xd_low[:width]))
            y_ref[first : first + STRIP, lanes] = jnp.where(narrow, halves[0], halves[1])


def group_specs(length):
    x_spec = pl.BlockSpec((length, GLANES), lambda g: (0, g))
    s_spec = pl.BlockSpec((STATE, GLANES), lambda g: (0, g))
    n_spec = pl.BlockSpec((length, STATE), lambda g: (0, 0))
    v_spec = pl.BlockSpec((1, length, 4 * GHEADS), lambda g: (g, 0, 0))
    r_spec = pl.BlockSpec((GHEADS, length), lambda g: (g, 0))
    return x_spec, s_spec, n_spec, v_spec, r_spec


def ssd_forward(x, b, c, vec, row, seg_col, seg_row):
    length = x.shape[0]
    x_spec, s_spec, n_spec, v_spec, r_spec = group_specs(length)
    return pl.pallas_call(
        ssd_forward_kernel,
        grid=(GROUPS,),
        in_specs=[
            x_spec, n_spec, n_spec, v_spec, r_spec,
            pl.BlockSpec((length, 1), lambda g: (0, 0)),
            pl.BlockSpec((1, length), lambda g: (0, 0)),
        ],
        out_specs=[x_spec, s_spec],
        out_shape=[
            jax.ShapeDtypeStruct((length, INNER), F32),
            jax.ShapeDtypeStruct((STATE, INNER), F32),
        ],
        scratch_shapes=[pltpu.VMEM((length, length), F32)],
        compiler_params=PARAMS,
        name="ssd_forward",
    )(x, b, c, vec, row, seg_col, seg_row)


def silu_parts(v):
    sig = 1.0 / (1.0 + jnp.exp(-v))
    return v * sig, sig * (1.0 + v * (1.0 - sig))


def ssd_finish_kernel(y0_ref, x_ref, z_ref, c_ref, st_ref, vec_ref, skip_ref, y_ref, ym_ref):
    length = x_ref.shape[0]
    wide = lane_is_low(length)
    ent = vec_ref[0, :, 3 * GHEADS : 4 * GHEADS]
    c_low = c_ref[...].astype(BF16)
    for pair in range(GHEADS // 2):
        lanes = slice(pair * 128, (pair + 1) * 128)
        cs = dot_nn(c_low, st_ref[:, lanes].astype(BF16))
        y = y0_ref[:, lanes] + spread(wide, ent, 2 * pair) * cs + skip_ref[:, lanes] * x_ref[:, lanes]
        gate, _ = silu_parts(z_ref[:, lanes].astype(F32))
        y_ref[:, lanes] = y
        ym_ref[:, lanes] = (y * gate).astype(BF16)


def ssd_finish(y0, x, z, c, state, vec, skip):
    length = x.shape[0]
    x_spec, s_spec, n_spec, v_spec, _ = group_specs(length)
    return pl.pallas_call(
        ssd_finish_kernel,
        grid=(GROUPS,),
        in_specs=[x_spec, x_spec, x_spec, n_spec, s_spec, v_spec, pl.BlockSpec((1, GLANES), lambda g: (0, g))],
        out_specs=[x_spec, x_spec],
        out_shape=[
            jax.ShapeDtypeStruct((length, INNER), F32),
            jax.ShapeDtypeStruct((length, INNER), BF16),
        ],
        compiler_params=PARAMS,
        name="ssd_finish",
    )(y0, x, z, c, state, vec, skip)


def ssd_gate_kernel(dym_ref, y_ref, x_ref, z_ref, c_ref, vec_ref, dy_ref, dz_ref, ds_ref, skip_ref):
    length = x_ref.shape[0]
    wide = lane_is_low(length)
    ent = vec_ref[0, :, 3 * GHEADS : 4 * GHEADS]
    c_low = c_ref[...].astype(BF16)
    for pair in range(GHEADS // 2):
        lanes = slice(pair * 128, (pair + 1) * 128)
        gate, slope = silu_parts(z_ref[:, lanes].astype(F32))
        dym = dym_ref[:, lanes]
        dy = dym * gate
        dy_ref[:, lanes] = dy
        dz_ref[:, lanes] = (dym * y_ref[:, lanes] * slope).astype(BF16)
        ds_ref[:, lanes] = dot_tn(c_low, (dy * spread(wide, ent, 2 * pair)).astype(BF16))
        skip_ref[:, lanes] = jnp.sum(dy * x_ref[:, lanes], axis=0, keepdims=True)


def ssd_gate(dym, y, x, z, c, vec):
    length = x.shape[0]
    x_spec, s_spec, n_spec, v_spec, _ = group_specs(length)
    one_spec = pl.BlockSpec((1, GLANES), lambda g: (0, g))
    return pl.pallas_call(
        ssd_gate_kernel,
        grid=(GROUPS,),
        in_specs=[x_spec, x_spec, x_spec, x_spec, n_spec, v_spec],
        out_specs=[x_spec, x_spec, s_spec, one_spec],
        out_shape=[
            jax.ShapeDtypeStruct((length, INNER), F32),
            jax.ShapeDtypeStruct((length, INNER), BF16),
            jax.ShapeDtypeStruct((STATE, INNER), F32),
            jax.ShapeDtypeStruct((1, INNER), F32),
        ],
        compiler_params=PARAMS,
        name="ssd_gate",
    )(dym, y, x, z, c, vec)


def ssd_backward_kernel(
    x_ref, dy_ref, b_ref, c_ref, st_ref, dst_ref, vec_ref, row_ref, segc_ref, segr_ref, skip_ref,
    dx_ref, db_ref, dc_ref, cols_ref, rows_ref, bc_ref, dbc_ref, xd_ref, sum_ref,
):
    length = x_ref.shape[0]
    group = pl.program_id(0)

    @pl.when(group == 0)
    def _():
        s = lax.broadcasted_iota(jnp.int32, (length, length), 0)
        t = lax.broadcasted_iota(jnp.int32, (length, length), 1)
        seen = (t >= s) & (segc_ref[...] == segr_ref[...])
        bc = dot_nt(b_ref[...].astype(BF16), c_ref[...].astype(BF16))
        bc_ref[...] = jnp.where(seen, bc, 0.0)
        dbc_ref[...] = jnp.zeros_like(dbc_ref)
        db_ref[...] = jnp.zeros_like(db_ref)
        dc_ref[...] = jnp.zeros_like(dc_ref)
        cols_ref[...] = jnp.zeros_like(cols_ref)

    b_low = b_ref[...].astype(BF16)
    c_low = c_ref[...].astype(BF16)
    wide = lane_is_low(length)
    narrow = lane_is_low(STRIP)
    lane = lax.broadcasted_iota(jnp.int32, (STRIP, 128), 1)
    spot = lax.broadcasted_iota(jnp.int32, (128, 128), 0) // MHDIM
    place = lax.broadcasted_iota(jnp.int32, (128, 128), 1)
    dt = vec_ref[0, :, 0:GHEADS]
    rem = vec_ref[0, :, 2 * GHEADS : 3 * GHEADS]
    ent = vec_ref[0, :, 3 * GHEADS : 4 * GHEADS]
    rows_ref[...] = jnp.zeros_like(rows_ref)
    for pair in range(GHEADS // 2):
        lanes = slice(pair * 128, (pair + 1) * 128)
        x = x_ref[:, lanes]
        dy = dy_ref[:, lanes]
        dtx = spread(wide, dt, 2 * pair)
        remx = spread(wide, rem, 2 * pair)
        entx = spread(wide, ent, 2 * pair)
        dy_low = dy.astype(BF16)
        xd_ref[...] = (x * dtx).astype(BF16)
        st_low = st_ref[:, lanes].astype(BF16)
        dst_low = dst_ref[:, lanes].astype(BF16)
        carried = remx * dot_nn(b_low, dst_low)
        entered = entx * dot_nn(c_low, st_low)
        dc_ref[...] += dot_nt((entx * dy).astype(BF16), st_low)
        db_ref[...] += dot_nt((dtx * remx * x).astype(BF16), dst_low)
        for strip in range(length // STRIP):
            first = strip * STRIP
            xd = xd_ref[first : first + STRIP, :]
            dys = dy_low[first:]
            halves = []
            for half in range(2):
                head = 2 * pair + half
                mine = narrow if half == 0 else ~narrow
                gap = row_ref[head : head + 1, first:] - vec_ref[0, first : first + STRIP, GHEADS + head : GHEADS + head + 1]
                decay = jnp.exp2(jnp.minimum(gap, 0.0))
                bc = bc_ref[first : first + STRIP, first:]
                m = (decay * bc).astype(BF16)
                halves.append(dot_nn(m, dys))
                dg = decay * dot_nt(jnp.where(mine, xd, jnp.zeros_like(xd)), dys)
                dbc_ref[first : first + STRIP, first:] += dg
                e = dg * bc
                rows_ref[head : head + 1, first:] += jnp.sum(e, axis=0, keepdims=True)
                gone = jnp.sum(e, axis=1, keepdims=True)
                at = group * GHEADS + head
                cols_ref[3, first : first + STRIP, :] += jnp.where(lane == at, gone, 0.0)
            dxd = jnp.where(narrow, halves[0], halves[1]) + carried[first : first + STRIP]
            sum_ref[first : first + STRIP, :] = dxd
        dxd = sum_ref[...]
        dx_ref[:, lanes] = dtx * dxd + skip_ref[:, lanes] * dy
        pick = (place == group * GHEADS + 2 * pair + spot).astype(BF16)

        def per_head(value):
            high = value.astype(BF16)
            rest = (value - high.astype(F32)).astype(BF16)
            return dot_nn(high, pick) + dot_nn(rest, pick)

        cols_ref[0] += per_head(dxd * x)
        cols_ref[1] += per_head(dtx * x * carried)
        cols_ref[2] += per_head(dy * entered)

    @pl.when(group == GROUPS - 1)
    def _():
        s = lax.broadcasted_iota(jnp.int32, (length, length), 0)
        t = lax.broadcasted_iota(jnp.int32, (length, length), 1)
        seen = (t >= s) & (segc_ref[...] == segr_ref[...])
        dbc = jnp.where(seen, dbc_ref[...], 0.0).astype(BF16)
        db_ref[...] += dot_nn(dbc, c_low)
        dc_ref[...] += dot_tn(dbc, b_low)


def ssd_backward(x, dy, b, c, state, dstate, vec, row, seg_col, seg_row, skip):
    length = x.shape[0]
    x_spec, s_spec, n_spec, v_spec, r_spec = group_specs(length)
    return pl.pallas_call(
        ssd_backward_kernel,
        grid=(GROUPS,),
        in_specs=[
            x_spec, x_spec, n_spec, n_spec, s_spec, s_spec, v_spec, r_spec,
            pl.BlockSpec((length, 1), lambda g: (0, 0)),
            pl.BlockSpec((1, length), lambda g: (0, 0)),
            pl.BlockSpec((1, GLANES), lambda g: (0, g)),
        ],
        out_specs=[x_spec, n_spec, n_spec, pl.BlockSpec((4, length, 128), lambda g: (0, 0, 0)), r_spec],
        out_shape=[
            jax.ShapeDtypeStruct((length, INNER), F32),
            jax.ShapeDtypeStruct((length, STATE), F32),
            jax.ShapeDtypeStruct((length, STATE), F32),
            jax.ShapeDtypeStruct((4, length, 128), F32),
            jax.ShapeDtypeStruct((MHEADS, length), F32),
        ],
        scratch_shapes=[
            pltpu.VMEM((length, length), F32),
            pltpu.VMEM((length, length), F32),
            pltpu.VMEM((length, 128), BF16),
            pltpu.VMEM((length, 128), F32),
        ],
        compiler_params=PARAMS,
        name="ssd_backward",
    )(x, dy, b, c, state, dstate, vec, row, seg_col, seg_row, skip)


def turn(value, cosine, sine):
    low = (lax.broadcasted_iota(jnp.int32, value.shape, 1) % AHDIM) < AHDIM // 2
    other = jnp.where(low, pltpu.roll(value, 128 - AHDIM // 2, 1), pltpu.roll(value, AHDIM // 2, 1))
    return value * cosine + other * sine


def rope_kernel(qkv_ref, cos_ref, sin_ref, q_ref, kv_ref):
    cosine, sine = cos_ref[...], sin_ref[...]
    scale = AHDIM ** (-0.5)
    for at in range(QWIDTH // 128):
        lanes = slice(at * 128, (at + 1) * 128)
        q_ref[:, lanes] = (turn(qkv_ref[:, lanes], cosine, sine).astype(BF16).astype(F32) * scale).astype(BF16)
    kv_ref[:, :KWIDTH] = turn(qkv_ref[:, QWIDTH : QWIDTH + KWIDTH], cosine, sine).astype(BF16)
    kv_ref[:, KWIDTH:] = qkv_ref[:, QWIDTH + KWIDTH :].astype(BF16)


def rope(qkv, cosine, sine):
    length = qkv.shape[0]
    return pl.pallas_call(
        rope_kernel,
        out_shape=[
            jax.ShapeDtypeStruct((length, QWIDTH), BF16),
            jax.ShapeDtypeStruct((length, 2 * KWIDTH), BF16),
        ],
        compiler_params=PARAMS,
        name="rope",
    )(qkv, cosine, sine)


def unrope_kernel(dq_ref, dkv_ref, more_ref, cos_ref, sin_ref, out_ref):
    cosine, sine = cos_ref[...], -sin_ref[...]
    scale = AHDIM ** (-0.5)
    for at in range(QWIDTH // 128):
        lanes = slice(at * 128, (at + 1) * 128)
        out_ref[:, lanes] = (turn(dq_ref[:, lanes], cosine, sine) * scale).astype(BF16)
    dkv = dkv_ref[...] + more_ref[...].astype(F32)
    out_ref[:, QWIDTH : QWIDTH + KWIDTH] = turn(dkv[:, :KWIDTH], cosine, sine).astype(BF16)
    out_ref[:, QWIDTH + KWIDTH :] = dkv[:, KWIDTH:].astype(BF16)


def unrope(dq, dkv, more, cosine, sine):
    length = dq.shape[0]
    return pl.pallas_call(
        unrope_kernel,
        out_shape=jax.ShapeDtypeStruct((length, QWIDTH + 2 * KWIDTH), BF16),
        compiler_params=PARAMS,
        name="unrope",
    )(dq, dkv, more, cosine, sine)


def attend_kernel(rank_ref, q_ref, k_ref, v_ref, segq_ref, segk_ref, o_ref, lse_ref, top_ref, sum_ref, acc_ref, mask_ref):
    length = q_ref.shape[0]
    rank = rank_ref[0]
    top_ref[...] = jnp.full_like(top_ref, NEGATIVE)
    sum_ref[...] = jnp.zeros_like(sum_ref)
    acc_ref[...] = jnp.zeros_like(acc_ref)
    narrow = lane_is_low(STRIP)

    def block(step, carry):
        at = rank - step
        t = lax.broadcasted_iota(jnp.int32, (length, length), 0) + rank * length
        s = lax.broadcasted_iota(jnp.int32, (length, length), 1) + at * length
        seen = (s <= t) & (segq_ref[...] == segk_ref[pl.ds(at, 1), :])
        mask_ref[...] = jnp.where(seen, 0.0, NEGATIVE)
        start = pl.multiple_of(at * length, length)
        for head in range(AHEADS):
            kv_head = head // (AHEADS // KVHEADS)
            mine = narrow if head % 2 == 0 else ~narrow
            lanes = slice(head // 2 * 128, (head // 2 + 1) * 128)
            keys = k_ref[kv_head, pl.ds(start, length), :]
            values = v_ref[kv_head, pl.ds(start, length), :]
            for strip in range(length // STRIP):
                rows = slice(strip * STRIP, (strip + 1) * STRIP)
                q = q_ref[rows, lanes]
                scores = dot_nt(jnp.where(mine, q, jnp.zeros_like(q)), keys) + mask_ref[rows, :]
                old = top_ref[head, rows, :]
                new = jnp.maximum(old, jnp.max(scores, axis=1, keepdims=True))
                fade = jnp.exp(old - new)
                probs = jnp.exp(scores - new[:, :1])
                sum_ref[head, rows, :] = sum_ref[head, rows, :] * fade + jnp.sum(probs, axis=1, keepdims=True)
                top_ref[head, rows, :] = new
                acc = acc_ref[rows, lanes]
                acc_ref[rows, lanes] = jnp.where(mine, acc * fade + dot_nn(probs.astype(BF16), values), acc)
        return carry

    lax.fori_loop(0, rank + 1, block, 0)
    lane = lax.broadcasted_iota(jnp.int32, (length, 128), 1)
    stats = jnp.zeros((length, 128), F32)
    low = lane_is_low(length)
    for pair in range(AHEADS // 2):
        lanes = slice(pair * 128, (pair + 1) * 128)
        o_ref[:, lanes] = acc_ref[:, lanes] / jnp.where(low, sum_ref[2 * pair], sum_ref[2 * pair + 1])
    for head in range(AHEADS):
        stats = jnp.where(lane == head, top_ref[head] + jnp.log(sum_ref[head]), stats)
    lse_ref[...] = stats


def attend(rank, q, keys, values, seg_col, seg_blocks):
    length = q.shape[0]
    vmem = pl.BlockSpec(memory_space=pltpu.VMEM)
    return pl.pallas_call(
        attend_kernel,
        in_specs=[pl.BlockSpec(memory_space=pltpu.SMEM)] + [vmem] * 5,
        out_specs=[vmem, vmem],
        out_shape=[
            jax.ShapeDtypeStruct((length, QWIDTH), F32),
            jax.ShapeDtypeStruct((length, 128), F32),
        ],
        scratch_shapes=[
            pltpu.VMEM((AHEADS, length, 128), F32),
            pltpu.VMEM((AHEADS, length, 128), F32),
            pltpu.VMEM((length, QWIDTH), F32),
            pltpu.VMEM((length, length), F32),
        ],
        compiler_params=PARAMS,
        name="attend",
    )(rank, q, keys, values, seg_col, seg_blocks)


def attend_backward_kernel(
    rank_ref, q_ref, k_ref, v_ref, do_ref, lse_ref, delta_ref, segq_ref, segk_ref, dq_ref, dkv_ref
):
    length = q_ref.shape[0]
    total = k_ref.shape[1]
    rank = rank_ref[0]
    dq_ref[...] = jnp.zeros_like(dq_ref)
    dkv_ref[...] = jnp.zeros_like(dkv_ref)
    narrow = lane_is_low(STRIP)
    per = AHEADS // KVHEADS

    def strip_of(step, carry):
        start = pl.multiple_of(step * STRIP, STRIP)
        s = lax.broadcasted_iota(jnp.int32, (STRIP, length), 0) + start
        t = lax.broadcasted_iota(jnp.int32, (STRIP, length), 1) + rank * length
        seen = (s <= t) & (segk_ref[pl.ds(start, STRIP), :] == segq_ref[...])
        mask = jnp.where(seen, 0.0, NEGATIVE)
        sums = []
        for kv_head in range(KVHEADS):
            keys = k_ref[kv_head, pl.ds(start, STRIP), :]
            values = v_ref[kv_head, pl.ds(start, STRIP), :]
            dk = jnp.zeros((STRIP, 128), F32)
            dv = jnp.zeros((STRIP, 128), F32)
            for head in range(kv_head * per, (kv_head + 1) * per):
                mine = narrow if head % 2 == 0 else ~narrow
                lanes = slice(head // 2 * 128, (head // 2 + 1) * 128)
                q = q_ref[:, lanes]
                do = do_ref[:, lanes]
                own_keys = jnp.where(mine, keys, jnp.zeros_like(keys))
                own_values = jnp.where(mine, values, jnp.zeros_like(values))
                probs = jnp.exp(dot_nt(own_keys, q) + mask - lse_ref[head : head + 1, :])
                dp = dot_nt(own_values, do)
                ds = (probs * (dp - delta_ref[head : head + 1, :])).astype(BF16)
                dv += jnp.where(mine, dot_nn(probs.astype(BF16), do), 0.0)
                dk += jnp.where(mine, dot_nn(ds, q), 0.0)
                dq_ref[:, lanes] += dot_tn(ds, own_keys)
            sums.append((dk + pltpu.roll(dk, AHDIM, 1), dv + pltpu.roll(dv, AHDIM, 1)))
        dkv_ref[pl.ds(start, STRIP), :KWIDTH] = jnp.where(narrow, sums[0][0], sums[1][0])
        dkv_ref[pl.ds(start, STRIP), KWIDTH:] = jnp.where(narrow, sums[0][1], sums[1][1])
        return carry

    lax.fori_loop(0, (rank + 1) * (length // STRIP), strip_of, 0)


def attend_backward(rank, q, keys, values, do, lse, delta, seg_row, seg_keys):
    length, total = q.shape[0], keys.shape[1]
    vmem = pl.BlockSpec(memory_space=pltpu.VMEM)
    return pl.pallas_call(
        attend_backward_kernel,
        in_specs=[pl.BlockSpec(memory_space=pltpu.SMEM)] + [vmem] * 8,
        out_specs=[vmem, vmem],
        out_shape=[
            jax.ShapeDtypeStruct((length, QWIDTH), F32),
            jax.ShapeDtypeStruct((total, 2 * KWIDTH), F32),
        ],
        compiler_params=PARAMS,
        name="attend_backward",
    )(rank, q, keys, values, do, lse, delta, seg_row, seg_keys)


def gather_keyvals(own):
    count = lax.axis_size("seq")
    if count == 2:
        got = lax.ppermute(own, "seq", [(0, 1)])
        first = lax.axis_index("seq") == 0
        return jnp.concatenate([jnp.where(first, own, got), own])
    return lax.all_gather(own, "seq", axis=0, tiled=True)


def scatter_keyval_grads(grads, length):
    count = lax.axis_size("seq")
    place = lax.axis_index("seq")
    if count == 2:
        own = lax.dynamic_slice_in_dim(grads, place * length, length)
        return own, lax.ppermute(grads[:length].astype(BF16), "seq", [(1, 0)])
    total = lax.psum_scatter(grads.astype(BF16), "seq", scatter_dimension=0, tiled=True)
    return jnp.zeros((length, grads.shape[1]), F32), total


def fit(value, rows):
    flat = value.reshape(-1)
    columns = -(-flat.shape[0] // rows)
    return jnp.pad(flat, (0, rows * columns - flat.shape[0])).reshape(rows, columns)


def on_device(
    tokens,
    segment_ids,
    norm1_gain,
    w_mamba_in,
    w_delta,
    conv_weight,
    conv_bias,
    delta_bias,
    decay_log,
    skip_gain,
    w_mamba_out,
    w_qkv,
    w_attn_out,
    norm2_gain,
    w_gate_up,
    w_down,
    cotangent,
):
    order_x, order_y, order_z = bit_orders()
    count = lax.axis_size("dp") * lax.axis_size("seq")
    rows = w_qkv.shape[0]
    width = rows * count
    taps_count, channels = conv_weight.shape
    conv_cols = -(-taps_count * channels // rows)
    bias_cols = -(-channels // rows)
    small = jnp.concatenate(
        [w_delta, norm1_gain[:, None], norm2_gain[:, None], fit(conv_weight, rows), fit(conv_bias, rows)], axis=1
    )
    small_width = 128 * (-(-small.shape[1] // 128))
    small = jnp.pad(small, ((0, 0), (0, small_width - small.shape[1])))

    gate_up = lax.all_gather(w_gate_up, ("dp", "seq"), axis=0, tiled=True)
    down = lax.all_gather(w_down, ("dp", "seq"), axis=0, tiled=True)
    w_q = double(jnp.concatenate([w_qkv, small], axis=1), order_z)
    w_x = double(w_mamba_in[:, INNER:], order_x)
    w_z = double(w_mamba_in[:, :INNER], order_y)
    w_mo = double(w_mamba_out, order_x)
    w_ao = double(w_attn_out, order_y)

    smalls = w_q[:, QWIDTH + 2 * KWIDTH :]
    gain_one = smalls[:, MHEADS].astype(F32)
    gain_two = smalls[:, MHEADS + 1].astype(F32)
    at = MHEADS + 2
    conv_kernel = smalls[:, at : at + conv_cols].reshape(count, rows * conv_cols)[:, : taps_count * channels]
    conv_kernel = conv_kernel.reshape(count, taps_count, channels).transpose(1, 0, 2)
    conv_kernel = conv_kernel.reshape(taps_count, count * channels).astype(F32)
    at += conv_cols
    conv_shift = smalls[:, at : at + bias_cols].reshape(count, rows * bias_cols)[:, :channels]
    conv_shift = conv_shift.reshape(count * channels).astype(F32)

    length = tokens.shape[1]
    seg_full = segment_ids[0]
    total = seg_full.shape[0]
    rank = lax.axis_index("seq")
    first_row = rank * length
    back = taps_count - 1
    seg_padded = jnp.concatenate([jnp.full((back,), -1, jnp.int32), seg_full])
    seg_own = lax.dynamic_slice_in_dim(seg_full, first_row, length)
    seg_before = lax.dynamic_slice_in_dim(seg_padded, first_row + back - 1, 1)[0]
    taps = [
        (lax.dynamic_slice_in_dim(seg_padded, first_row + back - j, length) == seg_own).astype(F32)[:, None]
        for j in range(taps_count)
    ]
    seg_col = seg_own[:, None]
    seg_row = seg_own[None, :]
    rank_arg = rank.astype(jnp.int32).reshape(1)

    inputs = tokens[0].astype(F32)
    r1 = lax.rsqrt(jnp.mean(inputs * inputs, axis=-1, keepdims=True) + EPSILON)
    n1 = (inputs * r1 * gain_one[None, :]).astype(BF16)
    qkv_small = dot_nn(n1, w_q)
    qkv = qkv_small[:, : QWIDTH + 2 * KWIDTH]
    delta_raw = qkv_small[:, QWIDTH + 2 * KWIDTH : QWIDTH + 2 * KWIDTH + MHEADS]
    xbc = dot_nn(n1, w_x).astype(BF16)
    z = dot_nn(n1, w_z).astype(BF16)

    freqs = ROPE_BASE ** (-(jnp.arange(AHDIM // 2).astype(F32) * 2.0 / AHDIM))
    angles = (first_row + jnp.arange(length, dtype=jnp.int32)).astype(F32)[:, None] * freqs[None, :]
    cosine = jnp.tile(jnp.cos(angles), (1, 4))
    sine_half = jnp.sin(angles)
    sine = jnp.tile(jnp.concatenate([-sine_half, sine_half], axis=1), (1, 2))
    q, keyvals = rope(qkv, cosine, sine)
    all_keyvals = gather_keyvals(keyvals)

    def doubled(start):
        return jnp.stack(
            [
                jnp.tile(all_keyvals[:, start + i * AHDIM : start + (i + 1) * AHDIM], (1, 2))
                for i in range(KVHEADS)
            ]
        )

    keys, values = doubled(0), doubled(KWIDTH)

    halo = neighbour(xbc[length - back :], 1)
    extended = jnp.concatenate([halo, xbc]).astype(F32)
    xc = conv_shift[None, :]
    for j in range(taps_count):
        xc = xc + conv_kernel[j][None, :] * extended[back - j : back - j + length] * taps[j]
    u = jax.nn.silu(xc)
    x_in, b_in, c_in = u[:, :INNER], u[:, INNER : INNER + STATE], u[:, INNER + STATE :]

    delta_shift = delta_bias.astype(F32)
    rate = jnp.exp(decay_log.astype(F32))
    dt = jax.nn.softplus(delta_raw + delta_shift[None, :])
    log_decay = -dt * rate[None, :]
    places = jnp.arange(length, dtype=jnp.int32)
    lower = (places[:, None] >= places[None, :]).astype(F32)
    cumulative = jnp.dot(lower, log_decay, precision=lax.Precision.HIGHEST)
    final = cumulative[-1]
    carry_gate = jnp.where(seg_own[-1] == seg_before, jnp.exp(final), 0.0)
    rem = jnp.where(seg_col == seg_own[-1], jnp.exp(final[None, :] - cumulative), 0.0)
    ent = jnp.where(seg_col == seg_before, jnp.exp(cumulative), 0.0)
    vec = jnp.stack([dt, cumulative * LOG2E, rem, ent], axis=1)
    vec = vec.reshape(length, 4, GROUPS, GHEADS).transpose(2, 0, 1, 3).reshape(GROUPS, length, 4 * GHEADS)
    row = (cumulative * LOG2E).T
    gate_lanes = jnp.repeat(carry_gate, MHDIM)
    skip_lanes = jnp.repeat(skip_gain.astype(F32), MHDIM)[None, :]

    y_local, state_part = ssd_forward(x_in, b_in, c_in, vec, row, seg_col, seg_row)
    state_in = state_from_behind(gate_lanes, state_part)

    attended, lse = attend(rank_arg, q, keys, values, seg_col, seg_full.reshape(total // length, length))
    attended_low = attended.astype(BF16)

    y, mixed_low = ssd_finish(y_local, x_in, z, c_in, state_in, vec, skip_lanes)
    residual = inputs + dot_nn(mixed_low, w_mo) + dot_nn(attended_low, w_ao)

    r2 = lax.rsqrt(jnp.mean(residual * residual, axis=-1, keepdims=True) + EPSILON)
    n2 = (residual * r2 * gain_two[None, :]).astype(BF16)
    gu = dot_nn(n2, gate_up)
    half = gu.shape[1] // 2
    gate, up = gu[:, :half], gu[:, half:]
    gate_act, gate_slope = silu_parts(gate)
    hidden = (gate_act * up).astype(BF16)
    block_out = (residual + dot_nn(hidden, down)).astype(BF16)

    upstream_low = cotangent[0]
    upstream = upstream_low.astype(F32)
    grad_down = halve(dot_tn(hidden, upstream_low).astype(BF16), order_x)
    dhidden = dot_nt(upstream_low, down)
    dgate = (dhidden * up * gate_slope).astype(BF16)
    dup = (dhidden * gate_act).astype(BF16)
    grad_gate = halve(dot_tn(n2, dgate).astype(BF16), order_y)
    grad_up = halve(dot_tn(n2, dup).astype(BF16), order_z)
    dn2 = dot_nt(dgate, gate_up[:, :half]) + dot_nt(dup, gate_up[:, half:])
    scaled = gain_two[None, :] * dn2
    grad_gain_two = jnp.sum(dn2 * residual * r2, axis=0)
    dhs = upstream + r2 * scaled - residual * (r2 * r2 * r2) * jnp.mean(scaled * residual, axis=-1, keepdims=True)
    dhs_low = dhs.astype(BF16)
    grad_mo = halve(dot_tn(mixed_low, dhs_low).astype(BF16), order_x)
    grad_ao = halve(dot_tn(attended_low, dhs_low).astype(BF16), order_y)
    dym = dot_nt(dhs_low, w_mo)
    do = dot_nt(dhs_low, w_ao).astype(BF16)

    dy, dz, dstate_part, skip_cols = ssd_gate(dym, y, x_in, z, c_in, vec)
    dstate = state_from_ahead(gate_lanes, dstate_part)
    grad_z = halve(dot_tn(n1, dz).astype(BF16), order_y)

    heads = (jnp.arange(QWIDTH)[None, :] // AHDIM == jnp.arange(AHEADS)[:, None]).astype(F32)
    delta = lax.dot_general(
        heads, do.astype(F32) * attended, (((1,), (1,)), ((), ())), precision=lax.Precision.HIGHEST
    )
    dq, dkv = attend_backward(
        rank_arg, q, keys, values, do, lse[:, :AHEADS].T, delta, seg_row, seg_full[:, None]
    )
    own_dkv, more_dkv = scatter_keyval_grads(dkv, length)
    dqkv = unrope(dq, own_dkv, more_dkv, cosine, sine)

    dx, db, dc, cols, rows_sum = ssd_backward(
        x_in, dy, b_in, c_in, state_in, dstate, vec, row, seg_row.T, seg_row, skip_lanes
    )
    direct, leaving, entering, gone = (cols[i, :, :MHEADS] for i in range(4))
    passed = jnp.sum((dstate * state_in).reshape(STATE, MHEADS, MHDIM), axis=(0, 2)) * carry_gate
    change = rows_sum.T - gone + entering - leaving
    upper = (places[:, None] <= places[None, :]).astype(F32)
    da = jnp.dot(upper, change, precision=lax.Precision.HIGHEST)
    da = da + (jnp.sum(leaving, axis=0) + passed)[None, :]
    ddt = direct - da * rate[None, :]
    ddelta = ddt * jax.nn.sigmoid(delta_raw + delta_shift[None, :])
    grad_decay = jnp.sum(da * log_decay, axis=0)
    grad_shift = jnp.sum(ddelta, axis=0)
    grad_skip = jnp.sum(skip_cols.reshape(MHEADS, MHDIM), axis=1)

    _, slope = silu_parts(xc)
    dxc = jnp.concatenate([dx, db, dc], axis=1) * slope
    grad_bias = jnp.sum(dxc, axis=0)
    kernel_rows = []
    spilled = jnp.zeros((length + back, dxc.shape[1]), F32)
    for j in range(taps_count):
        masked = dxc * taps[j]
        kernel_rows.append(jnp.sum(masked * extended[back - j : back - j + length], axis=0))
        spilled = spilled + jnp.pad(masked * conv_kernel[j][None, :], ((back - j, j), (0, 0)))
    incoming = neighbour(spilled[:back], -1)
    dxbc = spilled[back:]
    dxbc = jnp.concatenate([dxbc[: length - back], dxbc[length - back :] + incoming]).astype(BF16)

    kernel_grad = jnp.stack(kernel_rows).reshape(taps_count, count, channels).transpose(1, 0, 2)
    kernel_grad = kernel_grad.reshape(count, taps_count * channels)
    shift_grad = grad_bias.reshape(count, channels)
    head_grads = total_everywhere(jnp.concatenate([grad_shift, grad_decay, grad_skip]))

    def fit_all(value, columns):
        spare = rows * columns - value.shape[1]
        return jnp.pad(value, ((0, 0), (0, spare))).reshape(width, columns)

    ddelta_wide = jnp.pad(ddelta.astype(BF16), ((0, 0), (0, small_width - MHEADS)))
    dq_small = jnp.concatenate([dqkv, ddelta_wide], axis=1)
    dn1 = dot_nt(dq_small, w_q) + dot_nt(dz, w_z) + dot_nt(dxbc, w_x)
    scaled = gain_one[None, :] * dn1
    grad_gain_one = jnp.sum(dn1 * inputs * r1, axis=0)
    grad_tokens = dhs + r1 * scaled - inputs * (r1 * r1 * r1) * jnp.mean(scaled * inputs, axis=-1, keepdims=True)

    grad_qkv = halve(dot_tn(n1, dqkv).astype(BF16), order_z)
    parts = [
        dot_tn(n1, ddelta.astype(BF16)),
        grad_gain_one[:, None],
        grad_gain_two[:, None],
        fit_all(kernel_grad, conv_cols),
        fit_all(shift_grad, bias_cols),
    ]
    used = sum(p.shape[1] for p in parts)
    parts.append(jnp.zeros((width, small_width - used), F32))
    grad_small = halve(jnp.concatenate(parts, axis=1).astype(BF16), order_x)
    cut = 640
    grad_x = jnp.concatenate(
        [
            halve(dot_tn(n1, dxbc[:, :cut]).astype(BF16), order_x),
            halve(dot_tn(n1, dxbc[:, cut : 2 * cut]).astype(BF16), order_y),
            halve(dot_tn(n1, dxbc[:, 2 * cut :]).astype(BF16), order_z),
        ],
        axis=1,
    )

    at = MHEADS + 2
    kernel_own = grad_small[:, at : at + conv_cols].reshape(-1)[: taps_count * channels].reshape(taps_count, channels)
    at += conv_cols
    shift_own = grad_small[:, at : at + bias_cols].reshape(-1)[:channels]
    return (
        block_out[None],
        grad_tokens[None],
        grad_small[:, MHEADS],
        jnp.concatenate([grad_z, grad_x], axis=1),
        grad_small[:, :MHEADS],
        kernel_own,
        shift_own,
        head_grads[:MHEADS],
        head_grads[MHEADS : 2 * MHEADS],
        head_grads[2 * MHEADS :],
        grad_mo,
        grad_qkv,
        grad_ao,
        grad_small[:, MHEADS + 1],
        jnp.concatenate([grad_gate, grad_up], axis=1),
        grad_down,
    )


def solution(mesh):
    both = ("dp", "seq")
    in_specs = (
        P("dp", "seq", None),
        P("dp", None),
        P(both),
        P(both, None),
        P(both, None),
        P(None, both),
        P(both),
        P(),
        P(),
        P(),
        P(both, None),
        P(both, None),
        P(both, None),
        P(both),
        P(both, None),
        P(both, None),
        P("dp", "seq", None),
    )
    out_specs = (
        P("dp", "seq", None),
        P("dp", "seq", None),
        P(both),
        P(both, None),
        P(both, None),
        P(None, both),
        P(both),
        P(),
        P(),
        P(),
        P(both, None),
        P(both, None),
        P(both, None),
        P(both),
        P(both, None),
        P(both, None),
    )
    return jax.shard_map(
        on_device, mesh=mesh, in_specs=in_specs, out_specs=out_specs, check_vma=False
    )
```

time: 1950 us -> 718 us (0.37)
  waiting for transfers between devices: 1230 us -> 249 us
  blocking collectives: 249 us -> 0 us
  matrix products: 303 us -> 88.6 us
  starting transfers between devices: 5.96 us -> 106 us
  Pallas kernels: 0 us -> 74.3 us
  local copies, waits for them, and re-layouts: 52.1 us -> 97.7 us
    reduce_scatter x7 -> x0, waiting for transfers between devices: 1140 us -> none  [the longest x1 362 us: on_device(): lax.psum_scatter(grad_gate_up, ('dp', 'seq'), scatter_dimension=0, tiled=...]
    ppermute x2 -> x91, waiting for transfers between devices: 2.89 us -> 248 us  [the longest x85 236 us: swap(): return lax.ppermute(value, axis, [(i, i ^ level) for i in range(size)])]
    dot_general x46 -> x29, matrix products: 300 us -> 88.6 us  [the longest x11 30.3 us: dot_tn(): lax.dot_general(a, b, (((0,), (0,)), ((), ())), preferred_element_type=F32)]
    all_gather x6 -> x0, blocking collectives: 169 us -> none  [the longest x1 66.5 us: on_device(): lax.all_gather(conv_weight, ('dp', 'seq'), axis=1, tiled=True)]
    ppermute x2 -> x91, starting transfers between devices: 5.41 us -> 106 us  [the longest x85 79.3 us: swap(): return lax.ppermute(value, axis, [(i, i ^ level) for i in range(size)])]
    unnamed x2 -> x0, blocking collectives: 80.3 us -> none
    pallas_call x0 -> x8, Pallas kernels: none -> 74.3 us  [the longest x1 27.4 us: ssd_backward(): pl.pallas_call(ssd_backward_kernel, grid=(GROUPS,), in_specs=[x_spec, x_s...]
    unnamed x15 -> x2, waiting for transfers between devices: 45.6 us -> 0.7 us
  transfers between devices with their start and end apart: 16 -> 93, of which waited for: 9 -> 48; matrix products, arithmetic and copies ran while one was open for 14% -> 28% of each run, Pallas kernels for 0% -> 9%
where the time goes in v1:
time: 718 us; the launch traced here: 708 us
  waiting for transfers between devices  249 us (35%)
  starting transfers between devices  106 us (15%)
  local copies, waits for them, and re-layouts  97.7 us (14%)
  matrix products  88.6 us (12%)
  other arithmetic  74.5 us (10%)
  Pallas kernels  74.3 us (10%)
  between operations  18.5 us (3%)
    ppermute x85, waiting for transfers between devices, swap(): return lax.ppermute(value, axis, [(i, i ^ level) for i in range(size)])  236 us
    ppermute x85, starting transfers between devices, swap(): return lax.ppermute(value, axis, [(i, i ^ level) for i in range(size)])  79.3 us
    dot_general x11, matrix products, dot_tn(): lax.dot_general(a, b, (((0,), (0,)), ((), ())), preferred_element_type=F32)  30.3 us
    dot_general x8, matrix products, dot_nt(): lax.dot_general(a, b, (((1,), (1,)), ((), ())), preferred_element_type=F32)  27.8 us
    dot_general x7, matrix products, dot_nn(): lax.dot_general(a, b, (((1,), (0,)), ((), ())), preferred_element_type=F32)  27.7 us
    pallas_call x1, Pallas kernels, ssd_backward(): pl.pallas_call(ssd_backward_kernel, grid=(GROUPS,), in_specs=[x_spec, x_s...  27.4 us
    unnamed x267, local copies, waits for them, and re-layouts  21.9 us
    dynamic_slice x10, local copies, waits for them, and re-layouts, halve(): kept = lax.dynamic_index_in_dim(value, here, place, keepdims=False)  17.7 us
  transfers between devices with their start and end apart: 93, of which 48 were waited for; matrix products, arithmetic and copies ran while one was open for 28% of the time, Pallas kernels for 9%

profile of v1, /device:TPU:0, one launch (start us, length us, event | category | flops | bytes accessed | tf_op | source)
XLA Modules:
  0.0 708.1 jit_solution(9214755290110585469)
XLA Ops:
  53.7 6.5 collective-permute-done.12
  61.3 8.4 %collective-permute-done.18 = bf16[2,48,1024]{2,1,0:T(8,128)(2,1)S(1)} collective-permute-done((bf16[2,48,1024]{2,1,0:T(8,128)(2,1)S(1)}, bf16[2,48,1024]{2,1,0:T(8,128)(2,1)S(1)}, u32[]{:S(2)}, u32[]{:S(2)}) %collective-permute-start.18) | collective-permute-done | bytes 196640 | tf_op jit(solution)/shard_map/ppermute | solution.py:74
  78.9 15.6 %collective-permute-done.13 = bf16[2,2,32,1536]{3,2,1,0:T(8,128)(2,1)S(1)} collective-permute-done((bf16[2,2,32,1536]{3,2,1,0:T(8,128)(2,1)S(1)}, bf16[2,2,32,1536]{3,2,1,0:T(8,128)(2,1)S(1)}, u32[]{:S(2)}, u32[]{:S(2)}) %collective-permute-start.13) | collective-permute-done | bytes 393248 | tf_op jit(solution)/shard_map/ppermute | solution.py:74
  108.4 10.9 %collective-permute-done.14 = bf16[2,2,2,32,1536]{4,3,2,1,0:T(8,128)(2,1)S(1)} collective-permute-done((bf16[2,2,2,32,1536]{4,3,2,1,0:T(8,128)(2,1)S(1)}, bf16[2,2,2,32,1536]{4,3,2,1,0:T(8,128)(2,1)S(1)}, u32[]{:S(2)}, u32[]{:S(2)}) %collective-permute-start.14) | collective-permute-done | bytes 786464 | tf_op jit(solution)/shard_map/ppermute | solution.py:74
  123.0 7.5 %collective-permute-done.8 = bf16[2,2,2,32,1792]{4,3,2,1,0:T(8,128)(2,1)S(1)} collective-permute-done((bf16[2,2,2,32,1792]{4,3,2,1,0:T(8,128)(2,1)S(1)}, bf16[2,2,2,32,1792]{4,3,2,1,0:T(8,128)(2,1)S(1)}, u32[]{:S(2)}, u32[]{:S(2)}) %collective-permute-start.8) | collective-permute-done | bytes 917536 | tf_op jit(solution)/shard_map/ppermute | solution.py:74
  156.0 12.0 %attend.1 = (f32[512,512]{1,0:T(8,128)S(1)}, f32[512,128]{1,0:T(8,128)S(1)}) custom-call(s32[1]{0:T(128)} %bitcast.75.rank_ref, bf16[512,512]{1,0:T(8,128)(2,1)S(1)} %get-tuple-element.38.q_ref, bf16[2,1024,128]{2,1,0:T(8,128)(2,1)S(1)} %get-tuple-element.254.k_ref, bf16[2,1024,128]{2,1,0:T(8,128)(2,1)S(1)} %get-tuple-element.255.v_ref, ...), custom_call_target="tpu_custom_call" | custom-call | tf_op jit(solution)/shard_map/attend/pallas_call | solution.py:543
  183.0 15.2 %collective-permute-start.10 = (bf16[3,1792]{1,0:T(4,128)(2,1)S(1)}, bf16[3,1792]{1,0:T(4,128)(2,1)S(1)}, u32[]{:S(2)}, u32[]{:S(2)}) collective-permute-start(bf16[3,1792]{1,0:T(4,128)(2,1)S(1)} %slice.239), channel_id=1, source_target_pairs={{0,1},{2,3},{4,5},{6,7},{8,9},{10,11},{12,13},{14,15},{16,17},{18,... | collective-permute-start | bytes 32264 | tf_op jit(solution)/shard_map/ppermute | solution.py:172
  208.4 8.7 %ssd_forward.1 = (f32[512,1536]{1,0:T(8,128)S(1)}, f32[128,1536]{1,0:T(8,128)S(1)}) custom-call(f32[512,1536]{1,0:T(8,128)} %slice.247.x_ref, f32[512,128]{1,0:T(8,128)S(1)} %get-tuple-element.156.b_ref, f32[512,128]{1,0:T(8,128)S(1)} %get-tuple-element.155.c_ref, f32[3,512,32]{2,1,0:T(8,128)S(1)} %copy.496.vec_ref, ...), custom_call_target="tpu_custom_call" | custom-call | tf_op jit(solution)/shard_map/ssd_forward/pallas_call | solution.py:231
  228.6 6.6 ssd_finish.1
  242.0 11.5 %fusion.155 = f32[512,4096]{1,0:T(8,128)} fusion(bf16[512,1024]{1,0:T(8,128)(2,1)} %multiply_convert_fusion.3, bf16[1024,4096]{1,0:T(8,128)(2,1)} %all-gather.3.cloned.1.call-done), kind=kOutput, calls=%fused_computation.480 | convolution fusion | flops 4294967296 | bytes 17825792 | tf_op jit(solution)/shard_map/dot_general | solution.py:37
  253.5 10.1 %multiply_convert_fusion.1 = (bf16[512,2048]{1,0:T(8,128)(2,1)S(1)}, bf16[512,2048]{1,0:T(8,128)(2,1)S(1)}, bf16[512,2048]{1,0:T(8,128)(2,1)}) fusion(f32[512,4096]{1,0:T(8,128)} %fusion.155, bf16[2048,1024]{1,0:T(8,128)(2,1)} %all-gather.5.cloned.1.call-done, bf16[1,512,1024]{2,1,0:T(8,128)(2,1)} %param.33), kind=kOutput, calls=%fused_computation.11 | convolution fusion | flops 2163212288 | bytes 19922944 | tf_op jit(solution)/shard_map/dot_general | solution.py:41
  277.5 7.4 %ssd_gate.1 = (f32[512,1536]{1,0:T(8,128)}, bf16[512,1536]{1,0:T(8,128)(2,1)S(1)}, f32[128,1536]{1,0:T(8,128)S(1)}, f32[1,1536]{1,0:T(1,128)S(1)}) custom-call(f32[512,1536]{1,0:T(8,128)} %fusion.156.dym_ref, f32[512,1536]{1,0:T(8,128)} %get-tuple-element.44.y_ref, f32[512,1536]{1,0:T(8,128)} %slice.247.x_ref, bf16[512,1536]{1,0:T(8,128)(2,1)S(1)} %copy-done.1, ...), custom_call_target="tpu_custom_call" | custom-call | tf_op jit(solution)/shard_map/ssd_gate/pallas_call | solution.py:306
  309.1 10.7 %attend_backward.1 = (f32[512,512]{1,0:T(8,128)S(1)}, f32[1024,256]{1,0:T(8,128)}) custom-call(s32[1]{0:T(128)} %bitcast.75.rank_ref, bf16[512,512]{1,0:T(8,128)(2,1)S(1)} %copy-done.15, bf16[2,1024,128]{2,1,0:T(8,128)(2,1)S(1)} %get-tuple-element.254.k_ref, bf16[2,1024,128]{2,1,0:T(8,128)(2,1)S(1)} %copy-done.3, ...), custom_call_target="tpu_custom_call" | custom-call | tf_op jit(solution)/shard_map/attend_backward/pallas_call | solution.py:609
  362.4 27.4 %ssd_backward.1 = (f32[512,1536]{1,0:T(8,128)}, f32[512,128]{1,0:T(8,128)S(1)}, f32[512,128]{1,0:T(8,128)S(1)}, f32[4,512,128]{2,1,0:T(8,128)S(1)}, f32[24,512]{1,0:T(8,128)S(1)}) custom-call(f32[512,1536]{1,0:T(8,128)} %slice.247.x_ref, f32[512,1536]{1,0:T(8,128)} %get-tuple-element.45.dy_ref, f32[512,128]{1,0:T(8,128)S(1)} %copy-done.8, ...), custom_call_target="tpu_custom_call" | custom-call | tf_op jit(solution)/shard_map/ssd_backward/pallas_call | solution.py:415
  421.2 12.9 %collective-permute-start.60 = (f32[72]{0:T(128)S(1)}, f32[72]{0:T(128)S(1)}, u32[]{:S(2)}, u32[]{:S(2)}) collective-permute-start(f32[72]{0:T(128)S(1)} %add.743), channel_id=1, source_target_pairs={{0,1},{1,0},{2,3},{3,2},{4,5},{5,4},{6,7},{7,6},{8,9},{9,8},{10,11... | collective-permute-start | bytes 872 | tf_op jit(solution)/shard_map/ppermute | solution.py:74
  516.2 7.5 %collective-permute-done.52 = bf16[2,2,2,32,512]{4,3,1,2,0:T(8,128)(2,1)S(1)} collective-permute-done((bf16[2,2,2,32,512]{4,3,1,2,0:T(8,128)(2,1)S(1)}, bf16[2,2,2,32,512]{4,3,1,2,0:T(8,128)(2,1)S(1)}, u32[]{:S(2)}, u32[]{:S(2)}) %collective-permute-start.52) | collective-permute-done | bytes 262176 | tf_op jit(solution)/shard_map/ppermute | solution.py:74
  526.4 6.9 collective-permute-done.53
  538.1 7.5 %collective-permute-done.42 = bf16[2,2,2,32,640]{4,3,0,1,2:T(8,128)(2,1)S(1)} collective-permute-done((bf16[2,2,2,32,640]{4,3,0,1,2:T(8,128)(2,1)S(1)}, bf16[2,2,2,32,640]{4,3,0,1,2:T(8,128)(2,1)S(1)}, u32[]{:S(2)}, u32[]{:S(2)}) %collective-permute-start.42) | collective-permute-done | bytes 327712 | tf_op jit(solution)/shard_map/ppermute | solution.py:74
  549.8 6.4 collective-permute-done.48
  569.5 6.9 collective-permute-done.68
  608.5 10.7 %collective-permute-done.62 = bf16[2,2,2,48,1024]{4,3,0,1,2:T(8,128)(2,1)S(1)} collective-permute-done((bf16[2,2,2,48,1024]{4,3,0,1,2:T(8,128)(2,1)S(1)}, bf16[2,2,2,48,1024]{4,3,0,1,2:T(8,128)(2,1)S(1)}, u32[]{:S(2)}, u32[]{:S(2)}) %collective-permute-start.62) | collective-permute-done | bytes 786464 | tf_op jit(solution)/shard_map/ppermute | solution.py:74
  620.1 13.1 %collective-permute-done.38 = bf16[2,2,32,1536]{3,2,1,0:T(8,128)(2,1)S(1)} collective-permute-done((bf16[2,2,32,1536]{3,2,1,0:T(8,128)(2,1)S(1)}, bf16[2,2,32,1536]{3,2,1,0:T(8,128)(2,1)S(1)}, u32[]{:S(2)}, u32[]{:S(2)}) %collective-permute-start.38) | collective-permute-done | bytes 393248 | tf_op jit(solution)/shard_map/ppermute | solution.py:74
  636.8 6.6 collective-permute-done.39
  656.6 19.0 %collective-permute-done.83 = bf16[2,2,32,2048]{3,2,0,1:T(8,128)(2,1)S(1)} collective-permute-done((bf16[2,2,32,2048]{3,2,0,1:T(8,128)(2,1)S(1)}, bf16[2,2,32,2048]{3,2,0,1:T(8,128)(2,1)S(1)}, u32[]{:S(2)}, u32[]{:S(2)}) %collective-permute-start.83) | collective-permute-done | bytes 524320 | tf_op jit(solution)/shard_map/ppermute | solution.py:74
  (776 shorter events, 433.6 us)
Async XLA Ops:
  7.2 234.8 %all-gather.3.cloned.1.call-start = ((), (), s32[]{:S(2)}) async-start(), calls=%async_computation | async-start | bytes 8650752 | tf_op jit(solution)/shard_map/all_gather | solution.py:679
  7.9 245.5 %all-gather.5.cloned.1.call-start = ((), (), s32[]{:S(2)}) async-start(), calls=%async_computation.1 | async-start | bytes 4325376 | tf_op jit(solution)/shard_map/all_gather | solution.py:680
  45.0 29.6 %collective-permute-start.6 = (bf16[2,32,1792]{2,1,0:T(8,128)(2,1)S(1)}, bf16[2,32,1792]{2,1,0:T(8,128)(2,1)S(1)}, u32[]{:S(2)}, u32[]{:S(2)}) collective-permute-start(bf16[2,32,1792]{2,1,0:T(8,128)(2,1)S(1)} %pad_maximum_fusion.28), channel_id=1, source_target_pairs={{0,8},{2,10},{4,12},{6,14},{8,0},{10,2},{12,4},{14,6},{16,24},{18,... | collective-permute-start | bytes 688136 | tf_op jit(solution)/shard_map/ppermute | solution.py:74
  47.2 28.0 %collective-permute-start.2 = (bf16[2,2,32,896]{3,2,1,0:T(8,128)(2,1)S(1)}, bf16[2,2,32,896]{3,2,1,0:T(8,128)(2,1)S(1)}, u32[]{:S(2)}, u32[]{:S(2)}) collective-permute-start(bf16[2,2,32,896]{3,2,1,0:T(8,128)(2,1)S(1)} %pad_maximum_fusion.27), channel_id=1, source_target_pairs={{0,16},{2,18},{4,20},{6,22},{8,24},{10,26},{12,28},{14,30},{16,0},... | collective-permute-start | bytes 688136 | tf_op jit(solution)/shard_map/ppermute | solution.py:74
  60.3 34.2 %collective-permute-start.13 = (bf16[2,2,32,1536]{3,2,1,0:T(8,128)(2,1)S(1)}, bf16[2,2,32,1536]{3,2,1,0:T(8,128)(2,1)S(1)}, u32[]{:S(2)}, u32[]{:S(2)}) collective-permute-start(bf16[2,2,32,1536]{3,2,1,0:T(8,128)(2,1)S(1)} %pad_maximum_fusion.23), channel_id=1, source_target_pairs={{0,8},{2,10},{4,12},{6,14},{8,0},{10,2},{12,4},{14,6},{16,24},{18,... | collective-permute-start | bytes 1179656 | tf_op jit(solution)/shard_map/ppermute | solution.py:74
  74.7 27.9 %collective-permute-start.7 = (bf16[2,2,32,1792]{3,2,1,0:T(8,128)(2,1)S(1)}, bf16[2,2,32,1792]{3,2,1,0:T(8,128)(2,1)S(1)}, u32[]{:S(2)}, u32[]{:S(2)}) collective-permute-start(bf16[2,2,32,1792]{3,2,1,0:T(8,128)(2,1)S(1)} %pad_maximum_fusion.21), channel_id=1, source_target_pairs={{0,4},{2,6},{4,0},{6,2},{8,12},{10,14},{12,8},{14,10},{16,20},{18,... | collective-permute-start | bytes 1376264 | tf_op jit(solution)/shard_map/ppermute | solution.py:74
  75.3 31.6 %collective-permute-start.3 = (bf16[2,2,2,32,896]{4,3,2,1,0:T(8,128)(2,1)S(1)}, bf16[2,2,2,32,896]{4,3,2,1,0:T(8,128)(2,1)S(1)}, u32[]{:S(2)}, u32[]{:S(2)}) collective-permute-start(bf16[2,2,2,32,896]{4,3,2,1,0:T(8,128)(2,1)S(1)} %pad_maximum_fusion.20), channel_id=1, source_target_pairs={{0,8},{2,10},{4,12},{6,14},{8,0},{10,2},{12,4},{14,6},{16,24},{18,... | collective-permute-start | bytes 1376264 | tf_op jit(solution)/shard_map/ppermute | solution.py:74
  78.8 28.4 %collective-permute-start.27 = (bf16[2,2,2,2,16,1024]{5,4,3,2,1,0:T(8,128)(2,1)S(1)}, bf16[2,2,2,2,16,1024]{5,4,3,2,1,0:T(8,128)(2,1)S(1)}, u32[]{:S(2)}, u32[]{:S(2)}) collective-permute-start(bf16[2,2,2,2,16,1024]{5,4,3,2,1,0:T(8,128)(2,1)S(1)} %pad_maximum_fusion.18), channel_id=1, source_target_pairs={{0,2},{2,0},{4,6},{6,4},{8,10},{10,8},{12,14},{14,12},{16,18},{18,... | collective-permute-start | bytes 1572872 | tf_op jit(solution)/shard_map/ppermute | solution.py:74
  102.8 27.6 %collective-permute-start.8 = (bf16[2,2,2,32,1792]{4,3,2,1,0:T(8,128)(2,1)S(1)}, bf16[2,2,2,32,1792]{4,3,2,1,0:T(8,128)(2,1)S(1)}, u32[]{:S(2)}, u32[]{:S(2)}) collective-permute-start(bf16[2,2,2,32,1792]{4,3,2,1,0:T(8,128)(2,1)S(1)} %pad_maximum_fusion.13), channel_id=1, source_target_pairs={{0,1},{1,0},{2,3},{3,2},{4,5},{5,4},{6,7},{7,6},{8,9},{9,8},{10,11... | collective-permute-start | bytes 2752520 | tf_op jit(solution)/shard_map/ppermute | solution.py:74
  120.8 51.5 %collective-permute-start.15 = (bf16[2,2,2,2,32,1536]{5,4,3,2,1,0:T(8,128)(2,1)}, bf16[2,2,2,2,32,1536]{5,4,3,2,1,0:T(8,128)(2,1)}, u32[]{:S(2)}, u32[]{:S(2)}) collective-permute-start(bf16[2,2,2,2,32,1536]{5,4,3,2,1,0:T(8,128)(2,1)} %pad_maximum_fusion.7), channel_id=1, source_target_pairs={{0,2},{2,0},{4,6},{6,4},{8,10},{10,8},{12,14},{14,12},{16,18},{18,... | collective-permute-start | bytes 4718600 | tf_op jit(solution)/shard_map/ppermute | solution.py:74
  122.5 53.5 %collective-permute-start.21 = (bf16[2,2,2,2,48,1024]{5,4,3,2,1,0:T(8,128)(2,1)}, bf16[2,2,2,2,48,1024]{5,4,3,2,1,0:T(8,128)(2,1)}, u32[]{:S(2)}, u32[]{:S(2)}) collective-permute-start(bf16[2,2,2,2,48,1024]{5,4,3,2,1,0:T(8,128)(2,1)} %pad_maximum_fusion.8), channel_id=1, source_target_pairs={{0,2},{2,0},{4,6},{6,4},{8,10},{10,8},{12,14},{14,12},{16,18},{18,... | collective-permute-start | bytes 4718600 | tf_op jit(solution)/shard_map/ppermute | solution.py:74
  132.1 45.6 %collective-permute-start.9 = (bf16[2,2,2,2,32,1792]{5,4,3,2,1,0:T(8,128)(2,1)}, bf16[2,2,2,2,32,1792]{5,4,3,2,1,0:T(8,128)(2,1)}, u32[]{:S(2)}, u32[]{:S(2)}) collective-permute-start(bf16[2,2,2,2,32,1792]{5,4,3,2,1,0:T(8,128)(2,1)} %pad_maximum_fusion.6), channel_id=1, source_target_pairs={{0,2},{2,0},{4,6},{6,4},{8,10},{10,8},{12,14},{14,12},{16,18},{18,... | collective-permute-start | bytes 5505032 | tf_op jit(solution)/shard_map/ppermute | solution.py:74
  307.1 54.3 %collective-permute-start.29 = (bf16[128,1536]{1,0:T(8,128)(2,1)}, bf16[128,1536]{1,0:T(8,128)(2,1)}, u32[]{:S(2)}, u32[]{:S(2)}) collective-permute-start(bf16[128,1536]{1,0:T(8,128)(2,1)} %convert_element_type.869), channel_id=1, source_target_pairs={{1,0},{3,2},{5,4},{7,6},{9,8},{11,10},{13,12},{15,14},{17,16},{19,... | collective-permute-start | bytes 1179656 | tf_op jit(solution)/shard_map/ppermute | solution.py:150
  321.2 34.7 %collective-permute-start.28 = (bf16[512,256]{1,0:T(8,128)(2,1)S(1)}, bf16[512,256]{1,0:T(8,128)(2,1)S(1)}, u32[]{:S(2)}, u32[]{:S(2)}) collective-permute-start(bf16[512,256]{1,0:T(8,128)(2,1)S(1)} %slice.388), channel_id=1, source_target_pairs={{1,0},{3,2},{5,4},{7,6},{9,8},{11,10},{13,12},{15,14},{17,16},{19,... | collective-permute-start | bytes 786440 | tf_op jit(solution)/shard_map/ppermute | solution.py:636
  328.2 234.0 %collective-permute-start.36 = (bf16[2,2,2,2,32,1536]{5,4,3,0,1,2:T(8,128)(2,1)}, bf16[2,2,2,2,32,1536]{5,4,3,0,1,2:T(8,128)(2,1)}, u32[]{:S(2)}, u32[]{:S(2)}) collective-permute-start(bf16[2,2,2,2,32,1536]{5,4,3,0,1,2:T(8,128)(2,1)} %bitcast.621), channel_id=1, source_target_pairs={{0,2},{2,0},{4,6},{6,4},{8,10},{10,8},{12,14},{14,12},{16,18},{18,... | collective-permute-start | bytes 4718600 | tf_op jit(solution)/shard_map/ppermute | solution.py:74
  333.1 231.9 %collective-permute-start.61 = (bf16[2,2,2,2,48,1024]{5,4,0,1,2,3:T(8,128)(2,1)}, bf16[2,2,2,2,48,1024]{5,4,0,1,2,3:T(8,128)(2,1)}, u32[]{:S(2)}, u32[]{:S(2)}) collective-permute-start(bf16[2,2,2,2,48,1024]{5,4,0,1,2,3:T(8,128)(2,1)} %bitcast.620), channel_id=1, source_target_pairs={{0,2},{2,0},{4,6},{6,4},{8,10},{10,8},{12,14},{14,12},{16,18},{18,... | collective-permute-start | bytes 4718600 | tf_op jit(solution)/shard_map/ppermute | solution.py:74
  335.3 141.0 %collective-permute-start.71 = (bf16[2,2,2,2,16,1024]{5,4,3,0,1,2:T(8,128)(2,1)}, bf16[2,2,2,2,16,1024]{5,4,3,0,1,2:T(8,128)(2,1)}, u32[]{:S(2)}, u32[]{:S(2)}) collective-permute-start(bf16[2,2,2,2,16,1024]{5,4,3,0,1,2:T(8,128)(2,1)} %bitcast.625), channel_id=1, source_target_pairs={{0,2},{2,0},{4,6},{6,4},{8,10},{10,8},{12,14},{14,12},{16,18},{18,... | collective-permute-start | bytes 1572872 | tf_op jit(solution)/shard_map/ppermute | solution.py:74
  361.1 152.4 %collective-permute-start.66 = (bf16[2,2,2,2,32,768]{5,4,2,3,0,1:T(8,128)(2,1)}, bf16[2,2,2,2,32,768]{5,4,2,3,0,1:T(8,128)(2,1)}, u32[]{:S(2)}, u32[]{:S(2)}) collective-permute-start(bf16[2,2,2,2,32,768]{5,4,2,3,0,1:T(8,128)(2,1)} %bitcast.622), channel_id=1, source_target_pairs={{0,2},{2,0},{4,6},{6,4},{8,10},{10,8},{12,14},{14,12},{16,18},{18,... | collective-permute-start | bytes 2359304 | tf_op jit(solution)/shard_map/ppermute | solution.py:74
  512.8 86.8 %collective-permute-start.81 = (bf16[2,2,2,2,32,2048]{5,4,2,3,0,1:T(8,128)(2,1)S(1)}, bf16[2,2,2,2,32,2048]{5,4,2,3,0,1:T(8,128)(2,1)S(1)}, u32[]{:S(2)}, u32[]{:S(2)}) collective-permute-start(bf16[2,2,2,2,32,2048]{5,4,2,3,0,1:T(8,128)(2,1)S(1)} %bitcast.651), channel_id=1, source_target_pairs={{0,2},{2,0},{4,6},{6,4},{8,10},{10,8},{12,14},{14,12},{16,18},{18,... | collective-permute-start | bytes 6291464 | tf_op jit(solution)/shard_map/ppermute | solution.py:74
  549.5 51.4 %collective-permute-start.76 = (bf16[2,2,2,2,32,2048]{5,4,3,0,1,2:T(8,128)(2,1)S(1)}, bf16[2,2,2,2,32,2048]{5,4,3,0,1,2:T(8,128)(2,1)S(1)}, u32[]{:S(2)}, u32[]{:S(2)}) collective-permute-start(bf16[2,2,2,2,32,2048]{5,4,3,0,1,2:T(8,128)(2,1)S(1)} %bitcast.650), channel_id=1, source_target_pairs={{0,2},{2,0},{4,6},{6,4},{8,10},{10,8},{12,14},{14,12},{16,18},{18,... | collective-permute-start | bytes 6291464 | tf_op jit(solution)/shard_map/ppermute | solution.py:74
  562.1 41.6 %collective-permute-start.86 = (bf16[2,2,2,2,64,1024]{5,4,0,1,2,3:T(8,128)(2,1)S(1)}, bf16[2,2,2,2,64,1024]{5,4,0,1,2,3:T(8,128)(2,1)S(1)}, u32[]{:S(2)}, u32[]{:S(2)}) collective-permute-start(bf16[2,2,2,2,64,1024]{5,4,0,1,2,3:T(8,128)(2,1)S(1)} %bitcast.649), channel_id=1, source_target_pairs={{0,2},{2,0},{4,6},{6,4},{8,10},{10,8},{12,14},{14,12},{16,18},{18,... | collective-permute-start | bytes 6291464 | tf_op jit(solution)/shard_map/ppermute | solution.py:74
  600.7 51.4 %collective-permute-start.82 = (bf16[2,2,2,32,2048]{4,3,1,2,0:T(8,128)(2,1)S(1)}, bf16[2,2,2,32,2048]{4,3,1,2,0:T(8,128)(2,1)S(1)}, u32[]{:S(2)}, u32[]{:S(2)}) collective-permute-start(bf16[2,2,2,32,2048]{4,3,1,2,0:T(8,128)(2,1)S(1)} %dynamic-slice_bitcast_fusion.1), channel_id=1, source_target_pairs={{0,8},{2,10},{4,12},{6,14},{8,0},{10,2},{12,4},{14,6},{16,24},{18,... | collective-permute-start | bytes 3145736 | tf_op jit(solution)/shard_map/ppermute | solution.py:74
  603.2 49.4 %collective-permute-start.77 = (bf16[2,2,2,32,2048]{4,3,2,0,1:T(8,128)(2,1)S(1)}, bf16[2,2,2,32,2048]{4,3,2,0,1:T(8,128)(2,1)S(1)}, u32[]{:S(2)}, u32[]{:S(2)}) collective-permute-start(bf16[2,2,2,32,2048]{4,3,2,0,1:T(8,128)(2,1)S(1)} %dynamic-slice_bitcast_fusion.2), channel_id=1, source_target_pairs={{0,4},{2,6},{4,0},{6,2},{8,12},{10,14},{12,8},{14,10},{16,20},{18,... | collective-permute-start | bytes 3145736 | tf_op jit(solution)/shard_map/ppermute | solution.py:74
  606.7 48.8 %collective-permute-start.87 = (bf16[2,2,2,64,1024]{4,3,0,1,2:T(8,128)(2,1)S(1)}, bf16[2,2,2,64,1024]{4,3,0,1,2:T(8,128)(2,1)S(1)}, u32[]{:S(2)}, u32[]{:S(2)}) collective-permute-start(bf16[2,2,2,64,1024]{4,3,0,1,2:T(8,128)(2,1)S(1)} %dynamic-slice_bitcast_fusion), channel_id=1, source_target_pairs={{0,1},{1,0},{2,3},{3,2},{4,5},{5,4},{6,7},{7,6},{8,9},{9,8},{10,11... | collective-permute-start | bytes 3145736 | tf_op jit(solution)/shard_map/ppermute | solution.py:74
  (201 other events, 2282.1 us)
Sparse Core Ops, SparseCore 0:
  11.0 107.6 all-gather.2
  121.7 63.9 all-gather.4

commit v2 on v1

--- a/solution.py
+++ b/solution.py
@@ -61,11 +61,7 @@
     seq = [b for b in bits if b[0] == "seq"][::-1]
     dp = [b for b in bits if b[0] == "dp"][::-1]
     pair, second, rest = dp[:1], dp[1:2], dp[2:]
-    return (
-        pair + seq + second + rest,
-        pair + second + rest + seq,
-        pair + rest + seq + second,
-    )
+    return pair + seq + second + rest, pair + second + seq + rest
 
 
 def swap(value, bit):
@@ -79,43 +75,104 @@
     return (lax.axis_index(axis) // level) % 2
 
 
-def halve(full, order):
-    left = mesh_bits()
-    total = full.shape[0]
-    rows = total >> len(left)
-    value = full.reshape((2,) * len(left) + (rows, full.shape[1]))
-    for bit in order:
-        place = left.index(bit)
-        here = bit_here(bit)
-        out = lax.dynamic_index_in_dim(value, 1 - here, place, keepdims=False)
-        kept = lax.dynamic_index_in_dim(value, here, place, keepdims=False)
-        got = swap(out, bit)
-        left.remove(bit)
-        value = kept.astype(F32) + got.astype(F32)
-        if left:
-            value = value.astype(BF16)
-    return value
-
-
-def double(shard, order):
-    bits = mesh_bits()
-    held = []
-    value = shard
-    for bit in reversed(order):
-        got = swap(value, bit)
-        here = bit_here(bit)
-        held = [b for b in bits if b in held or b == bit]
-        place = held.index(bit)
-        low = jnp.where(here == 0, value, got)
-        high = jnp.where(here == 0, got, value)
-        value = jnp.stack([low, high], axis=place)
-    return value.reshape((shard.shape[0] << len(bits), shard.shape[1]))
-
-
-def total_everywhere(value):
-    for bit in mesh_bits():
-        value = value + swap(value, bit)
-    return value
+def tie(values, arrays):
+    return lax.optimization_barrier((values, arrays))
+
+
+class Halving:
+    def __init__(self, full, order):
+        self.left = mesh_bits()
+        rows = full.shape[0] >> len(self.left)
+        self.value = full.reshape((2,) * len(self.left) + (rows, full.shape[1]))
+        self.todo = list(order)
+        self.bit = self.out = self.got = None
+
+    def prepare(self):
+        if self.got is not None:
+            place = self.left.index(self.bit)
+            kept = lax.dynamic_index_in_dim(self.value, bit_here(self.bit), place, keepdims=False)
+            self.left.remove(self.bit)
+            value = kept.astype(F32) + self.got.astype(F32)
+            self.value = value.astype(BF16) if self.left else value
+            self.got = self.out = None
+        if self.todo:
+            self.bit = self.todo.pop(0)
+            place = self.left.index(self.bit)
+            self.out = lax.dynamic_index_in_dim(self.value, 1 - bit_here(self.bit), place, keepdims=False)
+
+    def arrays(self):
+        return (self.value,) if self.out is None else (self.value, self.out)
+
+    def launch(self, arrays):
+        self.value = arrays[0]
+        if self.out is not None:
+            self.out = arrays[1]
+            self.got = swap(self.out, self.bit)
+
+
+class Doubling:
+    def __init__(self, shard, order):
+        self.rows, self.columns = shard.shape
+        self.value = shard
+        self.todo = list(reversed(order))
+        self.held = []
+        self.bit = self.got = None
+
+    def prepare(self):
+        if self.got is not None:
+            here = bit_here(self.bit)
+            self.held = [b for b in mesh_bits() if b in self.held or b == self.bit]
+            place = self.held.index(self.bit)
+            own = (jnp.arange(2) == here).reshape((2,) + (1,) * (self.value.ndim - place))
+            self.value = jnp.where(own, jnp.expand_dims(self.value, place), jnp.expand_dims(self.got, place))
+            self.got = None
+        self.bit = self.todo.pop(0) if self.todo else None
+
+    def arrays(self):
+        return (self.value,)
+
+    def launch(self, arrays):
+        (self.value,) = arrays
+        if self.bit is not None:
+            self.got = swap(self.value, self.bit)
+
+    def whole(self):
+        return self.value.reshape((self.rows << len(self.held), self.columns))
+
+
+class Summing:
+    def __init__(self, value):
+        self.value = value
+        self.todo = mesh_bits()
+        self.bit = self.got = None
+
+    def prepare(self):
+        if self.got is not None:
+            self.value = self.value + self.got
+            self.got = None
+        self.bit = self.todo.pop(0) if self.todo else None
+
+    def arrays(self):
+        return (self.value,)
+
+    def launch(self, arrays):
+        (self.value,) = arrays
+        if self.bit is not None:
+            self.got = swap(self.value, self.bit)
+
+
+def step(values, *chains):
+    for chain in chains:
+        chain.prepare()
+    values, arrays = tie(values, [chain.arrays() for chain in chains])
+    for chain, own in zip(chains, arrays):
+        chain.launch(own)
+    return values
+
+
+def finish(*chains):
+    while any(chain.todo or chain.got is not None for chain in chains):
+        step((), *chains)
 
 
 def compose_maps(earlier, later):
@@ -172,7 +229,13 @@
     return lax.ppermute(value, "seq", [(s, s + steps) for s in range(first, last)])
 
 
+SHORT = pl.CostEstimate(flops=0, bytes_accessed=0, transcendentals=0)
 PARAMS = pltpu.CompilerParams(vmem_limit_bytes=48 * 1024 * 1024)
+
+
+def group_columns(vec_ref, which):
+    shift = lax.rem(128 - pl.program_id(0) * GHEADS, 128)
+    return pltpu.roll(vec_ref[which], shift, 1)
 
 
 def lane_is_low(rows):
@@ -183,7 +246,7 @@
     return jnp.where(low, vec[:, head : head + 1], vec[:, head + 1 : head + 2])
 
 
-def ssd_forward_kernel(x_ref, b_ref, c_ref, vec_ref, row_ref, segc_ref, segr_ref, y_ref, st_ref, cb_ref):
+def ssd_forward_kernel(x_ref, b_ref, c_ref, vec_ref, row_ref, segc_ref, segr_ref, y_ref, st_ref, cb_ref, cum_ref):
     length = x_ref.shape[0]
 
     @pl.when(pl.program_id(0) == 0)
@@ -197,8 +260,9 @@
     b_low = b_ref[...].astype(BF16)
     wide = lane_is_low(length)
     narrow = lane_is_low(STRIP)
-    dt = vec_ref[0, :, 0:GHEADS]
-    rem = vec_ref[0, :, 2 * GHEADS : 3 * GHEADS]
+    dt = group_columns(vec_ref, 0)
+    rem = group_columns(vec_ref, 2)
+    cum_ref[...] = group_columns(vec_ref, 1)
     for pair in range(GHEADS // 2):
         lanes = slice(pair * 128, (pair + 1) * 128)
         xd = x_ref[:, lanes] * spread(wide, dt, 2 * pair)
@@ -208,8 +272,7 @@
             first, width = strip * STRIP, (strip + 1) * STRIP
             halves = []
             for head in (2 * pair, 2 * pair + 1):
-                at = GHEADS + head
-                gap = vec_ref[0, first : first + STRIP, at : at + 1] - row_ref[head : head + 1, :width]
+                gap = cum_ref[first : first + STRIP, head : head + 1] - row_ref[head : head + 1, :width]
                 decay = jnp.exp2(jnp.minimum(gap, 0.0))
                 m = (decay * cb_ref[first : first + STRIP, :width]).astype(BF16)
                 halves.append(dot_nn(m, xd_low[:width]))
@@ -220,19 +283,21 @@
     x_spec = pl.BlockSpec((length, GLANES), lambda g: (0, g))
     s_spec = pl.BlockSpec((STATE, GLANES), lambda g: (0, g))
     n_spec = pl.BlockSpec((length, STATE), lambda g: (0, 0))
-    v_spec = pl.BlockSpec((1, length, 4 * GHEADS), lambda g: (g, 0, 0))
+    b_spec = pl.BlockSpec((length, STATE), lambda g: (0, INNER // STATE))
+    c_spec = pl.BlockSpec((length, STATE), lambda g: (0, INNER // STATE + 1))
+    v_spec = pl.BlockSpec((4, length, 128), lambda g: (0, 0, 0))
     r_spec = pl.BlockSpec((GHEADS, length), lambda g: (g, 0))
-    return x_spec, s_spec, n_spec, v_spec, r_spec
+    return x_spec, s_spec, n_spec, b_spec, c_spec, v_spec, r_spec
 
 
 def ssd_forward(x, b, c, vec, row, seg_col, seg_row):
     length = x.shape[0]
-    x_spec, s_spec, n_spec, v_spec, r_spec = group_specs(length)
+    x_spec, s_spec, n_spec, b_spec, c_spec, v_spec, r_spec = group_specs(length)
     return pl.pallas_call(
         ssd_forward_kernel,
         grid=(GROUPS,),
         in_specs=[
-            x_spec, n_spec, n_spec, v_spec, r_spec,
+            x_spec, b_spec, c_spec, v_spec, r_spec,
             pl.BlockSpec((length, 1), lambda g: (0, 0)),
             pl.BlockSpec((1, length), lambda g: (0, 0)),
         ],
@@ -241,8 +306,9 @@
             jax.ShapeDtypeStruct((length, INNER), F32),
             jax.ShapeDtypeStruct((STATE, INNER), F32),
         ],
-        scratch_shapes=[pltpu.VMEM((length, length), F32)],
+        scratch_shapes=[pltpu.VMEM((length, length), F32), pltpu.VMEM((length, 128), F32)],
         compiler_params=PARAMS,
+        cost_estimate=SHORT,
         name="ssd_forward",
     )(x, b, c, vec, row, seg_col, seg_row)
 
@@ -255,7 +321,7 @@
 def ssd_finish_kernel(y0_ref, x_ref, z_ref, c_ref, st_ref, vec_ref, skip_ref, y_ref, ym_ref):
     length = x_ref.shape[0]
     wide = lane_is_low(length)
-    ent = vec_ref[0, :, 3 * GHEADS : 4 * GHEADS]
+    ent = group_columns(vec_ref, 3)
     c_low = c_ref[...].astype(BF16)
     for pair in range(GHEADS // 2):
         lanes = slice(pair * 128, (pair + 1) * 128)
@@ -268,17 +334,18 @@
 
 def ssd_finish(y0, x, z, c, state, vec, skip):
     length = x.shape[0]
-    x_spec, s_spec, n_spec, v_spec, _ = group_specs(length)
+    x_spec, s_spec, n_spec, b_spec, c_spec, v_spec, _ = group_specs(length)
     return pl.pallas_call(
         ssd_finish_kernel,
         grid=(GROUPS,),
-        in_specs=[x_spec, x_spec, x_spec, n_spec, s_spec, v_spec, pl.BlockSpec((1, GLANES), lambda g: (0, g))],
+        in_specs=[x_spec, x_spec, x_spec, c_spec, s_spec, v_spec, pl.BlockSpec((1, GLANES), lambda g: (0, g))],
         out_specs=[x_spec, x_spec],
         out_shape=[
             jax.ShapeDtypeStruct((length, INNER), F32),
             jax.ShapeDtypeStruct((length, INNER), BF16),
         ],
         compiler_params=PARAMS,
+        cost_estimate=SHORT,
         name="ssd_finish",
     )(y0, x, z, c, state, vec, skip)
 
@@ -286,7 +353,7 @@
 def ssd_gate_kernel(dym_ref, y_ref, x_ref, z_ref, c_ref, vec_ref, dy_ref, dz_ref, ds_ref, skip_ref):
     length = x_ref.shape[0]
     wide = lane_is_low(length)
-    ent = vec_ref[0, :, 3 * GHEADS : 4 * GHEADS]
+    ent = group_columns(vec_ref, 3)
     c_low = c_ref[...].astype(BF16)
     for pair in range(GHEADS // 2):
         lanes = slice(pair * 128, (pair + 1) * 128)
@@ -301,12 +368,12 @@
 
 def ssd_gate(dym, y, x, z, c, vec):
     length = x.shape[0]
-    x_spec, s_spec, n_spec, v_spec, _ = group_specs(length)
+    x_spec, s_spec, n_spec, b_spec, c_spec, v_spec, _ = group_specs(length)
     one_spec = pl.BlockSpec((1, GLANES), lambda g: (0, g))
     return pl.pallas_call(
         ssd_gate_kernel,
         grid=(GROUPS,),
-        in_specs=[x_spec, x_spec, x_spec, x_spec, n_spec, v_spec],
+        in_specs=[x_spec, x_spec, x_spec, x_spec, c_spec, v_spec],
         out_specs=[x_spec, x_spec, s_spec, one_spec],
         out_shape=[
             jax.ShapeDtypeStruct((length, INNER), F32),
@@ -315,13 +382,14 @@
             jax.ShapeDtypeStruct((1, INNER), F32),
         ],
         compiler_params=PARAMS,
+        cost_estimate=SHORT,
         name="ssd_gate",
     )(dym, y, x, z, c, vec)
 
 
 def ssd_backward_kernel(
     x_ref, dy_ref, b_ref, c_ref, st_ref, dst_ref, vec_ref, row_ref, segc_ref, segr_ref, skip_ref,
-    dx_ref, db_ref, dc_ref, cols_ref, rows_ref, bc_ref, dbc_ref, xd_ref, sum_ref,
+    dx_ref, db_ref, dc_ref, cols_ref, rows_ref, bc_ref, dbc_ref, xd_ref, sum_ref, cum_ref,
 ):
     length = x_ref.shape[0]
     group = pl.program_id(0)
@@ -345,9 +413,10 @@
     lane = lax.broadcasted_iota(jnp.int32, (STRIP, 128), 1)
     spot = lax.broadcasted_iota(jnp.int32, (128, 128), 0) // MHDIM
     place = lax.broadcasted_iota(jnp.int32, (128, 128), 1)
-    dt = vec_ref[0, :, 0:GHEADS]
-    rem = vec_ref[0, :, 2 * GHEADS : 3 * GHEADS]
-    ent = vec_ref[0, :, 3 * GHEADS : 4 * GHEADS]
+    dt = group_columns(vec_ref, 0)
+    rem = group_columns(vec_ref, 2)
+    ent = group_columns(vec_ref, 3)
+    cum_ref[...] = group_columns(vec_ref, 1)
     rows_ref[...] = jnp.zeros_like(rows_ref)
     for pair in range(GHEADS // 2):
         lanes = slice(pair * 128, (pair + 1) * 128)
@@ -372,7 +441,7 @@
             for half in range(2):
                 head = 2 * pair + half
                 mine = narrow if half == 0 else ~narrow
-                gap = row_ref[head : head + 1, first:] - vec_ref[0, first : first + STRIP, GHEADS + head : GHEADS + head + 1]
+                gap = row_ref[head : head + 1, first:] - cum_ref[first : first + STRIP, head : head + 1]
                 decay = jnp.exp2(jnp.minimum(gap, 0.0))
                 bc = bc_ref[first : first + STRIP, first:]
                 m = (decay * bc).astype(BF16)
@@ -398,6 +467,10 @@
         cols_ref[0] += per_head(dxd * x)
         cols_ref[1] += per_head(dtx * x * carried)
         cols_ref[2] += per_head(dy * entered)
+        passed = jnp.sum(st_ref[:, lanes] * dst_ref[:, lanes], axis=0, keepdims=True) * entx[length - 1 :]
+        cols_ref[2, length - 8 :, :] += jnp.where(
+            lax.broadcasted_iota(jnp.int32, (8, 128), 0) == 7, per_head(jnp.broadcast_to(passed, (8, 128))), 0.0
+        )
 
     @pl.when(group == GROUPS - 1)
     def _():
@@ -411,12 +484,12 @@
 
 def ssd_backward(x, dy, b, c, state, dstate, vec, row, seg_col, seg_row, skip):
     length = x.shape[0]
-    x_spec, s_spec, n_spec, v_spec, r_spec = group_specs(length)
+    x_spec, s_spec, n_spec, b_spec, c_spec, v_spec, r_spec = group_specs(length)
     return pl.pallas_call(
         ssd_backward_kernel,
         grid=(GROUPS,),
         in_specs=[
-            x_spec, x_spec, n_spec, n_spec, s_spec, s_spec, v_spec, r_spec,
+            x_spec, x_spec, b_spec, c_spec, s_spec, s_spec, v_spec, r_spec,
             pl.BlockSpec((length, 1), lambda g: (0, 0)),
             pl.BlockSpec((1, length), lambda g: (0, 0)),
             pl.BlockSpec((1, GLANES), lambda g: (0, g)),
@@ -434,10 +507,212 @@
             pltpu.VMEM((length, length), F32),
             pltpu.VMEM((length, 128), BF16),
             pltpu.VMEM((length, 128), F32),
+            pltpu.VMEM((length, 128), F32),
         ],
         compiler_params=PARAMS,
+        cost_estimate=SHORT,
         name="ssd_backward",
     )(x, dy, b, c, state, dstate, vec, row, seg_col, seg_row, skip)
+
+
+def conv_of(ext_ref, kernel_ref, taps_ref, taps_count):
+    length = taps_ref.shape[0]
+    total = jnp.zeros((length, ext_ref.shape[1]), F32) + kernel_ref[taps_count : taps_count + 1, :]
+    for j in range(taps_count):
+        total = total + kernel_ref[j : j + 1, :] * ext_ref[8 - j : 8 - j + length, :] * taps_ref[:, j : j + 1]
+    return total
+
+
+def conv_kernel_body(taps_count, xbc_ref, halo_ref, kernel_ref, taps_ref, u_ref, ext_ref):
+    ext_ref[:8, :] = halo_ref[...]
+    ext_ref[8:, :] = xbc_ref[...].astype(F32)
+    xc = conv_of(ext_ref, kernel_ref, taps_ref, taps_count)
+    u_ref[...] = silu_parts(xc)[0]
+
+
+def conv_forward(xbc, halo, kernel, taps, taps_count):
+    length, channels = xbc.shape
+    wide = 256
+    spec = pl.BlockSpec((length, wide), lambda g: (0, g))
+    eight = pl.BlockSpec((8, wide), lambda g: (0, g))
+    return pl.pallas_call(
+        partial(conv_kernel_body, taps_count),
+        grid=(channels // wide,),
+        in_specs=[spec, eight, eight, pl.BlockSpec((length, 8), lambda g: (0, 0))],
+        out_specs=spec,
+        out_shape=jax.ShapeDtypeStruct((length, channels), F32),
+        scratch_shapes=[pltpu.VMEM((length + 8, wide), F32)],
+        compiler_params=PARAMS,
+        cost_estimate=SHORT,
+        name="conv_forward",
+    )(xbc, halo, kernel, taps)
+
+
+def conv_backward_body(
+    taps_count, dx_ref, db_ref, dc_ref, xbc_ref, halo_ref, kernel_ref, taps_ref,
+    out_ref, last_ref, spill_ref, grad_ref, ext_ref, du_ref, put_ref, mask_ref,
+):
+    length = taps_ref.shape[0]
+    block = pl.program_id(0)
+    heads_blocks = INNER // 128
+
+    @pl.when(block == 0)
+    def _():
+        for j in range(taps_count):
+            mask_ref[j] = jnp.broadcast_to(taps_ref[:, j : j + 1], (length, 128))
+
+    @pl.when(block < heads_blocks)
+    def _():
+        du_ref[...] = dx_ref[...]
+
+    @pl.when(block == heads_blocks)
+    def _():
+        du_ref[...] = db_ref[...]
+
+    @pl.when(block == heads_blocks + 1)
+    def _():
+        du_ref[...] = dc_ref[...]
+
+    ext_ref[:8, :] = halo_ref[...]
+    ext_ref[8:, :] = xbc_ref[...].astype(F32)
+    xc = jnp.zeros((length, 128), F32) + kernel_ref[taps_count : taps_count + 1, :]
+    for j in range(taps_count):
+        xc = xc + kernel_ref[j : j + 1, :] * ext_ref[8 - j : 8 - j + length, :] * mask_ref[j]
+    dxc = du_ref[...] * silu_parts(xc)[1]
+    put_ref[:8, :] = jnp.zeros((8, 128), F32)
+    put_ref[8 + length :, :] = jnp.zeros((8, 128), F32)
+    total = jnp.zeros((length + 8, 128), F32)
+    sums = []
+    for j in range(taps_count):
+        masked = dxc * mask_ref[j]
+        sums.append(jnp.sum(masked * ext_ref[8 - j : 8 - j + length, :], axis=0, keepdims=True))
+        put_ref[8 : 8 + length, :] = masked * kernel_ref[j : j + 1, :]
+        total = total + put_ref[j : j + length + 8, :]
+    sums.append(jnp.sum(dxc, axis=0, keepdims=True))
+    sums.append(jnp.zeros((7 - taps_count, 128), F32))
+    spill_ref[...] = total[:8]
+    out_ref[...] = total[8:].astype(BF16)
+    last_ref[...] = total[length:]
+    grad_ref[...] = jnp.concatenate(sums, axis=0)
+
+
+def conv_backward(dx, db, dc, xbc, halo, kernel, taps, taps_count):
+    length, channels = xbc.shape
+    last = INNER // 128 - 1
+    spec = pl.BlockSpec((length, 128), lambda g: (0, g))
+    whole = pl.BlockSpec((length, 128), lambda g: (0, 0))
+    eight = pl.BlockSpec((8, 128), lambda g: (0, g))
+    return pl.pallas_call(
+        partial(conv_backward_body, taps_count),
+        grid=(channels // 128,),
+        in_specs=[
+            pl.BlockSpec((length, 128), lambda g: (0, jnp.minimum(g, last))), whole, whole,
+            spec, eight, eight, pl.BlockSpec((length, 8), lambda g: (0, 0)),
+        ],
+        out_specs=[spec, eight, eight, eight],
+        out_shape=[
+            jax.ShapeDtypeStruct((length, channels), BF16),
+            jax.ShapeDtypeStruct((8, channels), F32),
+            jax.ShapeDtypeStruct((8, channels), F32),
+            jax.ShapeDtypeStruct((8, channels), F32),
+        ],
+        scratch_shapes=[
+            pltpu.VMEM((length + 8, 128), F32),
+            pltpu.VMEM((length, 128), F32),
+            pltpu.VMEM((length + 16, 128), F32),
+            pltpu.VMEM((taps_count, length, 128), F32),
+        ],
+        compiler_params=PARAMS,
+        cost_estimate=SHORT,
+        name="conv_backward",
+    )(dx, db, dc, xbc, halo, kernel, taps)
+
+
+def softplus(v):
+    return jnp.maximum(v, 0.0) + jnp.log1p(jnp.exp(-jnp.abs(v)))
+
+
+def exact_dot(a, b):
+    return lax.dot_general(
+        a, b, (((1,), (0,)), ((), ())), precision=lax.Precision.HIGHEST, preferred_element_type=F32
+    )
+
+
+def head_values(raw_ref, heads_ref):
+    real = lax.broadcasted_iota(jnp.int32, raw_ref.shape, 1) < MHEADS
+    shifted = jnp.where(real, raw_ref[...] + heads_ref[0:1, :], 0.0)
+    dt = jnp.where(real, softplus(shifted), 0.0)
+    rate = jnp.exp(heads_ref[1:2, :])
+    return shifted, dt, rate, -dt * rate
+
+
+def heads_kernel(before_ref, raw_ref, heads_ref, seg_ref, vec_ref, row_ref):
+    length = raw_ref.shape[0]
+    _, dt, _, log_decay = head_values(raw_ref, heads_ref)
+    t = lax.broadcasted_iota(jnp.int32, (length, length), 0)
+    s = lax.broadcasted_iota(jnp.int32, (length, length), 1)
+    cumulative = exact_dot(jnp.where(t >= s, 1.0, 0.0), log_decay)
+    final = cumulative[length - 1 :]
+    seg = seg_ref[...]
+    vec_ref[0] = dt
+    vec_ref[1] = cumulative * LOG2E
+    vec_ref[2] = jnp.where(seg == seg[length - 1 :], jnp.exp(final - cumulative), 0.0)
+    vec_ref[3] = jnp.where(seg == before_ref[0], jnp.exp(cumulative), 0.0)
+    row_ref[...] = (cumulative * LOG2E).T
+
+
+def heads_forward(before, raw, heads, seg_col):
+    length = raw.shape[0]
+    vmem = pl.BlockSpec(memory_space=pltpu.VMEM)
+    return pl.pallas_call(
+        heads_kernel,
+        in_specs=[pl.BlockSpec(memory_space=pltpu.SMEM)] + [vmem] * 3,
+        out_specs=[vmem, vmem],
+        out_shape=[
+            jax.ShapeDtypeStruct((4, length, 128), F32),
+            jax.ShapeDtypeStruct((128, length), F32),
+        ],
+        compiler_params=PARAMS,
+        cost_estimate=SHORT,
+        name="heads_forward",
+    )(before, raw, heads, seg_col)
+
+
+def heads_backward_kernel(raw_ref, heads_ref, cols_ref, rows_ref, low_ref, sums_ref):
+    length = raw_ref.shape[0]
+    shifted, _, rate, log_decay = head_values(raw_ref, heads_ref)
+    filler = jnp.zeros((128 - MHEADS, length), F32)
+    gained = jnp.concatenate([rows_ref[...], filler], axis=0).T
+    leaving = cols_ref[1]
+    change = gained - cols_ref[3] + cols_ref[2] - leaving
+    t = lax.broadcasted_iota(jnp.int32, (length, length), 0)
+    s = lax.broadcasted_iota(jnp.int32, (length, length), 1)
+    da = exact_dot(jnp.where(t <= s, 1.0, 0.0), change) + jnp.sum(leaving, axis=0, keepdims=True)
+    real = lax.broadcasted_iota(jnp.int32, raw_ref.shape, 1) < MHEADS
+    ddelta = jnp.where(real, (cols_ref[0] - da * rate) / (1.0 + jnp.exp(-shifted)), 0.0)
+    low_ref[...] = ddelta.astype(BF16)
+    sums_ref[...] = jnp.concatenate(
+        [
+            jnp.sum(ddelta, axis=0, keepdims=True),
+            jnp.sum(da * log_decay, axis=0, keepdims=True),
+            jnp.zeros((6, 128), F32),
+        ],
+        axis=0,
+    )
+
+
+def heads_backward(raw, heads, cols, rows):
+    length = raw.shape[0]
+    return pl.pallas_call(
+        heads_backward_kernel,
+        out_shape=[
+            jax.ShapeDtypeStruct((length, 128), BF16),
+            jax.ShapeDtypeStruct((8, 128), F32),
+        ],
+        compiler_params=PARAMS,
+        cost_estimate=SHORT,
+        name="heads_backward",
+    )(raw, heads, cols, rows)
 
 
 def turn(value, cosine, sine):
@@ -465,6 +740,7 @@
             jax.ShapeDtypeStruct((length, 2 * KWIDTH), BF16),
         ],
         compiler_params=PARAMS,
+        cost_estimate=SHORT,
         name="rope",
     )(qkv, cosine, sine)
 
@@ -486,12 +762,23 @@
         unrope_kernel,
         out_shape=jax.ShapeDtypeStruct((length, QWIDTH + 2 * KWIDTH), BF16),
         compiler_params=PARAMS,
+        cost_estimate=SHORT,
         name="unrope",
     )(dq, dkv, more, cosine, sine)
 
 
-def attend_kernel(rank_ref, q_ref, k_ref, v_ref, segq_ref, segk_ref, o_ref, lse_ref, top_ref, sum_ref, acc_ref, mask_ref):
+def repeat_heads(kv_ref, k_ref, v_ref):
+    low = lane_is_low(kv_ref.shape[0])
+    for start, out in ((0, k_ref), (KWIDTH, v_ref)):
+        own = kv_ref[:, start : start + KWIDTH].astype(F32)
+        moved = pltpu.roll(own, AHDIM, 1)
+        out[0] = jnp.where(low, own, moved).astype(BF16)
+        out[1] = jnp.where(low, moved, own).astype(BF16)
+
+
+def attend_kernel(rank_ref, q_ref, kv_ref, segq_ref, segk_ref, o_ref, lse_ref, top_ref, sum_ref, acc_ref, mask_ref, k_ref, v_ref):
     length = q_ref.shape[0]
+    repeat_heads(kv_ref, k_ref, v_ref)
     rank = rank_ref[0]
     top_ref[...] = jnp.full_like(top_ref, NEGATIVE)
     sum_ref[...] = jnp.zeros_like(sum_ref)
@@ -537,12 +824,12 @@
     lse_ref[...] = stats
 
 
-def attend(rank, q, keys, values, seg_col, seg_blocks):
-    length = q.shape[0]
+def attend(rank, q, keyvals, seg_col, seg_blocks):
+    length, total = q.shape[0], keyvals.shape[0]
     vmem = pl.BlockSpec(memory_space=pltpu.VMEM)
     return pl.pallas_call(
         attend_kernel,
-        in_specs=[pl.BlockSpec(memory_space=pltpu.SMEM)] + [vmem] * 5,
+        in_specs=[pl.BlockSpec(memory_space=pltpu.SMEM)] + [vmem] * 4,
         out_specs=[vmem, vmem],
         out_shape=[
             jax.ShapeDtypeStruct((length, QWIDTH), F32),
@@ -553,17 +840,20 @@
             pltpu.VMEM((AHEADS, length, 128), F32),
             pltpu.VMEM((length, QWIDTH), F32),
             pltpu.VMEM((length, length), F32),
+            pltpu.VMEM((KVHEADS, total, 128), BF16),
+            pltpu.VMEM((KVHEADS, total, 128), BF16),
         ],
         compiler_params=PARAMS,
+        cost_estimate=SHORT,
         name="attend",
-    )(rank, q, keys, values, seg_col, seg_blocks)
+    )(rank, q, keyvals, seg_col, seg_blocks)
 
 
 def attend_backward_kernel(
-    rank_ref, q_ref, k_ref, v_ref, do_ref, lse_ref, delta_ref, segq_ref, segk_ref, dq_ref, dkv_ref
+    rank_ref, q_ref, kv_ref, do_ref, lse_ref, delta_ref, segq_ref, segk_ref, dq_ref, dkv_ref, k_ref, v_ref
 ):
     length = q_ref.shape[0]
-    total = k_ref.shape[1]
+    repeat_heads(kv_ref, k_ref, v_ref)
     rank = rank_ref[0]
     dq_ref[...] = jnp.zeros_like(dq_ref)
     dkv_ref[...] = jnp.zeros_like(dkv_ref)
@@ -603,20 +893,25 @@
     lax.fori_loop(0, (rank + 1) * (length // STRIP), strip_of, 0)
 
 
-def attend_backward(rank, q, keys, values, do, lse, delta, seg_row, seg_keys):
-    length, total = q.shape[0], keys.shape[1]
+def attend_backward(rank, q, keyvals, do, lse, delta, seg_row, seg_keys):
+    length, total = q.shape[0], keyvals.shape[0]
     vmem = pl.BlockSpec(memory_space=pltpu.VMEM)
     return pl.pallas_call(
         attend_backward_kernel,
-        in_specs=[pl.BlockSpec(memory_space=pltpu.SMEM)] + [vmem] * 8,
+        in_specs=[pl.BlockSpec(memory_space=pltpu.SMEM)] + [vmem] * 7,
         out_specs=[vmem, vmem],
         out_shape=[
             jax.ShapeDtypeStruct((length, QWIDTH), F32),
             jax.ShapeDtypeStruct((total, 2 * KWIDTH), F32),
         ],
+        scratch_shapes=[
+            pltpu.VMEM((KVHEADS, total, 128), BF16),
+            pltpu.VMEM((KVHEADS, total, 128), BF16),
+        ],
         compiler_params=PARAMS,
+        cost_estimate=SHORT,
         name="attend_backward",
-    )(rank, q, keys, values, do, lse, delta, seg_row, seg_keys)
+    )(rank, q, keyvals, do, lse, delta, seg_row, seg_keys)
 
 
 def gather_keyvals(own):
@@ -663,7 +958,7 @@
     w_down,
     cotangent,
 ):
-    order_x, order_y, order_z = bit_orders()
+    order_x, order_y = bit_orders()
     count = lax.axis_size("dp") * lax.axis_size("seq")
     rows = w_qkv.shape[0]
     width = rows * count
@@ -676,13 +971,17 @@
     small_width = 128 * (-(-small.shape[1] // 128))
     small = jnp.pad(small, ((0, 0), (0, small_width - small.shape[1])))
 
+    packed = jnp.concatenate([w_mamba_in, w_qkv, small], axis=1)
+    w_in = lax.all_gather(packed, ("dp", "seq"), axis=0, tiled=True)
+    second = [Doubling(w_mamba_out, order_x), Doubling(w_attn_out, order_y)]
+    third = Doubling(w_down, order_y)
+    while len(third.todo) > 2:
+        step((), *second, third)
+    finish(*second)
+    w_mo, w_ao = (chain.whole() for chain in second)
     gate_up = lax.all_gather(w_gate_up, ("dp", "seq"), axis=0, tiled=True)
-    down = lax.all_gather(w_down, ("dp", "seq"), axis=0, tiled=True)
-    w_q = double(jnp.concatenate([w_qkv, small], axis=1), order_z)
-    w_x = double(w_mamba_in[:, INNER:], order_x)
-    w_z = double(w_mamba_in[:, :INNER], order_y)
-    w_mo = double(w_mamba_out, order_x)
-    w_ao = double(w_attn_out, order_y)
+    mamba_width = w_mamba_in.shape[1]
+    w_z, w_x, w_q = w_in[:, :INNER], w_in[:, INNER:mamba_width], w_in[:, mamba_width:]
 
     smalls = w_q[:, QWIDTH + 2 * KWIDTH :]
     gain_one = smalls[:, MHEADS].astype(F32)
@@ -715,11 +1014,13 @@
     inputs = tokens[0].astype(F32)
     r1 = lax.rsqrt(jnp.mean(inputs * inputs, axis=-1, keepdims=True) + EPSILON)
     n1 = (inputs * r1 * gain_one[None, :]).astype(BF16)
+    n1, w_mo, w_ao = step((n1, w_mo, w_ao), third)
     qkv_small = dot_nn(n1, w_q)
     qkv = qkv_small[:, : QWIDTH + 2 * KWIDTH]
-    delta_raw = qkv_small[:, QWIDTH + 2 * KWIDTH : QWIDTH + 2 * KWIDTH + MHEADS]
+    delta_raw = qkv_small[:, QWIDTH + 2 * KWIDTH : QWIDTH + 2 * KWIDTH + 128]
     xbc = dot_nn(n1, w_x).astype(BF16)
     z = dot_nn(n1, w_z).astype(BF16)
+
 
     freqs = ROPE_BASE ** (-(jnp.arange(AHDIM // 2).astype(F32) * 2.0 / AHDIM))
     angles = (first_row + jnp.arange(length, dtype=jnp.int32)).astype(F32)[:, None] * freqs[None, :]
@@ -729,138 +1030,118 @@
     q, keyvals = rope(qkv, cosine, sine)
     all_keyvals = gather_keyvals(keyvals)
 
-    def doubled(start):
-        return jnp.stack(
-            [
-                jnp.tile(all_keyvals[:, start + i * AHDIM : start + (i + 1) * AHDIM], (1, 2))
-                for i in range(KVHEADS)
-            ]
-        )
-
-    keys, values = doubled(0), doubled(KWIDTH)
-
-    halo = neighbour(xbc[length - back :], 1)
-    extended = jnp.concatenate([halo, xbc]).astype(F32)
-    xc = conv_shift[None, :]
-    for j in range(taps_count):
-        xc = xc + conv_kernel[j][None, :] * extended[back - j : back - j + length] * taps[j]
-    u = jax.nn.silu(xc)
-    x_in, b_in, c_in = u[:, :INNER], u[:, INNER : INNER + STATE], u[:, INNER + STATE :]
-
-    delta_shift = delta_bias.astype(F32)
-    rate = jnp.exp(decay_log.astype(F32))
-    dt = jax.nn.softplus(delta_raw + delta_shift[None, :])
-    log_decay = -dt * rate[None, :]
-    places = jnp.arange(length, dtype=jnp.int32)
-    lower = (places[:, None] >= places[None, :]).astype(F32)
-    cumulative = jnp.dot(lower, log_decay, precision=lax.Precision.HIGHEST)
-    final = cumulative[-1]
-    carry_gate = jnp.where(seg_own[-1] == seg_before, jnp.exp(final), 0.0)
-    rem = jnp.where(seg_col == seg_own[-1], jnp.exp(final[None, :] - cumulative), 0.0)
-    ent = jnp.where(seg_col == seg_before, jnp.exp(cumulative), 0.0)
-    vec = jnp.stack([dt, cumulative * LOG2E, rem, ent], axis=1)
-    vec = vec.reshape(length, 4, GROUPS, GHEADS).transpose(2, 0, 1, 3).reshape(GROUPS, length, 4 * GHEADS)
-    row = (cumulative * LOG2E).T
-    gate_lanes = jnp.repeat(carry_gate, MHDIM)
+    halo = jnp.pad(neighbour(xbc[length - back :], 1).astype(F32), ((8 - back, 0), (0, 0)))
+    kernel_wide = jnp.concatenate([conv_kernel, conv_shift[None, :]])
+    kernel_wide = jnp.pad(kernel_wide, ((0, 7 - taps_count), (0, 0)))
+    taps_wide = jnp.pad(jnp.concatenate(taps, axis=1), ((0, 0), (0, 8 - taps_count)))
+    u = conv_forward(xbc, halo, kernel_wide, taps_wide, taps_count)
+
+    heads = jnp.stack([delta_bias, decay_log]).astype(F32)
+    heads = jnp.pad(heads, ((0, 6), (0, 128 - MHEADS)))
+    vec, row = heads_forward(seg_before.reshape(1), delta_raw, heads, seg_col)
+    gate_lanes = jnp.repeat(vec[3, -1, :MHEADS], MHDIM)
     skip_lanes = jnp.repeat(skip_gain.astype(F32), MHDIM)[None, :]
 
-    y_local, state_part = ssd_forward(x_in, b_in, c_in, vec, row, seg_col, seg_row)
+    y_local, state_part = ssd_forward(u, u, u, vec, row, seg_col, seg_row)
     state_in = state_from_behind(gate_lanes, state_part)
 
-    attended, lse = attend(rank_arg, q, keys, values, seg_col, seg_full.reshape(total // length, length))
+    q, _ = tie(q, state_part)
+    attended, lse = attend(rank_arg, q, all_keyvals, seg_col, seg_full.reshape(total // length, length))
     attended_low = attended.astype(BF16)
 
-    y, mixed_low = ssd_finish(y_local, x_in, z, c_in, state_in, vec, skip_lanes)
+    y, mixed_low = ssd_finish(y_local, u, z, u, state_in, vec, skip_lanes)
+    mixed_low = step(mixed_low, third)
     residual = inputs + dot_nn(mixed_low, w_mo) + dot_nn(attended_low, w_ao)
 
     r2 = lax.rsqrt(jnp.mean(residual * residual, axis=-1, keepdims=True) + EPSILON)
     n2 = (residual * r2 * gain_two[None, :]).astype(BF16)
     gu = dot_nn(n2, gate_up)
+    gu = step(gu, third)
+    down = third.whole()
     half = gu.shape[1] // 2
     gate, up = gu[:, :half], gu[:, half:]
     gate_act, gate_slope = silu_parts(gate)
     hidden = (gate_act * up).astype(BF16)
-    block_out = (residual + dot_nn(hidden, down)).astype(BF16)
-
     upstream_low = cotangent[0]
     upstream = upstream_low.astype(F32)
-    grad_down = halve(dot_tn(hidden, upstream_low).astype(BF16), order_x)
+    sum_down = Halving(dot_tn(hidden, upstream_low).astype(BF16), order_x)
+    hidden = step(hidden, sum_down)
+    block_out = (residual + dot_nn(hidden, down)).astype(BF16)
+    upstream_low, block_out = step((upstream_low, block_out), sum_down)
     dhidden = dot_nt(upstream_low, down)
     dgate = (dhidden * up * gate_slope).astype(BF16)
     dup = (dhidden * gate_act).astype(BF16)
-    grad_gate = halve(dot_tn(n2, dgate).astype(BF16), order_y)
-    grad_up = halve(dot_tn(n2, dup).astype(BF16), order_z)
-    dn2 = dot_nt(dgate, gate_up[:, :half]) + dot_nt(dup, gate_up[:, half:])
+    dgu = jnp.concatenate([dgate, dup], axis=1)
+    grad_gate_up = dot_tn(n2, dgu).astype(BF16)
+    dgu, grad_gate_up = tie(dgu, grad_gate_up)
+    grad_gate_up = lax.psum_scatter(grad_gate_up, ("dp", "seq"), scatter_dimension=0, tiled=True).astype(F32)
+    dn2 = dot_nt(dgu, gate_up)
     scaled = gain_two[None, :] * dn2
     grad_gain_two = jnp.sum(dn2 * residual * r2, axis=0)
     dhs = upstream + r2 * scaled - residual * (r2 * r2 * r2) * jnp.mean(scaled * residual, axis=-1, keepdims=True)
     dhs_low = dhs.astype(BF16)
-    grad_mo = halve(dot_tn(mixed_low, dhs_low).astype(BF16), order_x)
-    grad_ao = halve(dot_tn(attended_low, dhs_low).astype(BF16), order_y)
     dym = dot_nt(dhs_low, w_mo)
     do = dot_nt(dhs_low, w_ao).astype(BF16)
-
-    dy, dz, dstate_part, skip_cols = ssd_gate(dym, y, x_in, z, c_in, vec)
+    sum_mo = Halving(dot_tn(mixed_low, dhs_low).astype(BF16), order_y)
+    sum_ao = Halving(dot_tn(attended_low, dhs_low).astype(BF16), order_x)
+    dym, do = step((dym, do), sum_mo, sum_ao)
+
+    dy, dz, dstate_part, skip_cols = ssd_gate(dym, y, u, z, u, vec)
     dstate = state_from_ahead(gate_lanes, dstate_part)
-    grad_z = halve(dot_tn(n1, dz).astype(BF16), order_y)
-
-    heads = (jnp.arange(QWIDTH)[None, :] // AHDIM == jnp.arange(AHEADS)[:, None]).astype(F32)
+    dz, dy = step((dz, dy), sum_down, sum_mo, sum_ao)
+    sum_z = Halving(dot_tn(n1, dz).astype(BF16), order_y)
+    dy = step(dy, sum_z)
+
+    dx, db, dc, cols, rows_sum = ssd_backward(
+        u, dy, u, u, state_in, dstate, vec, row, seg_row.T, seg_row, skip_lanes
+    )
+    cols, rows_sum, dx = step((cols, rows_sum, dx), sum_down, sum_ao, sum_mo, sum_z)
+    ddelta_low, head_sums = heads_backward(delta_raw, heads, cols, rows_sum)
+    grad_skip = jnp.sum(skip_cols.reshape(MHEADS, MHDIM), axis=1)
+    sum_heads = Summing(jnp.concatenate([head_sums[0, :MHEADS], head_sums[1, :MHEADS], grad_skip]))
+
+    dxbc, last_rows, spilled, conv_grads = conv_backward(dx, db, dc, xbc, halo, kernel_wide, taps_wide, taps_count)
+    incoming = jnp.pad(neighbour(spilled[8 - back :], -1), ((8 - back, 0), (0, 0)))
+    dxbc, last_rows = step((dxbc, last_rows), sum_down, sum_ao)
+    dxbc = lax.dynamic_update_slice_in_dim(dxbc, (last_rows + incoming).astype(BF16), length - 8, 0)
+    cut = 640
+    sum_x = [
+        Halving(dot_tn(n1, dxbc[:, :cut]).astype(BF16), order_y),
+        Halving(dot_tn(n1, dxbc[:, cut : 2 * cut]).astype(BF16), order_x),
+        Halving(dot_tn(n1, dxbc[:, 2 * cut :]).astype(BF16), order_x),
+    ]
+    do = step(do, *sum_x, sum_heads)
+
+    owner = (jnp.arange(QWIDTH)[None, :] // AHDIM == jnp.arange(AHEADS)[:, None]).astype(F32)
     delta = lax.dot_general(
-        heads, do.astype(F32) * attended, (((1,), (1,)), ((), ())), precision=lax.Precision.HIGHEST
+        owner, do.astype(F32) * attended, (((1,), (1,)), ((), ())), precision=lax.Precision.HIGHEST
     )
+    do, delta = step((do, delta), *sum_x, sum_mo, sum_z)
     dq, dkv = attend_backward(
-        rank_arg, q, keys, values, do, lse[:, :AHEADS].T, delta, seg_row, seg_full[:, None]
+        rank_arg, q, all_keyvals, do, lse[:, :AHEADS].T, delta, seg_row, seg_full[:, None]
     )
+    dq, dkv = step((dq, dkv), *sum_x, sum_heads, sum_z, sum_mo, sum_ao, sum_down)
     own_dkv, more_dkv = scatter_keyval_grads(dkv, length)
     dqkv = unrope(dq, own_dkv, more_dkv, cosine, sine)
-
-    dx, db, dc, cols, rows_sum = ssd_backward(
-        x_in, dy, b_in, c_in, state_in, dstate, vec, row, seg_row.T, seg_row, skip_lanes
-    )
-    direct, leaving, entering, gone = (cols[i, :, :MHEADS] for i in range(4))
-    passed = jnp.sum((dstate * state_in).reshape(STATE, MHEADS, MHDIM), axis=(0, 2)) * carry_gate
-    change = rows_sum.T - gone + entering - leaving
-    upper = (places[:, None] <= places[None, :]).astype(F32)
-    da = jnp.dot(upper, change, precision=lax.Precision.HIGHEST)
-    da = da + (jnp.sum(leaving, axis=0) + passed)[None, :]
-    ddt = direct - da * rate[None, :]
-    ddelta = ddt * jax.nn.sigmoid(delta_raw + delta_shift[None, :])
-    grad_decay = jnp.sum(da * log_decay, axis=0)
-    grad_shift = jnp.sum(ddelta, axis=0)
-    grad_skip = jnp.sum(skip_cols.reshape(MHEADS, MHDIM), axis=1)
-
-    _, slope = silu_parts(xc)
-    dxc = jnp.concatenate([dx, db, dc], axis=1) * slope
-    grad_bias = jnp.sum(dxc, axis=0)
-    kernel_rows = []
-    spilled = jnp.zeros((length + back, dxc.shape[1]), F32)
-    for j in range(taps_count):
-        masked = dxc * taps[j]
-        kernel_rows.append(jnp.sum(masked * extended[back - j : back - j + length], axis=0))
-        spilled = spilled + jnp.pad(masked * conv_kernel[j][None, :], ((back - j, j), (0, 0)))
-    incoming = neighbour(spilled[:back], -1)
-    dxbc = spilled[back:]
-    dxbc = jnp.concatenate([dxbc[: length - back], dxbc[length - back :] + incoming]).astype(BF16)
-
-    kernel_grad = jnp.stack(kernel_rows).reshape(taps_count, count, channels).transpose(1, 0, 2)
+    sum_qkv = Halving(dot_tn(n1, dqkv).astype(BF16), order_y)
+    dqkv = step(dqkv, *sum_x, sum_heads, sum_z, sum_mo, sum_ao, sum_qkv)
+
+    kernel_grad = conv_grads[:taps_count].reshape(taps_count, count, channels).transpose(1, 0, 2)
     kernel_grad = kernel_grad.reshape(count, taps_count * channels)
-    shift_grad = grad_bias.reshape(count, channels)
-    head_grads = total_everywhere(jnp.concatenate([grad_shift, grad_decay, grad_skip]))
-
+    shift_grad = conv_grads[taps_count].reshape(count, channels)
     def fit_all(value, columns):
         spare = rows * columns - value.shape[1]
         return jnp.pad(value, ((0, 0), (0, spare))).reshape(width, columns)
 
-    ddelta_wide = jnp.pad(ddelta.astype(BF16), ((0, 0), (0, small_width - MHEADS)))
+    ddelta_wide = jnp.pad(ddelta_low, ((0, 0), (0, small_width - 128)))
     dq_small = jnp.concatenate([dqkv, ddelta_wide], axis=1)
     dn1 = dot_nt(dq_small, w_q) + dot_nt(dz, w_z) + dot_nt(dxbc, w_x)
     scaled = gain_one[None, :] * dn1
     grad_gain_one = jnp.sum(dn1 * inputs * r1, axis=0)
     grad_tokens = dhs + r1 * scaled - inputs * (r1 * r1 * r1) * jnp.mean(scaled * inputs, axis=-1, keepdims=True)
 
-    grad_qkv = halve(dot_tn(n1, dqkv).astype(BF16), order_z)
     parts = [
-        dot_tn(n1, ddelta.astype(BF16)),
+        dot_tn(n1, ddelta_low)[:, :MHEADS],
         grad_gain_one[:, None],
         grad_gain_two[:, None],
         fit_all(kernel_grad, conv_cols),
@@ -868,16 +1149,12 @@
     ]
     used = sum(p.shape[1] for p in parts)
     parts.append(jnp.zeros((width, small_width - used), F32))
-    grad_small = halve(jnp.concatenate(parts, axis=1).astype(BF16), order_x)
-    cut = 640
-    grad_x = jnp.concatenate(
-        [
-            halve(dot_tn(n1, dxbc[:, :cut]).astype(BF16), order_x),
-            halve(dot_tn(n1, dxbc[:, cut : 2 * cut]).astype(BF16), order_y),
-            halve(dot_tn(n1, dxbc[:, 2 * cut :]).astype(BF16), order_z),
-        ],
-        axis=1,
-    )
+    small_sum = jnp.concatenate(parts, axis=1).astype(BF16).reshape(count, rows, small_width)
+    small_sum = lax.all_to_all(small_sum, ("dp", "seq"), 0, 0, tiled=True)
+    grad_small = jnp.sum(small_sum.astype(F32), axis=0)
+    finish(sum_z, sum_qkv, sum_mo, sum_ao, sum_down, sum_heads, *sum_x)
+    grad_x = jnp.concatenate([chain.value for chain in sum_x], axis=1)
+    head_grads = sum_heads.value
 
     at = MHEADS + 2
     kernel_own = grad_small[:, at : at + conv_cols].reshape(-1)[: taps_count * channels].reshape(taps_count, channels)
@@ -887,19 +1164,19 @@
         block_out[None],
         grad_tokens[None],
         grad_small[:, MHEADS],
-        jnp.concatenate([grad_z, grad_x], axis=1),
+        jnp.concatenate([sum_z.value, grad_x], axis=1),
         grad_small[:, :MHEADS],
         kernel_own,
         shift_own,
         head_grads[:MHEADS],
         head_grads[MHEADS : 2 * MHEADS],
         head_grads[2 * MHEADS :],
-        grad_mo,
-        grad_qkv,
-        grad_ao,
+        sum_mo.value,
+        sum_qkv.value,
+        sum_ao.value,
         grad_small[:, MHEADS + 1],
-        jnp.concatenate([grad_gate, grad_up], axis=1),
-        grad_down,
+        grad_gate_up,
+        sum_down.value,
     )
 
 

time: 718 us -> 578 us (0.81)
  waiting for transfers between devices: 249 us -> 146 us
  local copies, waits for them, and re-layouts: 97.7 us -> 57.7 us
  Pallas kernels: 74.3 us -> 95.8 us
  starting transfers between devices: 106 us -> 96.5 us
    ppermute x85 -> x60, waiting for transfers between devices: 236 us -> 126 us  [swap(): return lax.ppermute(value, axis, [(i, i ^ level) for i in range(size)])]
    dynamic_slice x20 -> x3, local copies, waits for them, and re-layouts: 29.4 us -> 0.3 us  [prepare(): lax.dynamic_index_in_dim(self.value, 1 - bit_here(self.bit), place, keepd...]
    pallas_call x1 -> x5, Pallas kernels: 8.73 us -> 29.8 us  [the longest x1 12.8 us: conv_backward(): pl.pallas_call(partial(conv_backward_body, taps_count), grid=(channels //...]
    select_n x2 -> x15, other arithmetic: 1.02 us -> 22 us  [prepare(): jnp.where(own, jnp.expand_dims(self.value, place), jnp.expand_dims(self.g...]
    another operation x52 -> x1, other arithmetic: 17.9 us -> 0.01 us  [the longest x50 16.9 us: double(): value = jnp.stack([low, high], axis=place)]
    squeeze x45 -> x39, local copies, waits for them, and re-layouts: 2.99 us -> 16 us  [the longest x38 16 us: prepare(): lax.dynamic_index_in_dim(self.value, 1 - bit_here(self.bit), place, keepd...]
    ppermute x1, waiting for transfers between devices: 0.01 us -> 11.2 us  [state_from_ahead(): return lax.ppermute(low, 'seq', [(1, 0)]).astype(F32)]
    dot_general x11 -> x10, matrix products: 30.3 us -> 19.4 us  [dot_tn(): lax.dot_general(a, b, (((0,), (0,)), ((), ())), preferred_element_type=F32)]
  transfers between devices with their start and end apart: 93 -> 70, of which waited for: 48 -> 23; matrix products, arithmetic and copies ran while one was open for 28% -> 25% of each run, Pallas kernels for 9% -> 17%
where the time goes in v2:
time: 578 us; the launch traced here: 569 us
  waiting for transfers between devices  146 us (25%)
  starting transfers between devices  96.5 us (17%)
  Pallas kernels  95.8 us (17%)
  matrix products  83.2 us (14%)
  other arithmetic  73.4 us (13%)
  local copies, waits for them, and re-layouts  57.7 us (10%)
  between operations  15.9 us (3%)
    ppermute x60, waiting for transfers between devices, swap(): return lax.ppermute(value, axis, [(i, i ^ level) for i in range(size)])  126 us
    ppermute x60, starting transfers between devices, swap(): return lax.ppermute(value, axis, [(i, i ^ level) for i in range(size)])  81.7 us
    dot_general x7, matrix products, dot_nt(): lax.dot_general(a, b, (((1,), (1,)), ((), ())), preferred_element_type=F32)  33.6 us
    dot_general x7, matrix products, dot_nn(): lax.dot_general(a, b, (((1,), (0,)), ((), ())), preferred_element_type=F32)  29.6 us
    pallas_call x1, Pallas kernels, ssd_backward(): pl.pallas_call(ssd_backward_kernel, grid=(GROUPS,), in_specs=[x_spec, x_s...  28.5 us
    select_n x15, other arithmetic, prepare(): jnp.where(own, jnp.expand_dims(self.value, place), jnp.expand_dims(self.g...  22 us
    dot_general x10, matrix products, dot_tn(): lax.dot_general(a, b, (((0,), (0,)), ((), ())), preferred_element_type=F32)  19.4 us
    convert_element_type x32, other arithmetic, prepare(): self.value = value.astype(BF16) if self.left else value  18.9 us
  transfers between devices with their start and end apart: 70, of which 23 were waited for; matrix products, arithmetic and copies ran while one was open for 25% of the time, Pallas kernels for 17%

profile of v2, /device:TPU:0, one launch (start us, length us, event | category | flops | bytes accessed | tf_op | source)
XLA Modules:
  0.0 569.0 jit_solution(14444718495566425272)
XLA Ops:
  20.2 7.2 %collective-permute-done.1 = bf16[16,1024]{1,0:T(8,128)(2,1)S(1)} collective-permute-done((bf16[16,1024]{1,0:T(8,128)(2,1)}, bf16[16,1024]{1,0:T(8,128)(2,1)S(1)}, u32[]{:S(2)}, u32[]{:S(2)}) %collective-permute-start.1) | collective-permute-done | bytes 32800 | tf_op jit(solution)/shard_map/ppermute | solution.py:70
  43.6 8.6 %collective-permute-done.5 = bf16[2,64,1024]{2,1,0:T(8,128)(2,1)S(1)} collective-permute-done((bf16[2,64,1024]{2,1,0:T(8,128)(2,1)S(1)}, bf16[2,64,1024]{2,1,0:T(8,128)(2,1)S(1)}, u32[]{:S(2)}, u32[]{:S(2)}) %collective-permute-start.5) | collective-permute-done | bytes 262176 | tf_op jit(solution)/shard_map/ppermute | solution.py:70
  71.2 15.7 %collective-permute-done.8 = bf16[2,2,2,48,1024]{4,3,2,1,0:T(8,128)(2,1)S(1)} collective-permute-done((bf16[2,2,2,48,1024]{4,3,2,1,0:T(8,128)(2,1)S(1)}, bf16[2,2,2,48,1024]{4,3,2,1,0:T(8,128)(2,1)S(1)}, u32[]{:S(2)}, u32[]{:S(2)}) %collective-permute-start.8) | collective-permute-done | bytes 786464 | tf_op jit(solution)/shard_map/ppermute | solution.py:70
  94.7 9.0 %collective-permute-done.12 = bf16[2,2,64,1024]{3,2,1,0:T(8,128)(2,1)S(1)} collective-permute-done((bf16[2,2,64,1024]{3,2,1,0:T(8,128)(2,1)S(1)}, bf16[2,2,64,1024]{3,2,1,0:T(8,128)(2,1)S(1)}, u32[]{:S(2)}, u32[]{:S(2)}) %collective-permute-start.12) | collective-permute-done | bytes 524320 | tf_op jit(solution)/shard_map/ppermute | solution.py:70
  143.7 9.5 %ssd_forward.1 = (f32[512,1536]{1,0:T(8,128)S(1)}, f32[128,1536]{1,0:T(8,128)S(1)}) custom-call(f32[512,1792]{1,0:T(8,128)} %copy-done, f32[512,1792]{1,0:T(8,128)} %copy-done, f32[512,1792]{1,0:T(8,128)} %copy-done, f32[4,512,128]{2,1,0:T(8,128)S(1)} %get-tuple-element.228.vec_ref, f32[128,512]{1,0:T(8,128)S(1)} %get-tuple-element.229.row_ref, ...), custom_call_target="tpu_custom_call" | custom-call | tf_op jit(solution)/shard_map/ssd_forward/pallas_call | solution.py:296
  158.4 11.8 %attend.1 = (f32[512,512]{1,0:T(8,128)S(1)}, f32[512,128]{1,0:T(8,128)S(1)}) custom-call(s32[1]{0:T(128)} %bitcast.13.rank_ref, bf16[512,512]{1,0:T(8,128)(2,1)S(1)} %get-tuple-element.237.q_ref, bf16[1024,256]{1,0:T(8,128)(2,1)S(1)} %pad_maximum_fusion.1.kv_ref, s32[512,1]{1,0:T(8,128)S(1)} %copy.184.seg_ref.segc_ref.segq_ref, ...), custom_call_target="tpu_custom_call" | custom-call | tf_op jit(solution)/shard_map/attend/pallas_call | solution.py:830
  170.4 6.9 %ssd_finish.1 = (f32[512,1536]{1,0:T(8,128)}, bf16[512,1536]{1,0:T(8,128)(2,1)S(1)}) custom-call(f32[512,1536]{1,0:T(8,128)} %copy-done.8, f32[512,1792]{1,0:T(8,128)} %copy-done, bf16[512,1536]{1,0:T(8,128)(2,1)S(1)} %convolution_convert_fusion.4.z_ref, f32[512,1792]{1,0:T(8,128)} %copy-done, f32[128,1536]{1,0:T(8,128)S(1)} %convert_element_type.644.st_ref, ...), custom_call_target="tpu_custom_call" | custom-call | tf_op jit(solution)/shard_map/ssd_finish/pallas_call | solution.py:338
  184.6 7.9 %all-gather.5.cloned.1.call-done = bf16[1024,4096]{1,0:T(8,128)(2,1)} async-done(((bf16[32,4096]{1,0:T(8,128)(2,1)}), bf16[1024,4096]{1,0:T(8,128)(2,1)}) %all-gather.5.cloned.1.call-update) | async-done | bytes 8388624 | tf_op jit(solution)/shard_map/all_gather | solution.py:982
  192.6 7.7 %fusion.95 = f32[512,4096]{1,0:T(8,128)S(1)} fusion(bf16[1024,4096]{1,0:T(8,128)(2,1)} %all-gather.5.cloned.1.call-done, f32[512,1024]{1,0:T(8,128)} %get-tuple-element.469, f32[1024]{0:T(1024)S(1)} %get-tuple-element.440, f32[512]{0:T(512)S(1)} %get-tuple-element.464), kind=kOutput, calls=%fused_computation.274 | convolution fusion | flops 4296540160 | bytes 18880512 | tf_op jit(solution)/shard_map/dot_general | solution.py:37
  200.3 7.7 %broadcast_select_fusion = bf16[2,2,2,2,2,64,1024]{6,5,4,3,2,1,0:T(8,128)(2,1)} fusion(pred[2]{0:T(512)(128)(4,1)S(1)} %copy-done.79, bf16[2,2,2,2,64,1024]{5,4,3,2,1,0:T(8,128)(2,1)} %collective-permute-done.17, bf16[2,2,2,2,64,1024]{5,4,3,2,1,0:T(8,128)(2,1)} %broadcast_select_fusion.2), kind=kLoop, calls=%fused_computation.15 | loop fusion | flops 2097152 | bytes 8388610 | tf_op jit(solution)/shard_map/jit(_where)/select_n | solution.py:127
  214.6 6.9 %add_convert_fusion = bf16[512,1024]{1,0:T(8,128)(2,1)} fusion(f32[512,1024]{1,0:T(8,128)} %get-tuple-element.469, bf16[512,2048]{1,0:T(8,128)(2,1)} %copy-done.57, bf16[2048,1024]{1,0:T(8,128)(2,1)} %bitcast.292), kind=kOutput, calls=%fused_computation.50 | convolution fusion | flops 2148532224 | bytes 9437184 | tf_op jit(solution)/shard_map/dot_general | solution.py:37
  233.2 7.2 %convolution_convert_fusion = bf16[1024,4096]{1,0:T(8,128)(2,1)} fusion(f32[512,1024]{1,0:T(8,128)S(1)} %copy-done.37, f32[1024]{0:T(1024)S(1)} %get-tuple-element.440, f32[512]{0:T(512)S(1)} %get-tuple-element.464, bf16[512,2048]{1,0:T(8,128)(2,1)S(1)} %get-tuple-element.451, bf16[512,2048]{1,0:T(8,128)(2,1)S(1)} %get-tuple-element.450), kind=kOutput, calls=%fused_computation | convolution fusion | flops 4309123072 | bytes 14686208 | tf_op jit(solution)/shard_map/dot_general | solution.py:45
  240.3 10.7 %multiply_reduce_fusion = (bf16[1024]{0:T(1024)(128)(2,1)}, f32[512]{0:T(512)S(1)}, f32[512,1024]{1,0:T(8,128)S(1)}) fusion(f32[512,1024]{1,0:T(8,128)} %get-tuple-element.469, f32[512]{0:T(512)S(1)} %get-tuple-element.464, f32[1024]{0:T(1024)S(1)} %get-tuple-element.440, bf16[512,4096]{1,0:T(8,128)(2,1)} %pad_maximum_fusion, ...), kind=kOutput, calls=%fused_computation.46 | convolution fusion | flops 4298111488 | bytes 16787456 | tf_op jit(solution)/shard_map/dot_general | solution.py:41
  264.0 6.6 %collective-permute-start.19 = (bf16[2,2,2,64,1024]{4,3,0,1,2:T(8,128)(2,1)}, bf16[2,2,2,64,1024]{4,3,0,1,2:T(8,128)(2,1)}, u32[]{:S(2)}, u32[]{:S(2)}) collective-permute-start(bf16[2,2,2,64,1024]{4,3,0,1,2:T(8,128)(2,1)} %dynamic-slice_bitcast_fusion), channel_id=1, source_target_pairs={{0,1},{1,0},{2,3},{3,2},{4,5},{5,4},{6,7},{7,6},{8,9},{9,8},{10,11... | collective-permute-start | bytes 3145736 | tf_op jit(solution)/shard_map/ppermute | solution.py:70
  270.5 7.4 %ssd_gate.1 = (f32[512,1536]{1,0:T(8,128)}, bf16[512,1536]{1,0:T(8,128)(2,1)S(1)}, f32[128,1536]{1,0:T(8,128)S(1)}, f32[1,1536]{1,0:T(1,128)S(1)}) custom-call(f32[512,1536]{1,0:T(8,128)} %fusion.99.dym_ref, f32[512,1536]{1,0:T(8,128)} %get-tuple-element.252.y_ref, f32[512,1792]{1,0:T(8,128)} %copy-done, bf16[512,1536]{1,0:T(8,128)(2,1)S(1)} %copy-done.5, ...), custom_call_target="tpu_custom_call" | custom-call | tf_op jit(solution)/shard_map/ssd_gate/pallas_call | solution.py:373
  291.6 11.2 %collective-permute-done.22 = bf16[128,1536]{1,0:T(8,128)(2,1)} collective-permute-done((bf16[128,1536]{1,0:T(8,128)(2,1)}, bf16[128,1536]{1,0:T(8,128)(2,1)}, u32[]{:S(2)}, u32[]{:S(2)}) %collective-permute-start.22) | collective-permute-done | bytes 393248 | tf_op jit(solution)/shard_map/ppermute | solution.py:207
  322.4 28.5 %ssd_backward.1 = (f32[512,1536]{1,0:T(8,128)}, f32[512,128]{1,0:T(8,128)S(1)}, f32[512,128]{1,0:T(8,128)S(1)}, f32[4,512,128]{2,1,0:T(8,128)S(1)}, f32[24,512]{1,0:T(8,128)S(1)}) custom-call(f32[512,1792]{1,0:T(8,128)} %copy-done, f32[512,1536]{1,0:T(8,128)} %get-tuple-element.263.dy_ref, f32[512,1792]{1,0:T(8,128)} %copy-done, f32[512,1792]{1,0:T(8,128)} %copy-done, ...), custom_call_target="tpu_custom_call" | custom-call | tf_op jit(solution)/shard_map/ssd_backward/pallas_call | solution.py:488
  358.4 12.8 %conv_backward.1 = (bf16[512,1792]{1,0:T(8,128)(2,1)S(1)}, f32[8,1792]{1,0:T(8,128)S(1)}, f32[8,1792]{1,0:T(8,128)S(1)}, f32[8,1792]{1,0:T(8,128)S(1)}) custom-call(f32[512,1536]{1,0:T(8,128)} %get-tuple-element.276.dx_ref, f32[512,128]{1,0:T(8,128)S(1)} %get-tuple-element.277.db_ref, f32[512,128]{1,0:T(8,128)S(1)} %get-tuple-element.278.dc_ref, ...), custom_call_target="tpu_custom_call" | custom-call | tf_op jit(solution)/shard_map/conv_backward/pallas_call | solution.py:605
  394.6 8.2 %collective-permute-start.38 = (f32[72]{0:T(128)S(1)}, f32[72]{0:T(128)S(1)}, u32[]{:S(2)}, u32[]{:S(2)}) collective-permute-start(f32[72]{0:T(128)S(1)} %pad_maximum_fusion.4), channel_id=1, source_target_pairs={{0,16},{2,18},{4,20},{6,22},{8,24},{10,26},{12,28},{14,30},{16,0},... | collective-permute-start | bytes 872 | tf_op jit(solution)/shard_map/ppermute | solution.py:70
  422.3 9.8 %attend_backward.1 = (f32[512,512]{1,0:T(8,128)S(1)}, f32[1024,256]{1,0:T(8,128)S(1)}) custom-call(s32[1]{0:T(128)} %bitcast.13.rank_ref, bf16[512,512]{1,0:T(8,128)(2,1)S(1)} %copy-done.16, bf16[1024,256]{1,0:T(8,128)(2,1)S(1)} %copy-done.7, bf16[512,512]{1,0:T(8,128)(2,1)S(1)} %copy-done.17, f32[8,512]{1,0:T(8,128)S(1)} %slice_bitcast_fusion.lse_ref, ...), custom_call_target="tpu_custom_call" | custom-call | tf_op jit(solution)/shard_map/attend_backward/pallas_call | solution.py:899
  432.2 15.7 %collective-permute-done.37 = bf16[2,2,2,32,512]{4,3,0,1,2:T(8,128)(2,1)S(1)} collective-permute-done((bf16[2,2,2,32,512]{4,3,0,1,2:T(8,128)(2,1)S(1)}, bf16[2,2,2,32,512]{4,3,0,1,2:T(8,128)(2,1)S(1)}, u32[]{:S(2)}, u32[]{:S(2)}) %collective-permute-start.37) | collective-permute-done | bytes 262176 | tf_op jit(solution)/shard_map/ppermute | solution.py:70
  448.2 16.2 %collective-permute-done.39 = bf16[2,2,32,1536]{3,2,0,1:T(8,128)(2,1)S(1)} collective-permute-done((bf16[2,2,32,1536]{3,2,0,1:T(8,128)(2,1)S(1)}, bf16[2,2,32,1536]{3,2,0,1:T(8,128)(2,1)S(1)}, u32[]{:S(2)}, u32[]{:S(2)}) %collective-permute-start.39) | collective-permute-done | bytes 393248 | tf_op jit(solution)/shard_map/ppermute | solution.py:70
  480.2 8.6 %collective-permute-done.44 = bf16[2,2,32,640]{3,2,0,1:T(8,128)(2,1)S(1)} collective-permute-done((bf16[2,2,32,640]{3,2,0,1:T(8,128)(2,1)S(1)}, bf16[2,2,32,640]{3,2,0,1:T(8,128)(2,1)S(1)}, u32[]{:S(2)}, u32[]{:S(2)}) %collective-permute-start.44) | collective-permute-done | bytes 163872 | tf_op jit(solution)/shard_map/ppermute | solution.py:70
  531.1 6.1 %collective-permute-done.59 = bf16[32,640]{1,0:T(8,128)(2,1)S(1)} collective-permute-done((bf16[32,640]{1,0:T(8,128)(2,1)}, bf16[32,640]{1,0:T(8,128)(2,1)S(1)}, u32[]{:S(2)}, u32[]{:S(2)}) %collective-permute-start.59) | collective-permute-done | bytes 40992 | tf_op jit(solution)/shard_map/ppermute | solution.py:70
  (539 shorter events, 305.2 us)
Async XLA Ops:
  7.2 103.8 %all-gather.3.cloned.1.call-start = ((), (), s32[]{:S(2)}) async-start(), calls=%async_computation.2 | async-start | bytes 8921088 | tf_op jit(solution)/shard_map/all_gather | solution.py:975
  12.3 180.3 %all-gather.5.cloned.1.call-start = ((), (), s32[]{:S(2)}) async-start(), calls=%async_computation.3 | async-start | bytes 8650752 | tf_op jit(solution)/shard_map/all_gather | solution.py:982
  13.0 547.4 %reduce-scatter.2.cloned.1.call-start = ((), (), s32[]{:S(2)}) async-start(), calls=%async_computation.4 | async-start | bytes 8650752 | tf_op jit(solution)/shard_map/reduce_scatter | solution.py:1077
  61.4 25.6 %collective-permute-start.8 = (bf16[2,2,2,48,1024]{4,3,2,1,0:T(8,128)(2,1)S(1)}, bf16[2,2,2,48,1024]{4,3,2,1,0:T(8,128)(2,1)S(1)}, u32[]{:S(2)}, u32[]{:S(2)}) collective-permute-start(bf16[2,2,2,48,1024]{4,3,2,1,0:T(8,128)(2,1)S(1)} %broadcast_select_fusion.6), channel_id=1, source_target_pairs={{0,1},{1,0},{2,3},{3,2},{4,5},{5,4},{6,7},{7,6},{8,9},{9,8},{10,11... | collective-permute-start | bytes 2359304 | tf_op jit(solution)/shard_map/ppermute | solution.py:70
  132.1 26.2 %collective-permute-start.16 = (bf16[512,256]{1,0:T(8,128)(2,1)S(1)}, bf16[512,256]{1,0:T(8,128)(2,1)S(1)}, u32[]{:S(2)}, u32[]{:S(2)}) collective-permute-start(bf16[512,256]{1,0:T(8,128)(2,1)S(1)} %get-tuple-element.238), channel_id=1, source_target_pairs={{0,1},{2,3},{4,5},{6,7},{8,9},{10,11},{12,13},{14,15},{16,17},{18,... | collective-permute-start | bytes 786440 | tf_op jit(solution)/shard_map/ppermute | solution.py:920
  133.6 43.7 %collective-permute-start.15 = (bf16[2,2,2,64,1024]{4,3,2,1,0:T(8,128)(2,1)S(1)}, bf16[2,2,2,64,1024]{4,3,2,1,0:T(8,128)(2,1)S(1)}, u32[]{:S(2)}, u32[]{:S(2)}) collective-permute-start(bf16[2,2,2,64,1024]{4,3,2,1,0:T(8,128)(2,1)S(1)} %copy-done.41), channel_id=1, source_target_pairs={{0,4},{2,6},{4,0},{6,2},{8,12},{10,14},{12,8},{14,10},{16,20},{18,... | collective-permute-start | bytes 3145736 | tf_op jit(solution)/shard_map/ppermute | solution.py:70
  263.7 45.0 %collective-permute-start.20 = (bf16[2,2,2,2,48,1024]{5,4,0,1,3,2:T(8,128)(2,1)}, bf16[2,2,2,2,48,1024]{5,4,0,1,3,2:T(8,128)(2,1)}, u32[]{:S(2)}, u32[]{:S(2)}) collective-permute-start(bf16[2,2,2,2,48,1024]{5,4,0,1,3,2:T(8,128)(2,1)} %copy_bitcast_fusion.2), channel_id=1, source_target_pairs={{0,2},{2,0},{4,6},{6,4},{8,10},{10,8},{12,14},{14,12},{16,18},{18,... | collective-permute-start | bytes 4718600 | tf_op jit(solution)/shard_map/ppermute | solution.py:70
  264.0 42.1 %collective-permute-start.19 = (bf16[2,2,2,64,1024]{4,3,0,1,2:T(8,128)(2,1)}, bf16[2,2,2,64,1024]{4,3,0,1,2:T(8,128)(2,1)}, u32[]{:S(2)}, u32[]{:S(2)}) collective-permute-start(bf16[2,2,2,64,1024]{4,3,0,1,2:T(8,128)(2,1)} %dynamic-slice_bitcast_fusion), channel_id=1, source_target_pairs={{0,1},{1,0},{2,3},{3,2},{4,5},{5,4},{6,7},{7,6},{8,9},{9,8},{10,11... | collective-permute-start | bytes 3145736 | tf_op jit(solution)/shard_map/ppermute | solution.py:70
  270.5 33.4 %collective-permute-start.21 = (bf16[2,2,2,2,16,1024]{5,4,0,1,2,3:T(8,128)(2,1)}, bf16[2,2,2,2,16,1024]{5,4,0,1,2,3:T(8,128)(2,1)}, u32[]{:S(2)}, u32[]{:S(2)}) collective-permute-start(bf16[2,2,2,2,16,1024]{5,4,0,1,2,3:T(8,128)(2,1)} %copy_bitcast_fusion.7), channel_id=1, source_target_pairs={{0,2},{2,0},{4,6},{6,4},{8,10},{10,8},{12,14},{14,12},{16,18},{18,... | collective-permute-start | bytes 1572872 | tf_op jit(solution)/shard_map/ppermute | solution.py:70
  279.8 23.0 %collective-permute-start.22 = (bf16[128,1536]{1,0:T(8,128)(2,1)}, bf16[128,1536]{1,0:T(8,128)(2,1)}, u32[]{:S(2)}, u32[]{:S(2)}) collective-permute-start(bf16[128,1536]{1,0:T(8,128)(2,1)} %convert_element_type.680), channel_id=1, source_target_pairs={{1,0},{3,2},{5,4},{7,6},{9,8},{11,10},{13,12},{15,14},{17,16},{19,... | collective-permute-start | bytes 1179656 | tf_op jit(solution)/shard_map/ppermute | solution.py:207
  315.0 36.8 %collective-permute-start.23 = (bf16[2,2,64,1024]{3,2,0,1:T(8,128)(2,1)}, bf16[2,2,64,1024]{3,2,0,1:T(8,128)(2,1)}, u32[]{:S(2)}, u32[]{:S(2)}) collective-permute-start(bf16[2,2,64,1024]{3,2,0,1:T(8,128)(2,1)} %dynamic-slice_bitcast_fusion.3), channel_id=1, source_target_pairs={{0,4},{2,6},{4,0},{6,2},{8,12},{10,14},{12,8},{14,10},{16,20},{18,... | collective-permute-start | bytes 1572872 | tf_op jit(solution)/shard_map/ppermute | solution.py:70
  317.2 33.7 %collective-permute-start.24 = (bf16[2,2,2,16,1024]{4,3,0,1,2:T(8,128)(2,1)}, bf16[2,2,2,16,1024]{4,3,0,1,2:T(8,128)(2,1)S(1)}, u32[]{:S(2)}, u32[]{:S(2)}) collective-permute-start(bf16[2,2,2,16,1024]{4,3,0,1,2:T(8,128)(2,1)} %dynamic-slice_bitcast_fusion.11), channel_id=1, source_target_pairs={{0,1},{1,0},{2,3},{3,2},{4,5},{5,4},{6,7},{7,6},{8,9},{9,8},{10,11... | collective-permute-start | bytes 786440 | tf_op jit(solution)/shard_map/ppermute | solution.py:70
  317.2 36.6 %collective-permute-start.25 = (bf16[2,2,2,48,1024]{4,3,0,1,2:T(8,128)(2,1)}, bf16[2,2,2,48,1024]{4,3,0,1,2:T(8,128)(2,1)S(1)}, u32[]{:S(2)}, u32[]{:S(2)}) collective-permute-start(bf16[2,2,2,48,1024]{4,3,0,1,2:T(8,128)(2,1)} %dynamic-slice_bitcast_fusion.2), channel_id=1, source_target_pairs={{0,4},{2,6},{4,0},{6,2},{8,12},{10,14},{12,8},{14,10},{16,20},{18,... | collective-permute-start | bytes 2359304 | tf_op jit(solution)/shard_map/ppermute | solution.py:70
  317.3 37.6 %collective-permute-start.26 = (bf16[2,2,2,2,32,1536]{5,4,0,1,3,2:T(8,128)(2,1)}, bf16[2,2,2,2,32,1536]{5,4,0,1,3,2:T(8,128)(2,1)}, u32[]{:S(2)}, u32[]{:S(2)}) collective-permute-start(bf16[2,2,2,2,32,1536]{5,4,0,1,3,2:T(8,128)(2,1)} %copy_bitcast_fusion.1), channel_id=1, source_target_pairs={{0,2},{2,0},{4,6},{6,4},{8,10},{10,8},{12,14},{14,12},{16,18},{18,... | collective-permute-start | bytes 4718600 | tf_op jit(solution)/shard_map/ppermute | solution.py:70
  378.5 28.9 %collective-permute-start.33 = (bf16[2,2,48,1024]{3,2,0,1:T(8,128)(2,1)}, bf16[2,2,48,1024]{3,2,0,1:T(8,128)(2,1)}, u32[]{:S(2)}, u32[]{:S(2)}) collective-permute-start(bf16[2,2,48,1024]{3,2,0,1:T(8,128)(2,1)} %dynamic-slice_bitcast_fusion.6), channel_id=1, source_target_pairs={{0,1},{1,0},{2,3},{3,2},{4,5},{5,4},{6,7},{7,6},{8,9},{9,8},{10,11... | collective-permute-start | bytes 1179656 | tf_op jit(solution)/shard_map/ppermute | solution.py:70
  381.8 28.0 %collective-permute-start.34 = (bf16[2,2,2,32,1536]{4,3,0,1,2:T(8,128)(2,1)}, bf16[2,2,2,32,1536]{4,3,0,1,2:T(8,128)(2,1)}, u32[]{:S(2)}, u32[]{:S(2)}) collective-permute-start(bf16[2,2,2,32,1536]{4,3,0,1,2:T(8,128)(2,1)} %dynamic-slice_bitcast_fusion.1), channel_id=1, source_target_pairs={{0,4},{2,6},{4,0},{6,2},{8,12},{10,14},{12,8},{14,10},{16,20},{18,... | collective-permute-start | bytes 2359304 | tf_op jit(solution)/shard_map/ppermute | solution.py:70
  419.0 29.0 %collective-permute-start.35 = (bf16[2,2,2,32,640]{4,3,0,1,2:T(8,128)(2,1)S(1)}, bf16[2,2,2,32,640]{4,3,0,1,2:T(8,128)(2,1)S(1)}, u32[]{:S(2)}, u32[]{:S(2)}) collective-permute-start(bf16[2,2,2,32,640]{4,3,0,1,2:T(8,128)(2,1)S(1)} %dynamic-slice_bitcast_fusion.8), channel_id=1, source_target_pairs={{0,4},{2,6},{4,0},{6,2},{8,12},{10,14},{12,8},{14,10},{16,20},{18,... | collective-permute-start | bytes 983048 | tf_op jit(solution)/shard_map/ppermute | solution.py:70
  419.0 29.1 %collective-permute-start.36 = (bf16[2,2,2,32,640]{4,3,0,1,2:T(8,128)(2,1)S(1)}, bf16[2,2,2,32,640]{4,3,0,1,2:T(8,128)(2,1)S(1)}, u32[]{:S(2)}, u32[]{:S(2)}) collective-permute-start(bf16[2,2,2,32,640]{4,3,0,1,2:T(8,128)(2,1)S(1)} %dynamic-slice_bitcast_fusion.7), channel_id=1, source_target_pairs={{0,1},{1,0},{2,3},{3,2},{4,5},{5,4},{6,7},{7,6},{8,9},{9,8},{10,11... | collective-permute-start | bytes 983048 | tf_op jit(solution)/shard_map/ppermute | solution.py:70
  420.3 27.6 %collective-permute-start.37 = (bf16[2,2,2,32,512]{4,3,0,1,2:T(8,128)(2,1)S(1)}, bf16[2,2,2,32,512]{4,3,0,1,2:T(8,128)(2,1)S(1)}, u32[]{:S(2)}, u32[]{:S(2)}) collective-permute-start(bf16[2,2,2,32,512]{4,3,0,1,2:T(8,128)(2,1)S(1)} %dynamic-slice_bitcast_fusion.9), channel_id=1, source_target_pairs={{0,1},{1,0},{2,3},{3,2},{4,5},{5,4},{6,7},{7,6},{8,9},{9,8},{10,11... | collective-permute-start | bytes 786440 | tf_op jit(solution)/shard_map/ppermute | solution.py:70
  421.0 43.5 %collective-permute-start.39 = (bf16[2,2,32,1536]{3,2,0,1:T(8,128)(2,1)S(1)}, bf16[2,2,32,1536]{3,2,0,1:T(8,128)(2,1)S(1)}, u32[]{:S(2)}, u32[]{:S(2)}) collective-permute-start(bf16[2,2,32,1536]{3,2,0,1:T(8,128)(2,1)S(1)} %dynamic-slice_bitcast_fusion.5), channel_id=1, source_target_pairs={{0,1},{1,0},{2,3},{3,2},{4,5},{5,4},{6,7},{7,6},{8,9},{9,8},{10,11... | collective-permute-start | bytes 1179656 | tf_op jit(solution)/shard_map/ppermute | solution.py:70
  465.6 23.5 %collective-permute-start.43 = (bf16[512,256]{1,0:T(8,128)(2,1)S(1)}, bf16[512,256]{1,0:T(8,128)(2,1)S(1)}, u32[]{:S(2)}, u32[]{:S(2)}) collective-permute-start(bf16[512,256]{1,0:T(8,128)(2,1)S(1)} %slice.208), channel_id=1, source_target_pairs={{1,0},{3,2},{5,4},{7,6},{9,8},{11,10},{13,12},{15,14},{17,16},{19,... | collective-permute-start | bytes 786440 | tf_op jit(solution)/shard_map/ppermute | solution.py:931
  467.1 21.7 %collective-permute-start.44 = (bf16[2,2,32,640]{3,2,0,1:T(8,128)(2,1)S(1)}, bf16[2,2,32,640]{3,2,0,1:T(8,128)(2,1)S(1)}, u32[]{:S(2)}, u32[]{:S(2)}) collective-permute-start(bf16[2,2,32,640]{3,2,0,1:T(8,128)(2,1)S(1)} %dynamic-slice_bitcast_fusion.16), channel_id=1, source_target_pairs={{0,1},{1,0},{2,3},{3,2},{4,5},{5,4},{6,7},{7,6},{8,9},{9,8},{10,11... | collective-permute-start | bytes 491528 | tf_op jit(solution)/shard_map/ppermute | solution.py:70
  491.1 22.4 %collective-permute-start.51 = (bf16[32,1536]{1,0:T(8,128)(2,1)S(1)}, bf16[32,1536]{1,0:T(8,128)(2,1)S(1)}, u32[]{:S(2)}, u32[]{:S(2)}) collective-permute-start(bf16[32,1536]{1,0:T(8,128)(2,1)S(1)} %dynamic-slice_bitcast_fusion.21), channel_id=1, source_target_pairs={{0,16},{2,18},{4,20},{6,22},{8,24},{10,26},{12,28},{14,30},{16,0},... | collective-permute-start | bytes 294920 | tf_op jit(solution)/shard_map/ppermute | solution.py:70
  521.7 27.1 %all-to-all-start = ((bf16[32,32,128]{2,1,0:T(8,128)(2,1)}), bf16[32,32,128]{2,1,0:T(8,128)(2,1)S(1)}, u32[]{:S(2)}, u32[]{:S(2)}) async-start(bf16[32,32,128]{2,1,0:T(8,128)(2,1)} %concatenate.65), calls=%async_computation | async-start | bytes 524288 | tf_op jit(solution)/shard_map/all_to_all | solution.py:1153
  (133 other events, 1424.4 us)
Sparse Core Ops, SparseCore 0:
  12.4 93.6 all-gather.2
  109.1 83.4 all-gather.4
  290.4 236.4 reduce-scatter.1

commit v3 on v2

--- a/solution.py
+++ b/solution.py
@@ -183,7 +183,7 @@
     count = lax.axis_size("seq")
     low = part.astype(BF16)
     if count == 2:
-        return lax.ppermute(low, "seq", [(0, 1)]).astype(F32)
+        return lax.ppermute(low, "seq", [(0, 1)])
     gates = lax.all_gather(gate.astype(BF16), "seq")
     parts = lax.all_gather(low, "seq")
     start = (jnp.ones_like(gate), jnp.zeros_like(part))
@@ -204,7 +204,7 @@
     count = lax.axis_size("seq")
     low = part.astype(BF16)
     if count == 2:
-        return lax.ppermute(low, "seq", [(1, 0)]).astype(F32)
+        return lax.ppermute(low, "seq", [(1, 0)])
     gates = lax.all_gather(gate.astype(BF16), "seq")
     parts = lax.all_gather(low, "seq")
     start = (jnp.ones_like(gate), jnp.zeros_like(part))
@@ -352,6 +352,13 @@
 
 def ssd_gate_kernel(dym_ref, y_ref, x_ref, z_ref, c_ref, vec_ref, dy_ref, dz_ref, ds_ref, skip_ref):
     length = x_ref.shape[0]
+    spot = lax.broadcasted_iota(jnp.int32, (128, 128), 0) // MHDIM
+    place = lax.broadcasted_iota(jnp.int32, (128, 128), 1)
+
+    @pl.when(pl.program_id(0) == 0)
+    def _():
+        skip_ref[...] = jnp.zeros_like(skip_ref)
+
     wide = lane_is_low(length)
     ent = group_columns(vec_ref, 3)
     c_low = c_ref[...].astype(BF16)
@@ -363,13 +370,17 @@
         dy_ref[:, lanes] = dy
         dz_ref[:, lanes] = (dym * y_ref[:, lanes] * slope).astype(BF16)
         ds_ref[:, lanes] = dot_tn(c_low, (dy * spread(wide, ent, 2 * pair)).astype(BF16))
-        skip_ref[:, lanes] = jnp.sum(dy * x_ref[:, lanes], axis=0, keepdims=True)
+        total = jnp.broadcast_to(jnp.sum(dy * x_ref[:, lanes], axis=0, keepdims=True), (8, 128))
+        pick = (place == pl.program_id(0) * GHEADS + 2 * pair + spot).astype(BF16)
+        high = total.astype(BF16)
+        rest = (total - high.astype(F32)).astype(BF16)
+        skip_ref[...] += dot_nn(high, pick) + dot_nn(rest, pick)
 
 
 def ssd_gate(dym, y, x, z, c, vec):
     length = x.shape[0]
     x_spec, s_spec, n_spec, b_spec, c_spec, v_spec, _ = group_specs(length)
-    one_spec = pl.BlockSpec((1, GLANES), lambda g: (0, g))
+    one_spec = pl.BlockSpec((8, 128), lambda g: (0, 0))
     return pl.pallas_call(
         ssd_gate_kernel,
         grid=(GROUPS,),
@@ -379,7 +390,7 @@
             jax.ShapeDtypeStruct((length, INNER), F32),
             jax.ShapeDtypeStruct((length, INNER), BF16),
             jax.ShapeDtypeStruct((STATE, INNER), F32),
-            jax.ShapeDtypeStruct((1, INNER), F32),
+            jax.ShapeDtypeStruct((8, 128), F32),
         ],
         compiler_params=PARAMS,
         cost_estimate=SHORT,
@@ -438,6 +449,8 @@
             xd = xd_ref[first : first + STRIP, :]
             dys = dy_low[first:]
             halves = []
+            dgs = []
+            gones = []
             for half in range(2):
                 head = 2 * pair + half
                 mine = narrow if half == 0 else ~narrow
@@ -447,12 +460,15 @@
                 m = (decay * bc).astype(BF16)
                 halves.append(dot_nn(m, dys))
                 dg = decay * dot_nt(jnp.where(mine, xd, jnp.zeros_like(xd)), dys)
-                dbc_ref[first : first + STRIP, first:] += dg
+                dgs.append(dg)
                 e = dg * bc
                 rows_ref[head : head + 1, first:] += jnp.sum(e, axis=0, keepdims=True)
-                gone = jnp.sum(e, axis=1, keepdims=True)
-                at = group * GHEADS + head
-                cols_ref[3, first : first + STRIP, :] += jnp.where(lane == at, gone, 0.0)
+                gones.append(jnp.sum(e, axis=1, keepdims=True))
+            dbc_ref[first : first + STRIP, first:] += dgs[0] + dgs[1]
+            at = group * GHEADS + 2 * pair
+            cols_ref[3, first : first + STRIP, :] += jnp.where(
+                lane == at, gones[0], jnp.where(lane == at + 1, gones[1], 0.0)
+            )
             dxd = jnp.where(narrow, halves[0], halves[1]) + carried[first : first + STRIP]
             sum_ref[first : first + STRIP, :] = dxd
         dxd = sum_ref[...]
@@ -467,7 +483,7 @@
         cols_ref[0] += per_head(dxd * x)
         cols_ref[1] += per_head(dtx * x * carried)
         cols_ref[2] += per_head(dy * entered)
-        passed = jnp.sum(st_ref[:, lanes] * dst_ref[:, lanes], axis=0, keepdims=True) * entx[length - 1 :]
+        passed = jnp.sum(st_ref[:, lanes].astype(F32) * dst_ref[:, lanes].astype(F32), axis=0, keepdims=True) * entx[length - 1 :]
         cols_ref[2, length - 8 :, :] += jnp.where(
             lax.broadcasted_iota(jnp.int32, (8, 128), 0) == 7, per_head(jnp.broadcast_to(passed, (8, 128))), 0.0
         )
@@ -678,7 +694,7 @@
     )(before, raw, heads, seg_col)
 
 
-def heads_backward_kernel(raw_ref, heads_ref, cols_ref, rows_ref, low_ref, sums_ref):
+def heads_backward_kernel(raw_ref, heads_ref, cols_ref, rows_ref, skip_ref, low_ref, sums_ref):
     length = raw_ref.shape[0]
     shifted, _, rate, log_decay = head_values(raw_ref, heads_ref)
     filler = jnp.zeros((128 - MHEADS, length), F32)
@@ -695,13 +711,14 @@
         [
             jnp.sum(ddelta, axis=0, keepdims=True),
             jnp.sum(da * log_decay, axis=0, keepdims=True),
-            jnp.zeros((6, 128), F32),
+            skip_ref[0:1, :],
+            jnp.zeros((5, 128), F32),
         ],
         axis=0,
     )
 
 
-def heads_backward(raw, heads, cols, rows):
+def heads_backward(raw, heads, cols, rows, skip):
     length = raw.shape[0]
     return pl.pallas_call(
         heads_backward_kernel,
@@ -712,7 +729,7 @@
         compiler_params=PARAMS,
         cost_estimate=SHORT,
         name="heads_backward",
-    )(raw, heads, cols, rows)
+    )(raw, heads, cols, rows, skip)
 
 
 def turn(value, cosine, sine):
@@ -785,7 +802,7 @@
     acc_ref[...] = jnp.zeros_like(acc_ref)
     narrow = lane_is_low(STRIP)
 
-    def block(step, carry):
+    def block(step, carry, diagonal=False):
         at = rank - step
         t = lax.broadcasted_iota(jnp.int32, (length, length), 0) + rank * length
         s = lax.broadcasted_iota(jnp.int32, (length, length), 1) + at * length
@@ -800,8 +817,9 @@
             values = v_ref[kv_head, pl.ds(start, length), :]
             for strip in range(length // STRIP):
                 rows = slice(strip * STRIP, (strip + 1) * STRIP)
+                width = (strip + 1) * STRIP if diagonal else length
                 q = q_ref[rows, lanes]
-                scores = dot_nt(jnp.where(mine, q, jnp.zeros_like(q)), keys) + mask_ref[rows, :]
+                scores = dot_nt(jnp.where(mine, q, jnp.zeros_like(q)), keys[:width]) + mask_ref[rows, :width]
                 old = top_ref[head, rows, :]
                 new = jnp.maximum(old, jnp.max(scores, axis=1, keepdims=True))
                 fade = jnp.exp(old - new)
@@ -809,10 +827,11 @@
                 sum_ref[head, rows, :] = sum_ref[head, rows, :] * fade + jnp.sum(probs, axis=1, keepdims=True)
                 top_ref[head, rows, :] = new
                 acc = acc_ref[rows, lanes]
-                acc_ref[rows, lanes] = jnp.where(mine, acc * fade + dot_nn(probs.astype(BF16), values), acc)
+                acc_ref[rows, lanes] = jnp.where(mine, acc * fade + dot_nn(probs.astype(BF16), values[:width]), acc)
         return carry
 
-    lax.fori_loop(0, rank + 1, block, 0)
+    block(0, 0, diagonal=True)
+    lax.fori_loop(1, rank + 1, block, 0)
     lane = lax.broadcasted_iota(jnp.int32, (length, 128), 1)
     stats = jnp.zeros((length, 128), F32)
     low = lane_is_low(length)
@@ -821,7 +840,7 @@
         o_ref[:, lanes] = acc_ref[:, lanes] / jnp.where(low, sum_ref[2 * pair], sum_ref[2 * pair + 1])
     for head in range(AHEADS):
         stats = jnp.where(lane == head, top_ref[head] + jnp.log(sum_ref[head]), stats)
-    lse_ref[...] = stats
+    lse_ref[...] = stats.T
 
 
 def attend(rank, q, keyvals, seg_col, seg_blocks):
@@ -833,7 +852,7 @@
         out_specs=[vmem, vmem],
         out_shape=[
             jax.ShapeDtypeStruct((length, QWIDTH), F32),
-            jax.ShapeDtypeStruct((length, 128), F32),
+            jax.ShapeDtypeStruct((128, length), F32),
         ],
         scratch_shapes=[
             pltpu.VMEM((AHEADS, length, 128), F32),
@@ -1096,9 +1115,8 @@
         u, dy, u, u, state_in, dstate, vec, row, seg_row.T, seg_row, skip_lanes
     )
     cols, rows_sum, dx = step((cols, rows_sum, dx), sum_down, sum_ao, sum_mo, sum_z)
-    ddelta_low, head_sums = heads_backward(delta_raw, heads, cols, rows_sum)
-    grad_skip = jnp.sum(skip_cols.reshape(MHEADS, MHDIM), axis=1)
-    sum_heads = Summing(jnp.concatenate([head_sums[0, :MHEADS], head_sums[1, :MHEADS], grad_skip]))
+    ddelta_low, head_sums = heads_backward(delta_raw, heads, cols, rows_sum, skip_cols)
+    sum_heads = Summing(head_sums)
 
     dxbc, last_rows, spilled, conv_grads = conv_backward(dx, db, dc, xbc, halo, kernel_wide, taps_wide, taps_count)
     incoming = jnp.pad(neighbour(spilled[8 - back :], -1), ((8 - back, 0), (0, 0)))
@@ -1118,7 +1136,7 @@
     )
     do, delta = step((do, delta), *sum_x, sum_mo, sum_z)
     dq, dkv = attend_backward(
-        rank_arg, q, all_keyvals, do, lse[:, :AHEADS].T, delta, seg_row, seg_full[:, None]
+        rank_arg, q, all_keyvals, do, lse, delta, seg_row, seg_full[:, None]
     )
     dq, dkv = step((dq, dkv), *sum_x, sum_heads, sum_z, sum_mo, sum_ao, sum_down)
     own_dkv, more_dkv = scatter_keyval_grads(dkv, length)
@@ -1168,9 +1186,9 @@
         grad_small[:, :MHEADS],
         kernel_own,
         shift_own,
-        head_grads[:MHEADS],
-        head_grads[MHEADS : 2 * MHEADS],
-        head_grads[2 * MHEADS :],
+        head_grads[0, :MHEADS],
+        head_grads[1, :MHEADS],
+        head_grads[2, :MHEADS],
         sum_mo.value,
         sum_qkv.value,
         sum_ao.value,

time: 578 us -> 568 us (0.983)
  waiting for transfers between devices: 146 us -> 138 us
    ppermute x2, waiting for transfers between devices: 11.2 us -> 0.49 us  [the longest x1 0.49 us: state_from_behind(): return lax.ppermute(low, 'seq', [(0, 1)])]
    ppermute x60, waiting for transfers between devices: 126 us -> 136 us  [swap(): return lax.ppermute(value, axis, [(i, i ^ level) for i in range(size)])]
    all_gather x1, waiting for transfers between devices: 7.95 us -> 0.61 us  [on_device(): gate_up = lax.all_gather(w_gate_up, ('dp', 'seq'), axis=0, tiled=True)]
    pallas_call x1, Pallas kernels: 6.88 us -> 13.9 us  [ssd_finish(): pl.pallas_call(ssd_finish_kernel, grid=(GROUPS,), in_specs=[x_spec, x_spe...]
    unnamed x177 -> x163, local copies, waits for them, and re-layouts: 13.2 us -> 15.8 us
  transfers between devices with their start and end apart: 70 -> 70, of which waited for: 23 -> 25; matrix products, arithmetic and copies ran while one was open for 25% -> 24% of each run, Pallas kernels for 17% -> 18%
where the time goes in v3:
time: 568 us; the launch traced here: 560 us
  waiting for transfers between devices  138 us (24%)
  Pallas kernels  101 us (18%)
  starting transfers between devices  95.8 us (17%)
  matrix products  83.1 us (15%)
  other arithmetic  70.9 us (12%)
  local copies, waits for them, and re-layouts  55.2 us (10%)
  between operations  16.1 us (3%)
    ppermute x60, waiting for transfers between devices, swap(): return lax.ppermute(value, axis, [(i, i ^ level) for i in range(size)])  136 us
    ppermute x60, starting transfers between devices, swap(): return lax.ppermute(value, axis, [(i, i ^ level) for i in range(size)])  81.4 us
    dot_general x7, matrix products, dot_nt(): lax.dot_general(a, b, (((1,), (1,)), ((), ())), preferred_element_type=F32)  33.3 us
    dot_general x7, matrix products, dot_nn(): lax.dot_general(a, b, (((1,), (0,)), ((), ())), preferred_element_type=F32)  29.4 us
    pallas_call x1, Pallas kernels, ssd_backward(): pl.pallas_call(ssd_backward_kernel, grid=(GROUPS,), in_specs=[x_spec, x_s...  28.7 us
    select_n x15, other arithmetic, prepare(): jnp.where(own, jnp.expand_dims(self.value, place), jnp.expand_dims(self.g...  22.1 us
    dot_general x10, matrix products, dot_tn(): lax.dot_general(a, b, (((0,), (0,)), ((), ())), preferred_element_type=F32)  19.7 us
    convert_element_type x32, other arithmetic, prepare(): self.value = value.astype(BF16) if self.left else value  19.3 us
  transfers between devices with their start and end apart: 70, of which 25 were waited for; matrix products, arithmetic and copies ran while one was open for 24% of the time, Pallas kernels for 18%

profile of v3, /device:TPU:0, one launch (start us, length us, event | category | flops | bytes accessed | tf_op | source)
XLA Modules:
  0.0 559.9 jit_solution(15401543263854078135)
XLA Ops:
  20.2 7.2 %collective-permute-done.1 = bf16[16,1024]{1,0:T(8,128)(2,1)S(1)} collective-permute-done((bf16[16,1024]{1,0:T(8,128)(2,1)}, bf16[16,1024]{1,0:T(8,128)(2,1)S(1)}, u32[]{:S(2)}, u32[]{:S(2)}) %collective-permute-start.1) | collective-permute-done | bytes 32800 | tf_op jit(solution)/shard_map/ppermute | solution.py:70
  43.6 8.6 %collective-permute-done.5 = bf16[2,64,1024]{2,1,0:T(8,128)(2,1)S(1)} collective-permute-done((bf16[2,64,1024]{2,1,0:T(8,128)(2,1)S(1)}, bf16[2,64,1024]{2,1,0:T(8,128)(2,1)S(1)}, u32[]{:S(2)}, u32[]{:S(2)}) %collective-permute-start.5) | collective-permute-done | bytes 262176 | tf_op jit(solution)/shard_map/ppermute | solution.py:70
  71.2 15.7 %collective-permute-done.8 = bf16[2,2,2,48,1024]{4,3,2,1,0:T(8,128)(2,1)S(1)} collective-permute-done((bf16[2,2,2,48,1024]{4,3,2,1,0:T(8,128)(2,1)S(1)}, bf16[2,2,2,48,1024]{4,3,2,1,0:T(8,128)(2,1)S(1)}, u32[]{:S(2)}, u32[]{:S(2)}) %collective-permute-start.8) | collective-permute-done | bytes 786464 | tf_op jit(solution)/shard_map/ppermute | solution.py:70
  94.7 9.0 %collective-permute-done.12 = bf16[2,2,64,1024]{3,2,1,0:T(8,128)(2,1)S(1)} collective-permute-done((bf16[2,2,64,1024]{3,2,1,0:T(8,128)(2,1)S(1)}, bf16[2,2,64,1024]{3,2,1,0:T(8,128)(2,1)S(1)}, u32[]{:S(2)}, u32[]{:S(2)}) %collective-permute-start.12) | collective-permute-done | bytes 524320 | tf_op jit(solution)/shard_map/ppermute | solution.py:70
  144.3 9.5 %ssd_forward.1 = (f32[512,1536]{1,0:T(8,128)S(1)}, f32[128,1536]{1,0:T(8,128)S(1)}) custom-call(f32[512,1792]{1,0:T(8,128)} %copy-done, f32[512,1792]{1,0:T(8,128)} %copy-done, f32[512,1792]{1,0:T(8,128)} %copy-done, f32[4,512,128]{2,1,0:T(8,128)S(1)} %get-tuple-element.228.vec_ref, f32[128,512]{1,0:T(8,128)S(1)} %get-tuple-element.229.row_ref, ...), custom_call_target="tpu_custom_call" | custom-call | tf_op jit(solution)/shard_map/ssd_forward/pallas_call | solution.py:296
  160.8 9.8 %attend.1 = (f32[512,512]{1,0:T(8,128)S(1)}, f32[128,512]{1,0:T(8,128)S(1)}) custom-call(s32[1]{0:T(128)} %bitcast.13.rank_ref, bf16[512,512]{1,0:T(8,128)(2,1)S(1)} %get-tuple-element.237.q_ref, bf16[1024,256]{1,0:T(8,128)(2,1)S(1)} %pad_maximum_fusion.1.kv_ref, s32[512,1]{1,0:T(8,128)S(1)} %copy.180.seg_ref.segc_ref.segq_ref, ...), custom_call_target="tpu_custom_call" | custom-call | tf_op jit(solution)/shard_map/attend/pallas_call | solution.py:849
  171.1 13.9 %ssd_finish.1 = (f32[512,1536]{1,0:T(8,128)}, bf16[512,1536]{1,0:T(8,128)(2,1)S(1)}) custom-call(f32[512,1536]{1,0:T(8,128)} %copy-done.6, f32[512,1792]{1,0:T(8,128)} %copy-done, bf16[512,1536]{1,0:T(8,128)(2,1)S(1)} %convolution_convert_fusion.4.z_ref, f32[512,1792]{1,0:T(8,128)} %copy-done, bf16[128,1536]{1,0:T(8,128)(2,1)S(1)} %collective-permute-done.14.st_ref, ...), custom_call_target="tpu_custom_call" | custom-call | tf_op jit(solution)/shard_map/ssd_finish/pallas_call | solution.py:338
  192.8 7.7 %fusion.95 = f32[512,4096]{1,0:T(8,128)S(1)} fusion(bf16[1024,4096]{1,0:T(8,128)(2,1)} %all-gather.5.cloned.1.call-done, f32[512,1024]{1,0:T(8,128)} %get-tuple-element.467, f32[1024]{0:T(1024)S(1)} %copy-done.70, f32[512]{0:T(512)S(1)} %get-tuple-element.465), kind=kOutput, calls=%fused_computation.273 | convolution fusion | flops 4296540160 | bytes 18880512 | tf_op jit(solution)/shard_map/dot_general | solution.py:37
  200.5 7.7 %broadcast_select_fusion = bf16[2,2,2,2,2,64,1024]{6,5,4,3,2,1,0:T(8,128)(2,1)} fusion(pred[2]{0:T(512)(128)(4,1)S(1)} %copy-done.75, bf16[2,2,2,2,64,1024]{5,4,3,2,1,0:T(8,128)(2,1)} %collective-permute-done.17, bf16[2,2,2,2,64,1024]{5,4,3,2,1,0:T(8,128)(2,1)} %broadcast_select_fusion.2), kind=kLoop, calls=%fused_computation.15 | loop fusion | flops 2097152 | bytes 8388610 | tf_op jit(solution)/shard_map/jit(_where)/select_n | solution.py:127
  214.8 6.9 %add_convert_fusion = bf16[512,1024]{1,0:T(8,128)(2,1)} fusion(f32[512,1024]{1,0:T(8,128)} %get-tuple-element.467, bf16[512,2048]{1,0:T(8,128)(2,1)} %copy-done.57, bf16[2048,1024]{1,0:T(8,128)(2,1)} %bitcast.292), kind=kOutput, calls=%fused_computation.50 | convolution fusion | flops 2148532224 | bytes 9437184 | tf_op jit(solution)/shard_map/dot_general | solution.py:37
  233.6 7.2 %convolution_convert_fusion = bf16[1024,4096]{1,0:T(8,128)(2,1)} fusion(f32[512,1024]{1,0:T(8,128)S(1)} %copy-done.37, f32[1024]{0:T(1024)S(1)} %copy-done.70, f32[512]{0:T(512)S(1)} %get-tuple-element.465, bf16[512,2048]{1,0:T(8,128)(2,1)S(1)} %get-tuple-element.451, bf16[512,2048]{1,0:T(8,128)(2,1)S(1)} %get-tuple-element.450), kind=kOutput, calls=%fused_computation | convolution fusion | flops 4309123072 | bytes 14686208 | tf_op jit(solution)/shard_map/dot_general | solution.py:45
  240.8 10.1 %multiply_reduce_fusion = (bf16[1024]{0:T(1024)(128)(2,1)S(1)}, f32[512]{0:T(512)S(1)}, f32[512,1024]{1,0:T(8,128)S(1)}) fusion(f32[512,1024]{1,0:T(8,128)} %get-tuple-element.467, f32[512]{0:T(512)S(1)} %get-tuple-element.465, f32[1024]{0:T(1024)S(1)} %copy-done.70, bf16[512,4096]{1,0:T(8,128)(2,1)} %pad_maximum_fusion, ...), kind=kOutput, calls=%fused_computation.46 | convolution fusion | flops 4298111488 | bytes 16787456 | tf_op jit(solution)/shard_map/dot_general | solution.py:41
  264.1 6.7 %collective-permute-start.19 = (bf16[2,2,2,64,1024]{4,3,0,1,2:T(8,128)(2,1)}, bf16[2,2,2,64,1024]{4,3,0,1,2:T(8,128)(2,1)}, u32[]{:S(2)}, u32[]{:S(2)}) collective-permute-start(bf16[2,2,2,64,1024]{4,3,0,1,2:T(8,128)(2,1)} %dynamic-slice_bitcast_fusion), channel_id=1, source_target_pairs={{0,1},{1,0},{2,3},{3,2},{4,5},{5,4},{6,7},{7,6},{8,9},{9,8},{10,11... | collective-permute-start | bytes 3145736 | tf_op jit(solution)/shard_map/ppermute | solution.py:70
  273.3 7.5 %ssd_gate.1 = (f32[512,1536]{1,0:T(8,128)}, bf16[512,1536]{1,0:T(8,128)(2,1)S(1)}, f32[128,1536]{1,0:T(8,128)S(1)}, f32[8,128]{1,0:T(8,128)S(1)}) custom-call(f32[512,1536]{1,0:T(8,128)} %fusion.98.dym_ref, f32[512,1536]{1,0:T(8,128)} %get-tuple-element.252.y_ref, f32[512,1792]{1,0:T(8,128)} %copy-done, bf16[512,1536]{1,0:T(8,128)(2,1)S(1)} %copy-done.5, ...), custom_call_target="tpu_custom_call" | custom-call | tf_op jit(solution)/shard_map/ssd_gate/pallas_call | solution.py:384
  287.0 8.1 %collective-permute-done.19 = bf16[2,2,2,64,1024]{4,3,0,1,2:T(8,128)(2,1)} collective-permute-done((bf16[2,2,2,64,1024]{4,3,0,1,2:T(8,128)(2,1)}, bf16[2,2,2,64,1024]{4,3,0,1,2:T(8,128)(2,1)}, u32[]{:S(2)}, u32[]{:S(2)}) %collective-permute-start.19) | collective-permute-done | bytes 1048608 | tf_op jit(solution)/shard_map/ppermute | solution.py:70
  312.5 28.7 %ssd_backward.1 = (f32[512,1536]{1,0:T(8,128)}, f32[512,128]{1,0:T(8,128)S(1)}, f32[512,128]{1,0:T(8,128)S(1)}, f32[4,512,128]{2,1,0:T(8,128)S(1)}, f32[24,512]{1,0:T(8,128)S(1)}) custom-call(f32[512,1792]{1,0:T(8,128)} %copy-done, f32[512,1536]{1,0:T(8,128)} %get-tuple-element.263.dy_ref, f32[512,1792]{1,0:T(8,128)} %copy-done, f32[512,1792]{1,0:T(8,128)} %copy-done, ...), custom_call_target="tpu_custom_call" | custom-call | tf_op jit(solution)/shard_map/ssd_backward/pallas_call | solution.py:504
  351.7 12.8 %conv_backward.1 = (bf16[512,1792]{1,0:T(8,128)(2,1)S(1)}, f32[8,1792]{1,0:T(8,128)S(1)}, f32[8,1792]{1,0:T(8,128)S(1)}, f32[8,1792]{1,0:T(8,128)S(1)}) custom-call(f32[512,1536]{1,0:T(8,128)} %get-tuple-element.276.dx_ref, f32[512,128]{1,0:T(8,128)S(1)} %get-tuple-element.277.db_ref, f32[512,128]{1,0:T(8,128)S(1)} %get-tuple-element.278.dc_ref, ...), custom_call_target="tpu_custom_call" | custom-call | tf_op jit(solution)/shard_map/conv_backward/pallas_call | solution.py:621
  384.2 7.6 %collective-permute-start.38 = (f32[8,128]{1,0:T(8,128)S(1)}, f32[8,128]{1,0:T(8,128)S(1)}, u32[]{:S(2)}, u32[]{:S(2)}) collective-permute-start(f32[8,128]{1,0:T(8,128)S(1)} %get-tuple-element.314), channel_id=1, source_target_pairs={{0,16},{2,18},{4,20},{6,22},{8,24},{10,26},{12,28},{14,30},{16,0},... | collective-permute-start | bytes 12296 | tf_op jit(solution)/shard_map/ppermute | solution.py:70
  401.1 6.4 %collective-permute-done.42 = bf16[64,1024]{1,0:T(8,128)(2,1)S(1)} collective-permute-done((bf16[64,1024]{1,0:T(8,128)(2,1)S(1)}, bf16[64,1024]{1,0:T(8,128)(2,1)S(1)}, u32[]{:S(2)}, u32[]{:S(2)}) %collective-permute-start.42) | collective-permute-done | bytes 131104 | tf_op jit(solution)/shard_map/ppermute | solution.py:70
  411.8 9.8 %attend_backward.1 = (f32[512,512]{1,0:T(8,128)S(1)}, f32[1024,256]{1,0:T(8,128)S(1)}) custom-call(s32[1]{0:T(128)} %bitcast.13.rank_ref, bf16[512,512]{1,0:T(8,128)(2,1)S(1)} %copy-done.14, bf16[1024,256]{1,0:T(8,128)(2,1)S(1)} %pad_maximum_fusion.1.kv_ref, bf16[512,512]{1,0:T(8,128)(2,1)S(1)} %copy-done.15, f32[128,512]{1,0:T(8,128)S(1)} %copy-done.22, ...), custom_call_target="tpu_custom_call" | custom-call | tf_op jit(solution)/shard_map/attend_backward/pallas_call | solution.py:918
  421.7 15.4 %collective-permute-done.37 = bf16[2,2,2,32,512]{4,3,0,1,2:T(8,128)(2,1)S(1)} collective-permute-done((bf16[2,2,2,32,512]{4,3,0,1,2:T(8,128)(2,1)S(1)}, bf16[2,2,2,32,512]{4,3,0,1,2:T(8,128)(2,1)S(1)}, u32[]{:S(2)}, u32[]{:S(2)}) %collective-permute-start.37) | collective-permute-done | bytes 262176 | tf_op jit(solution)/shard_map/ppermute | solution.py:70
  437.4 16.4 %collective-permute-done.39 = bf16[2,2,32,1536]{3,2,0,1:T(8,128)(2,1)S(1)} collective-permute-done((bf16[2,2,32,1536]{3,2,0,1:T(8,128)(2,1)S(1)}, bf16[2,2,32,1536]{3,2,0,1:T(8,128)(2,1)S(1)}, u32[]{:S(2)}, u32[]{:S(2)}) %collective-permute-start.39) | collective-permute-done | bytes 393248 | tf_op jit(solution)/shard_map/ppermute | solution.py:70
  469.7 8.4 %collective-permute-done.44 = bf16[2,2,32,640]{3,2,0,1:T(8,128)(2,1)S(1)} collective-permute-done((bf16[2,2,32,640]{3,2,0,1:T(8,128)(2,1)S(1)}, bf16[2,2,32,640]{3,2,0,1:T(8,128)(2,1)S(1)}, u32[]{:S(2)}, u32[]{:S(2)}) %collective-permute-start.44) | collective-permute-done | bytes 163872 | tf_op jit(solution)/shard_map/ppermute | solution.py:70
  520.1 6.8 %collective-permute-done.59 = bf16[32,640]{1,0:T(8,128)(2,1)S(1)} collective-permute-done((bf16[32,640]{1,0:T(8,128)(2,1)}, bf16[32,640]{1,0:T(8,128)(2,1)S(1)}, u32[]{:S(2)}, u32[]{:S(2)}) %collective-permute-start.59) | collective-permute-done | bytes 40992 | tf_op jit(solution)/shard_map/ppermute | solution.py:70
  (516 shorter events, 296.2 us)
Async XLA Ops:
  7.2 103.9 %all-gather.3.cloned.1.call-start = ((), (), s32[]{:S(2)}) async-start(), calls=%async_computation.2 | async-start | bytes 8921088 | tf_op jit(solution)/shard_map/all_gather | solution.py:994
  12.3 180.5 %all-gather.5.cloned.1.call-start = ((), (), s32[]{:S(2)}) async-start(), calls=%async_computation.3 | async-start | bytes 8650752 | tf_op jit(solution)/shard_map/all_gather | solution.py:1001
  13.0 538.1 %reduce-scatter.2.cloned.1.call-start = ((), (), s32[]{:S(2)}) async-start(), calls=%async_computation.4 | async-start | bytes 8650752 | tf_op jit(solution)/shard_map/reduce_scatter | solution.py:1096
  61.4 25.6 %collective-permute-start.8 = (bf16[2,2,2,48,1024]{4,3,2,1,0:T(8,128)(2,1)S(1)}, bf16[2,2,2,48,1024]{4,3,2,1,0:T(8,128)(2,1)S(1)}, u32[]{:S(2)}, u32[]{:S(2)}) collective-permute-start(bf16[2,2,2,48,1024]{4,3,2,1,0:T(8,128)(2,1)S(1)} %broadcast_select_fusion.6), channel_id=1, source_target_pairs={{0,1},{1,0},{2,3},{3,2},{4,5},{5,4},{6,7},{7,6},{8,9},{9,8},{10,11... | collective-permute-start | bytes 2359304 | tf_op jit(solution)/shard_map/ppermute | solution.py:70
  132.7 28.0 %collective-permute-start.16 = (bf16[512,256]{1,0:T(8,128)(2,1)S(1)}, bf16[512,256]{1,0:T(8,128)(2,1)S(1)}, u32[]{:S(2)}, u32[]{:S(2)}) collective-permute-start(bf16[512,256]{1,0:T(8,128)(2,1)S(1)} %get-tuple-element.238), channel_id=1, source_target_pairs={{0,1},{2,3},{4,5},{6,7},{8,9},{10,11},{12,13},{14,15},{16,17},{18,... | collective-permute-start | bytes 786440 | tf_op jit(solution)/shard_map/ppermute | solution.py:939
  134.2 50.8 %collective-permute-start.15 = (bf16[2,2,2,64,1024]{4,3,2,1,0:T(8,128)(2,1)S(1)}, bf16[2,2,2,64,1024]{4,3,2,1,0:T(8,128)(2,1)S(1)}, u32[]{:S(2)}, u32[]{:S(2)}) collective-permute-start(bf16[2,2,2,64,1024]{4,3,2,1,0:T(8,128)(2,1)S(1)} %copy-done.41), channel_id=1, source_target_pairs={{0,4},{2,6},{4,0},{6,2},{8,12},{10,14},{12,8},{14,10},{16,20},{18,... | collective-permute-start | bytes 3145736 | tf_op jit(solution)/shard_map/ppermute | solution.py:70
  263.9 33.6 %collective-permute-start.20 = (bf16[2,2,2,2,48,1024]{5,4,0,1,3,2:T(8,128)(2,1)}, bf16[2,2,2,2,48,1024]{5,4,0,1,3,2:T(8,128)(2,1)}, u32[]{:S(2)}, u32[]{:S(2)}) collective-permute-start(bf16[2,2,2,2,48,1024]{5,4,0,1,3,2:T(8,128)(2,1)} %copy_bitcast_fusion.2), channel_id=1, source_target_pairs={{0,2},{2,0},{4,6},{6,4},{8,10},{10,8},{12,14},{14,12},{16,18},{18,... | collective-permute-start | bytes 4718600 | tf_op jit(solution)/shard_map/ppermute | solution.py:70
  264.1 30.9 %collective-permute-start.19 = (bf16[2,2,2,64,1024]{4,3,0,1,2:T(8,128)(2,1)}, bf16[2,2,2,64,1024]{4,3,0,1,2:T(8,128)(2,1)}, u32[]{:S(2)}, u32[]{:S(2)}) collective-permute-start(bf16[2,2,2,64,1024]{4,3,0,1,2:T(8,128)(2,1)} %dynamic-slice_bitcast_fusion), channel_id=1, source_target_pairs={{0,1},{1,0},{2,3},{3,2},{4,5},{5,4},{6,7},{7,6},{8,9},{9,8},{10,11... | collective-permute-start | bytes 3145736 | tf_op jit(solution)/shard_map/ppermute | solution.py:70
  282.7 29.8 %collective-permute-start.22 = (bf16[128,1536]{1,0:T(8,128)(2,1)}, bf16[128,1536]{1,0:T(8,128)(2,1)}, u32[]{:S(2)}, u32[]{:S(2)}) collective-permute-start(bf16[128,1536]{1,0:T(8,128)(2,1)} %convert_element_type.673), channel_id=1, source_target_pairs={{1,0},{3,2},{5,4},{7,6},{9,8},{11,10},{13,12},{15,14},{17,16},{19,... | collective-permute-start | bytes 1179656 | tf_op jit(solution)/shard_map/ppermute | solution.py:207
  303.9 39.1 %collective-permute-start.23 = (bf16[2,2,64,1024]{3,2,0,1:T(8,128)(2,1)}, bf16[2,2,64,1024]{3,2,0,1:T(8,128)(2,1)}, u32[]{:S(2)}, u32[]{:S(2)}) collective-permute-start(bf16[2,2,64,1024]{3,2,0,1:T(8,128)(2,1)} %dynamic-slice_bitcast_fusion.3), channel_id=1, source_target_pairs={{0,4},{2,6},{4,0},{6,2},{8,12},{10,14},{12,8},{14,10},{16,20},{18,... | collective-permute-start | bytes 1572872 | tf_op jit(solution)/shard_map/ppermute | solution.py:70
  305.4 35.8 %collective-permute-start.24 = (bf16[2,2,2,16,1024]{4,3,0,1,2:T(8,128)(2,1)S(1)}, bf16[2,2,2,16,1024]{4,3,0,1,2:T(8,128)(2,1)}, u32[]{:S(2)}, u32[]{:S(2)}) collective-permute-start(bf16[2,2,2,16,1024]{4,3,0,1,2:T(8,128)(2,1)S(1)} %dynamic-slice_bitcast_fusion.11), channel_id=1, source_target_pairs={{0,1},{1,0},{2,3},{3,2},{4,5},{5,4},{6,7},{7,6},{8,9},{9,8},{10,11... | collective-permute-start | bytes 786440 | tf_op jit(solution)/shard_map/ppermute | solution.py:70
  306.8 38.2 %collective-permute-start.25 = (bf16[2,2,2,48,1024]{4,3,0,1,2:T(8,128)(2,1)}, bf16[2,2,2,48,1024]{4,3,0,1,2:T(8,128)(2,1)}, u32[]{:S(2)}, u32[]{:S(2)}) collective-permute-start(bf16[2,2,2,48,1024]{4,3,0,1,2:T(8,128)(2,1)} %dynamic-slice_bitcast_fusion.2), channel_id=1, source_target_pairs={{0,4},{2,6},{4,0},{6,2},{8,12},{10,14},{12,8},{14,10},{16,20},{18,... | collective-permute-start | bytes 2359304 | tf_op jit(solution)/shard_map/ppermute | solution.py:70
  307.4 39.9 %collective-permute-start.26 = (bf16[2,2,2,2,32,1536]{5,4,0,1,3,2:T(8,128)(2,1)}, bf16[2,2,2,2,32,1536]{5,4,0,1,3,2:T(8,128)(2,1)S(1)}, u32[]{:S(2)}, u32[]{:S(2)}) collective-permute-start(bf16[2,2,2,2,32,1536]{5,4,0,1,3,2:T(8,128)(2,1)} %copy_bitcast_fusion.1), channel_id=1, source_target_pairs={{0,2},{2,0},{4,6},{6,4},{8,10},{10,8},{12,14},{14,12},{16,18},{18,... | collective-permute-start | bytes 4718600 | tf_op jit(solution)/shard_map/ppermute | solution.py:70
  348.7 28.2 %collective-permute-start.27 = (bf16[2,64,1024]{2,1,0:T(8,128)(2,1)}, bf16[2,64,1024]{2,1,0:T(8,128)(2,1)}, u32[]{:S(2)}, u32[]{:S(2)}) collective-permute-start(bf16[2,64,1024]{2,1,0:T(8,128)(2,1)} %dynamic-slice_bitcast_fusion.10), channel_id=1, source_target_pairs={{0,8},{2,10},{4,12},{6,14},{8,0},{10,2},{12,4},{14,6},{16,24},{18,... | collective-permute-start | bytes 786440 | tf_op jit(solution)/shard_map/ppermute | solution.py:70
  350.2 25.7 %collective-permute-start.28 = (bf16[2,2,16,1024]{3,2,0,1:T(8,128)(2,1)}, bf16[2,2,16,1024]{3,2,0,1:T(8,128)(2,1)}, u32[]{:S(2)}, u32[]{:S(2)}) collective-permute-start(bf16[2,2,16,1024]{3,2,0,1:T(8,128)(2,1)} %dynamic-slice_bitcast_fusion.19), channel_id=1, source_target_pairs={{0,4},{2,6},{4,0},{6,2},{8,12},{10,14},{12,8},{14,10},{16,20},{18,... | collective-permute-start | bytes 393224 | tf_op jit(solution)/shard_map/ppermute | solution.py:70
  366.6 29.9 %collective-permute-start.33 = (bf16[2,2,48,1024]{3,2,0,1:T(8,128)(2,1)}, bf16[2,2,48,1024]{3,2,0,1:T(8,128)(2,1)}, u32[]{:S(2)}, u32[]{:S(2)}) collective-permute-start(bf16[2,2,48,1024]{3,2,0,1:T(8,128)(2,1)} %dynamic-slice_bitcast_fusion.6), channel_id=1, source_target_pairs={{0,1},{1,0},{2,3},{3,2},{4,5},{5,4},{6,7},{7,6},{8,9},{9,8},{10,11... | collective-permute-start | bytes 1179656 | tf_op jit(solution)/shard_map/ppermute | solution.py:70
  369.9 28.9 %collective-permute-start.34 = (bf16[2,2,2,32,1536]{4,3,0,1,2:T(8,128)(2,1)}, bf16[2,2,2,32,1536]{4,3,0,1,2:T(8,128)(2,1)}, u32[]{:S(2)}, u32[]{:S(2)}) collective-permute-start(bf16[2,2,2,32,1536]{4,3,0,1,2:T(8,128)(2,1)} %dynamic-slice_bitcast_fusion.1), channel_id=1, source_target_pairs={{0,4},{2,6},{4,0},{6,2},{8,12},{10,14},{12,8},{14,10},{16,20},{18,... | collective-permute-start | bytes 2359304 | tf_op jit(solution)/shard_map/ppermute | solution.py:70
  408.2 29.0 %collective-permute-start.35 = (bf16[2,2,2,32,640]{4,3,0,1,2:T(8,128)(2,1)S(1)}, bf16[2,2,2,32,640]{4,3,0,1,2:T(8,128)(2,1)S(1)}, u32[]{:S(2)}, u32[]{:S(2)}) collective-permute-start(bf16[2,2,2,32,640]{4,3,0,1,2:T(8,128)(2,1)S(1)} %dynamic-slice_bitcast_fusion.8), channel_id=1, source_target_pairs={{0,4},{2,6},{4,0},{6,2},{8,12},{10,14},{12,8},{14,10},{16,20},{18,... | collective-permute-start | bytes 983048 | tf_op jit(solution)/shard_map/ppermute | solution.py:70
  408.2 29.1 %collective-permute-start.36 = (bf16[2,2,2,32,640]{4,3,0,1,2:T(8,128)(2,1)S(1)}, bf16[2,2,2,32,640]{4,3,0,1,2:T(8,128)(2,1)S(1)}, u32[]{:S(2)}, u32[]{:S(2)}) collective-permute-start(bf16[2,2,2,32,640]{4,3,0,1,2:T(8,128)(2,1)S(1)} %dynamic-slice_bitcast_fusion.7), channel_id=1, source_target_pairs={{0,1},{1,0},{2,3},{3,2},{4,5},{5,4},{6,7},{7,6},{8,9},{9,8},{10,11... | collective-permute-start | bytes 983048 | tf_op jit(solution)/shard_map/ppermute | solution.py:70
  409.7 27.3 %collective-permute-start.37 = (bf16[2,2,2,32,512]{4,3,0,1,2:T(8,128)(2,1)S(1)}, bf16[2,2,2,32,512]{4,3,0,1,2:T(8,128)(2,1)S(1)}, u32[]{:S(2)}, u32[]{:S(2)}) collective-permute-start(bf16[2,2,2,32,512]{4,3,0,1,2:T(8,128)(2,1)S(1)} %dynamic-slice_bitcast_fusion.9), channel_id=1, source_target_pairs={{0,1},{1,0},{2,3},{3,2},{4,5},{5,4},{6,7},{7,6},{8,9},{9,8},{10,11... | collective-permute-start | bytes 786440 | tf_op jit(solution)/shard_map/ppermute | solution.py:70
  410.2 43.6 %collective-permute-start.39 = (bf16[2,2,32,1536]{3,2,0,1:T(8,128)(2,1)S(1)}, bf16[2,2,32,1536]{3,2,0,1:T(8,128)(2,1)S(1)}, u32[]{:S(2)}, u32[]{:S(2)}) collective-permute-start(bf16[2,2,32,1536]{3,2,0,1:T(8,128)(2,1)S(1)} %dynamic-slice_bitcast_fusion.5), channel_id=1, source_target_pairs={{0,1},{1,0},{2,3},{3,2},{4,5},{5,4},{6,7},{7,6},{8,9},{9,8},{10,11... | collective-permute-start | bytes 1179656 | tf_op jit(solution)/shard_map/ppermute | solution.py:70
  454.8 23.6 %collective-permute-start.43 = (bf16[512,256]{1,0:T(8,128)(2,1)S(1)}, bf16[512,256]{1,0:T(8,128)(2,1)S(1)}, u32[]{:S(2)}, u32[]{:S(2)}) collective-permute-start(bf16[512,256]{1,0:T(8,128)(2,1)S(1)} %slice.195), channel_id=1, source_target_pairs={{1,0},{3,2},{5,4},{7,6},{9,8},{11,10},{13,12},{15,14},{17,16},{19,... | collective-permute-start | bytes 786440 | tf_op jit(solution)/shard_map/ppermute | solution.py:950
  456.5 21.6 %collective-permute-start.44 = (bf16[2,2,32,640]{3,2,0,1:T(8,128)(2,1)S(1)}, bf16[2,2,32,640]{3,2,0,1:T(8,128)(2,1)S(1)}, u32[]{:S(2)}, u32[]{:S(2)}) collective-permute-start(bf16[2,2,32,640]{3,2,0,1:T(8,128)(2,1)S(1)} %dynamic-slice_bitcast_fusion.16), channel_id=1, source_target_pairs={{0,1},{1,0},{2,3},{3,2},{4,5},{5,4},{6,7},{7,6},{8,9},{9,8},{10,11... | collective-permute-start | bytes 491528 | tf_op jit(solution)/shard_map/ppermute | solution.py:70
  510.8 28.5 %all-to-all-start = ((bf16[32,32,128]{2,1,0:T(8,128)(2,1)}), bf16[32,32,128]{2,1,0:T(8,128)(2,1)S(1)}, u32[]{:S(2)}, u32[]{:S(2)}) async-start(bf16[32,32,128]{2,1,0:T(8,128)(2,1)} %concatenate.61), calls=%async_computation | async-start | bytes 524288 | tf_op jit(solution)/shard_map/all_to_all | solution.py:1171
  (126 other events, 1330.4 us)
Sparse Core Ops, SparseCore 0:
  12.4 93.6 all-gather.2
  109.1 83.6 all-gather.4
  285.5 243.6 reduce-scatter.1
